TPU v7x, 128 devices: a whole 4x4x4 slice. The times are simulated.
128 devices in a mesh: rep: 4 (over y), set: 32 (over z, x, core).
Axes of the slice: x: 4, y: 4, z: 4, core: 2. Of those that a mesh axis runs over, the one named last changes fastest.
Arguments:
- scenarios: bfloat16 [3, 8192, 20000], P(None, ('rep', 'set')), may hold values from -6 to 6
- projection: bfloat16 [20000, 256], replicated, may hold values from -0.0390625 to 0.0390625
- coefs: bfloat16 [3, 256, 1024, 64], P(None, None, 'set'), may hold values from -0.0234375 to 0.0234375
- exercise: float32 [3, 1024, 64], P(None, 'set'), may hold values from -0.2 to 0
- block_set: int32 [1024], P('set'), may hold values from 0 to 127, as said below
- block_live: int32 [1024], P('set'), may hold values from 1 to 64
Outputs:
- exposure: float32 [3, 128], P(None, 'set')
- spread: float32 [3, 128], P(None, 'set')
Inputs may be any that keep to these rules, and one draw needn't show every extreme that they name: `block_set`: every netting set owns at least one block.
All inputs are finite; a program needn't handle non-finite values.
Results may differ from a plain program's by a relative error of at most 0.0011.
Values may be sent and summed in bfloat16 or wider, within the bound.
No kernel may reach another device: no remote copies, remote signals or barrier semaphores. Data moves between devices by JAX's collectives and lax.ppermute only.
A program may use at most 128 MiB of HBM per device.

v0:
```python
import jax
import jax.numpy as jnp
from jax import lax
from jax.sharding import PartitionSpec as P

STEPS = 3
PATHS = 1024
RPD = 2
SPD = 4


def body(scenarios, projection, coefs, exercise, block_set, block_live):
    rep_count = lax.axis_size("rep")
    set_count = lax.axis_size("set")
    total_sets = SPD * set_count
    replicates = RPD * rep_count
    blocks = block_set.shape[0]
    trade_width = coefs.shape[3]
    basis_width = projection.shape[1]
    onehot_t = (jnp.arange(total_sets, dtype=jnp.int32)[:, None] == block_set[None, :]).astype(
        jnp.float32
    )
    live = jnp.arange(trade_width, dtype=jnp.int32)[None, :] < block_live[:, None]
    results = []
    for step in range(STEPS):
        basis = jnp.tanh(
            jnp.dot(scenarios[step], projection, preferred_element_type=jnp.float32)
        ).astype(jnp.bfloat16)
        local_rows = basis.reshape(-1, replicates, basis_width)
        weights = coefs[step].reshape(basis_width, blocks * trade_width)
        floor_now = exercise[step]
        gathered = lax.all_gather(local_rows, "set", axis=0, tiled=True)
        grouped = lax.all_to_all(gathered, "rep", split_axis=1, concat_axis=0, tiled=True)
        flat = grouped.reshape(-1, basis_width)
        values = jnp.dot(flat, weights, preferred_element_type=jnp.float32).reshape(
            -1, blocks, trade_width
        )
        values = jnp.where(live[None], jnp.maximum(values, floor_now[None]), 0.0)
        block_sums = jnp.sum(values, axis=2)
        terms = jnp.dot(onehot_t, block_sums.T, precision=lax.Precision.HIGHEST)
        netted = lax.psum_scatter(terms, "set", scatter_dimension=0, tiled=True)
        positive = jnp.maximum(netted, 0.0).reshape(SPD, -1, RPD)
        results.append(jnp.mean(positive, axis=1))
    stacked = jnp.stack(results)
    per_replicate = lax.all_gather(stacked, "rep", axis=2, tiled=True)
    exposure = jnp.mean(per_replicate, axis=2)
    deviation = per_replicate - exposure[:, :, None]
    spread = jnp.sqrt(
        PATHS * jnp.sum(deviation * deviation, axis=2) / ((replicates - 1) * replicates)
    )
    return (exposure, spread)


def solution(mesh):
    return jax.shard_map(
        body,
        mesh=mesh,
        in_specs=(
            P(None, ("rep", "set"), None),
            P(),
            P(None, None, "set", None),
            P(None, "set", None),
            P("set"),
            P("set"),
        ),
        out_specs=(P(None, "set"), P(None, "set")),
        check_vma=False,
    )
```

profile of v0, /device:TPU:0, one launch (start us, length us, event | category | flops | bytes accessed | tf_op | source)
XLA Modules:
  0.0 309.3 jit_solution(7874158053762437890)
XLA Ops:
  7.2 6.6 %fusion.33 = bf16[8,8,256]{2,1,0:T(8,128)(2,1)S(1)} fusion(bf16[20000,256]{1,0:T(8,128)(2,1)} %param.7, bf16[3,64,20000]{2,1,0:T(8,128)(2,1)} %param.6), kind=kOutput, calls=%fused_computation.20 | convolution fusion | flops 655376384 | bytes 12845056 | tf_op jit(solution)/shard_map/dot_general | solution.py:27
  13.8 0.6 copy.26
  14.5 6.6 %fusion.30 = bf16[8,8,256]{2,1,0:T(8,128)(2,1)S(1)} fusion(bf16[20000,256]{1,0:T(8,128)(2,1)} %param.7, bf16[3,64,20000]{2,1,0:T(8,128)(2,1)} %param.6), kind=kOutput, calls=%fused_computation.19 | convolution fusion | flops 655376384 | bytes 12845056 | tf_op jit(solution)/shard_map/dot_general | solution.py:27
  21.1 0.6 copy.23
  21.8 6.6 %fusion.27 = bf16[8,8,256]{2,1,0:T(8,128)(2,1)S(1)} fusion(bf16[20000,256]{1,0:T(8,128)(2,1)} %param.7, bf16[3,64,20000]{2,1,0:T(8,128)(2,1)} %param.6), kind=kOutput, calls=%fused_computation.18 | convolution fusion | flops 655376384 | bytes 12845056 | tf_op jit(solution)/shard_map/dot_general | solution.py:27
  28.4 0.6 copy.20
  29.1 31.0 %all-gather.8.cloned.1.call-done = bf16[256,8,256]{2,0,1:T(8,128)(2,1)} async-done(((bf16[8,8,256]{2,0,1:T(8,128)(2,1)}), bf16[256,8,256]{2,0,1:T(8,128)(2,1)}) %all-gather.8.cloned.1.call-update) | async-done | bytes 1048592 | tf_op jit(solution)/shard_map/all_gather | solution.py:32
  60.0 4.3 %all-to-all-start.2 = ((bf16[256,8,256]{2,0,1:T(8,128)(2,1)}), bf16[256,8,256]{2,0,1:T(8,128)(2,1)S(1)}, u32[]{:S(2)}, u32[]{:S(2)}) async-start(bf16[256,8,256]{2,0,1:T(8,128)(2,1)} %all-gather.8.cloned.1.call-done), calls=%async_computation.2 | async-start | bytes 2097152 | tf_op jit(solution)/shard_map/all_to_all | solution.py:33
  64.3 40.2 %all-gather.6.cloned.1.call-done = bf16[256,8,256]{2,0,1:T(8,128)(2,1)} async-done(((bf16[8,8,256]{2,0,1:T(8,128)(2,1)}), bf16[256,8,256]{2,0,1:T(8,128)(2,1)}) %all-gather.6.cloned.1.call-update) | async-done | bytes 1048592 | tf_op jit(solution)/shard_map/all_gather | solution.py:32
  104.5 4.3 %all-to-all-start.1 = ((bf16[256,8,256]{2,0,1:T(8,128)(2,1)}), bf16[256,8,256]{2,0,1:T(8,128)(2,1)S(1)}, u32[]{:S(2)}, u32[]{:S(2)}) async-start(bf16[256,8,256]{2,0,1:T(8,128)(2,1)} %all-gather.6.cloned.1.call-done), calls=%async_computation.1 | async-start | bytes 2097152 | tf_op jit(solution)/shard_map/all_to_all | solution.py:33
  108.9 1.1 copy.27
  109.9 1.2 reshape.100
  111.2 37.8 %all-gather.4.cloned.1.call-done = bf16[256,8,256]{2,0,1:T(8,128)(2,1)} async-done(((bf16[8,8,256]{2,0,1:T(8,128)(2,1)}), bf16[256,8,256]{2,0,1:T(8,128)(2,1)}) %all-gather.4.cloned.1.call-update) | async-done | bytes 1048592 | tf_op jit(solution)/shard_map/all_gather | solution.py:32
  148.9 4.3 %all-to-all-start = ((bf16[256,8,256]{2,0,1:T(8,128)(2,1)}), bf16[256,8,256]{2,0,1:T(8,128)(2,1)S(1)}, u32[]{:S(2)}, u32[]{:S(2)}) async-start(bf16[256,8,256]{2,0,1:T(8,128)(2,1)} %all-gather.4.cloned.1.call-done), calls=%async_computation | async-start | bytes 2097152 | tf_op jit(solution)/shard_map/all_to_all | solution.py:33
  153.2 1.1 copy.24
  154.3 0.6 reshape.99
  154.9 4.3 %select_reduce_fusion = f32[2048,32]{0,1:T(8,128)S(1)} fusion(f32[32,64]{1,0:T(8,128)S(1)} %get-tuple-element.6, pred[32,64]{1,0:T(8,128)(4,1)S(1)} %iota_compare_fusion.4, bf16[2048,256,1]{1,0,2:T(8,128)(2,1)} %reshape.100, bf16[3,256,32,64]{1,3,2,0:T(8,128)(2,1)} %param.8), kind=kOutput, calls=%fused_computation | convolution fusion | flops 2160001024 | bytes 2369536 | tf_op jit(solution)/shard_map/dot_general | solution.py:35
  159.3 1.6 fusion.42
  160.9 4.0 %select_reduce_fusion.1 = f32[2048,32]{0,1:T(8,128)S(1)} fusion(f32[32,64]{1,0:T(8,128)S(1)} %get-tuple-element.7, pred[32,64]{1,0:T(8,128)(4,1)S(1)} %iota_compare_fusion.4, bf16[2048,256,1]{1,0,2:T(8,128)(2,1)S(1)} %reshape.99, bf16[3,256,32,64]{1,3,2,0:T(8,128)(2,1)} %param.8), kind=kOutput, calls=%fused_computation.1 | convolution fusion | flops 2160001024 | bytes 2369536 | tf_op jit(solution)/shard_map/dot_general | solution.py:35
  164.9 1.6 fusion.43
  166.5 2.2 all-to-all-done
  168.7 1.1 copy.21
  170.2 4.0 %select_reduce_fusion.2 = f32[2048,32]{0,1:T(8,128)S(1)} fusion(f32[32,64]{1,0:T(8,128)S(1)} %get-tuple-element.5, pred[32,64]{1,0:T(8,128)(4,1)S(1)} %iota_compare_fusion.4, bf16[2048,256,1]{1,0,2:T(8,128)(2,1)S(1)} %reshape.98, bf16[3,256,32,64]{1,3,2,0:T(8,128)(2,1)} %param.8), kind=kOutput, calls=%fused_computation.2 | convolution fusion | flops 2160001024 | bytes 2369536 | tf_op jit(solution)/shard_map/dot_general | solution.py:35
  174.3 1.6 fusion.44
  177.1 106.5 %all-reduce.6.cloned.1.call-done = (f32[128,2048]{1,0:T(8,128)}, f32[128,2048]{1,0:T(8,128)}, f32[128,2048]{1,0:T(8,128)}) async-done(((f32[128,2048]{1,0:T(8,128)}, f32[128,2048]{1,0:T(8,128)}, f32[128,2048]{1,0:T(8,128)}), (f32[128,2048]{1,0:T(8,128)}, f32[128,2048]{1,0:T(8,128)}, f32[128,2048]{1,0:T(8,128)})) %all-reduce.6.cloned.1.call-update) | async-done | bytes 3145744
  283.6 0.9 dynamic-slice_maximum_fusion
  284.9 1.1 reduce_sum.77
  286.3 1.1 reduce_sum.75
  287.4 0.9 dynamic-slice_maximum_fusion.2
  288.7 1.1 reduce_sum.73
  289.8 12.4 %all_gather.15 = f32[3,4,8]{1,0,2:T(4,128)S(1)} all-gather(f32[3,4,2]{1,0,2:T(4,128)S(1)} %copy.29), channel_id=1, replica_groups=mesh['rep'=4,'set'=32] {'rep'}, dimensions={2}, use_global_device_ids=true | all-gather | bytes 480 | tf_op jit(solution)/shard_map/all_gather | solution.py:45
  302.2 0.6 multiply_sqrt_fusion
  (35 shorter events, 2.5 us)
Async XLA Ops:
  7.2 52.9 %all-gather.8.cloned.1.call-start = ((), (), s32[]{:S(2)}) async-start(), calls=%async_computation.5 | async-start | bytes 1081344 | tf_op jit(solution)/shard_map/all_gather | solution.py:32
  14.5 90.0 %all-gather.6.cloned.1.call-start = ((), (), s32[]{:S(2)}) async-start(), calls=%async_computation.4 | async-start | bytes 1081344 | tf_op jit(solution)/shard_map/all_gather | solution.py:32
  21.7 87.0 %copy-start.3 = (s32[32]{0:T(128)S(1)}, s32[32]{0:T(128)}, u32[]{:S(2)}) copy-start(s32[32]{0:T(128)} %param.11) | copy-start | bytes 388
  21.8 87.1 %copy-start = (f32[3,32,64]{2,1,0:T(8,128)S(1)}, f32[3,32,64]{2,1,0:T(8,128)}, u32[]{:S(2)}) copy-start(f32[3,32,64]{2,1,0:T(8,128)} %param.9) | copy-start | bytes 73732
  21.8 127.2 %all-gather.4.cloned.1.call-start = ((), (), s32[]{:S(2)}) async-start(), calls=%async_computation.3 | async-start | bytes 1081344 | tf_op jit(solution)/shard_map/all_gather | solution.py:32
  60.0 44.4 %all-to-all-start.2 = ((bf16[256,8,256]{2,0,1:T(8,128)(2,1)}), bf16[256,8,256]{2,0,1:T(8,128)(2,1)S(1)}, u32[]{:S(2)}, u32[]{:S(2)}) async-start(bf16[256,8,256]{2,0,1:T(8,128)(2,1)} %all-gather.8.cloned.1.call-done), calls=%async_computation.2 | async-start | bytes 2097152 | tf_op jit(solution)/shard_map/all_to_all | solution.py:33
  104.5 44.4 %all-to-all-start.1 = ((bf16[256,8,256]{2,0,1:T(8,128)(2,1)}), bf16[256,8,256]{2,0,1:T(8,128)(2,1)S(1)}, u32[]{:S(2)}, u32[]{:S(2)}) async-start(bf16[256,8,256]{2,0,1:T(8,128)(2,1)} %all-gather.6.cloned.1.call-done), calls=%async_computation.1 | async-start | bytes 2097152 | tf_op jit(solution)/shard_map/all_to_all | solution.py:33
  148.9 19.8 %all-to-all-start = ((bf16[256,8,256]{2,0,1:T(8,128)(2,1)}), bf16[256,8,256]{2,0,1:T(8,128)(2,1)S(1)}, u32[]{:S(2)}, u32[]{:S(2)}) async-start(bf16[256,8,256]{2,0,1:T(8,128)(2,1)} %all-gather.4.cloned.1.call-done), calls=%async_computation | async-start | bytes 2097152 | tf_op jit(solution)/shard_map/all_to_all | solution.py:33
  153.2 130.4 %all-reduce.6.cloned.1.call-start = ((), (), s32[]{:S(2)}) async-start(), calls=%async_computation.6 | async-start | bytes 6291456
  154.9 4.4 %copy-start.2 = (s32[32]{0:T(128)S(1)}, s32[32]{0:T(128)}, u32[]{:S(2)}) copy-start(s32[32]{0:T(128)} %param.10) | copy-start | bytes 388
  170.2 5.6 %copy-start.4 = (u32[128]{0:T(128)S(1)}, u32[128]{0:T(128)}, u32[]{:S(2)}) copy-start(u32[128]{0:T(128)} %constant.19) | copy-start | bytes 1540
  302.2 0.6 copy-start.1
Sparse Core Ops, SparseCore 0:
  14.6 45.4 all-gather.7
  62.2 42.2 all-gather.5
  106.7 42.2 all-gather.3
  176.0 107.5 all-reduce.5
where the time goes:
time: 311 us; the launch traced here: 309 us
  waiting for transfers between devices  218 us (70%)
  matrix products  36.9 us (12%)
  between operations  14.6 us (5%)
  starting transfers between devices  13 us (4%)
  blocking collectives  12.4 us (4%)
  local copies, waits for them, and re-layouts  9.09 us (3%)
  other arithmetic  5.75 us (2%)
    all_gather x3, waiting for transfers between devices, body(): gathered = lax.all_gather(local_rows, 'set', axis=0, tiled=True)  109 us
    unnamed x5, waiting for transfers between devices  107 us
    dot_general x3, matrix products, body(): jnp.dot(scenarios[step], projection, preferred_element_type=jnp.float32)  19.8 us
    all_to_all x3, starting transfers between devices, body(): lax.all_to_all(gathered, 'rep', split_axis=1, concat_axis=0, tiled=True)  12.8 us
    all_gather x1, blocking collectives, body(): per_replicate = lax.all_gather(stacked, 'rep', axis=2, tiled=True)  12.4 us
    dot_general x3, matrix products, body(): jnp.dot(flat, weights, preferred_element_type=jnp.float32)  12.3 us
  transfers between devices with their start and end apart: 7, of which 5 were waited for; matrix products, arithmetic and copies ran while one was open for 10% of the time, Pallas kernels for 0%

commit v1 on v0

v1 whole, which is shorter than its diff:
```python
import functools

import jax
import jax.numpy as jnp
from jax import lax
from jax.experimental import pallas as pl
from jax.experimental.pallas import tpu as pltpu
from jax.sharding import PartitionSpec as P

STEPS = 3
PATHS = 1024
REPL = 8
SPD = 4
SIDE = 4
BPD = 32
TB = 64
BASIS = 256
ROWS = 64
CHUNK = SIDE * ROWS
OWN = 2 * SPD
F32 = jnp.float32
BF16 = jnp.bfloat16


def ring_pairs(shift, stage):
    pairs = []
    for z in range(SIDE):
        for x in range(SIDE):
            for core in range(2):
                if (core + stage) % 2 == 0:
                    to = (z, (x + shift) % SIDE, core)
                else:
                    to = ((z + shift) % SIDE, x, core)
                pairs.append((z * 8 + x * 2 + core, to[0] * 8 + to[1] * 2 + to[2]))
    return pairs


CORE_PAIRS = [(i, i ^ 1) for i in range(2 * SIDE * SIDE)]


def shift_by(value, shift, stage):
    return lax.ppermute(value, "set", ring_pairs(shift, stage))


def swap_core(value):
    return lax.ppermute(value, "set", CORE_PAIRS)


def dot(a, b, dims):
    return lax.dot_general(a, b, (dims, ((), ())), preferred_element_type=F32)


def split(value):
    high = value.astype(BF16)
    rest = value - high.astype(F32)
    middle = rest.astype(BF16)
    low = (rest - middle.astype(F32)).astype(BF16)
    return high, middle, low


def net_kernel(rows_ref, mine_ref, other_ref, floor_ref, hot_ref, out_ref):
    for step in range(STEPS):
        rows = rows_ref[:, step].reshape(CHUNK, BASIS)
        total = None
        for half, weights in enumerate((mine_ref, other_ref)):
            sums = None
            for tile in range(BPD * TB // 256):
                cols = slice(tile * 256, (tile + 1) * 256)
                value = dot(rows, weights[step, :, cols], ((1,), (0,)))
                value = jnp.maximum(value, floor_ref[half, step, :, cols])
                both = value[:, :128] + value[:, 128:]
                sums = both if sums is None else sums + both
            for part in split(sums):
                term = dot(hot_ref[half], part, ((1,), (1,)))
                total = term if total is None else total + term
        out_ref[step] = total


def net(rows, mine, other, floors, hot):
    vmem = pl.BlockSpec(memory_space=pltpu.VMEM)
    return pl.pallas_call(
        net_kernel,
        in_specs=[vmem] * 5,
        out_specs=vmem,
        out_shape=jax.ShapeDtypeStruct((STEPS, SIDE * SIDE * OWN, CHUNK), F32),
        name="net",
    )(rows, mine, other, floors, hot)


def body(scenarios, projection, coefs, exercise, block_set, block_live):
    place = lax.axis_index("set")
    z, x, core = place // 8, (place // 2) % SIDE, place % 2

    live = jnp.arange(TB, dtype=jnp.int32)[None, :] < block_live[:, None]
    weights = jnp.where(live[None, None], coefs, 0).astype(BF16)
    weights = jnp.swapaxes(weights, 2, 3).reshape(STEPS, BASIS, TB * BPD)
    floors = jnp.swapaxes(jnp.where(live[None], exercise, 0.0), 1, 2).reshape(STEPS, 1, TB * BPD)

    basis = jnp.tanh(
        jnp.dot(
            scenarios.reshape(STEPS * ROWS, -1), projection, preferred_element_type=F32
        )
    ).astype(BF16)
    basis = basis.reshape(STEPS, ROWS, BASIS)

    first = jnp.where(core == 0, x, z)
    line = [basis] + [shift_by(basis, shift, 0) for shift in (3, 2, 1)]
    line = jnp.stack(line + line)
    line = lax.dynamic_slice_in_dim(line, SIDE - first, SIDE, 0)

    other_weights = swap_core(weights)
    other_floors = swap_core(floors)
    other_set = swap_core(block_set)

    near = (first + jnp.arange(SIDE)) % SIDE
    second = jnp.where(core == 0, z, x)
    far = (second + jnp.arange(SIDE)) % SIDE
    chip = jnp.where(
        core == 0, far[None, :] * SIDE + near[:, None], near[:, None] * SIDE + far[None, :]
    )
    ids = (chip[:, :, None] * OWN + jnp.arange(OWN)).reshape(-1)
    owners = jnp.tile(jnp.stack([block_set, other_set]), (1, SIDE))
    hot = (ids[None, :, None] == owners[:, None, :]).astype(BF16)
    both_floors = jnp.stack([floors, other_floors])

    run = functools.partial(
        net, mine=weights, other=other_weights, floors=both_floors, hot=hot
    )
    arrived = {0: line}
    for shift in (1, 3, 2):
        arrived[shift] = shift_by(line, shift, 1)
    terms = [None] * SIDE
    for shift in (0, 1, 3, 2):
        terms[shift] = run(arrived[shift]).reshape(STEPS, SIDE, SIDE, OWN, CHUNK)

    def message(near_step):
        parts = []
        for far_step in range(SIDE):
            parts.append(
                jnp.concatenate(
                    [
                        terms[(place_ - far_step) % SIDE][:, near_step, far_step]
                        for place_ in range(SIDE)
                    ],
                    axis=2,
                )
            )
        return jnp.stack(parts)

    held = message(0)
    for shift in (1, 3, 2):
        held = held + shift_by(message(shift).astype(jnp.float16), shift, 0).astype(F32)
    netted = held[0]
    for shift in (1, 3, 2):
        netted = netted + shift_by(held[shift], shift, 1)

    positive = jnp.maximum(netted, 0.0).reshape(STEPS * OWN, SIDE * CHUNK)
    pick = (jnp.arange(SIDE * CHUNK)[:, None] % REPL == jnp.arange(REPL)[None, :]).astype(F32)
    sums = jnp.dot(positive, pick, precision=lax.Precision.HIGHEST).reshape(STEPS, 2, SPD, REPL)
    kept = lax.dynamic_index_in_dim(sums, core, 1, keepdims=False)
    given = lax.dynamic_index_in_dim(sums, 1 - core, 1, keepdims=False)
    sums = kept + swap_core(given)
    total = sums
    for shift in (1, 3, 2):
        total = total + lax.ppermute(
            sums, "rep", [(i, (i + shift) % SIDE) for i in range(SIDE)]
        )
    per_replicate = total * (1.0 / PATHS)
    exposure = jnp.mean(per_replicate, axis=2)
    deviation = per_replicate - exposure[:, :, None]
    spread = jnp.sqrt(
        PATHS * jnp.sum(deviation * deviation, axis=2) / ((REPL - 1) * REPL)
    )
    return (exposure, spread)


def solution(mesh):
    return jax.shard_map(
        body,
        mesh=mesh,
        in_specs=(
            P(None, ("rep", "set"), None),
            P(),
            P(None, None, "set", None),
            P(None, "set", None),
            P("set"),
            P("set"),
        ),
        out_specs=(P(None, "set"), P(None, "set")),
        check_vma=False,
    )
```

time: 311 us -> 116 us (0.37)
  waiting for transfers between devices: 218 us -> 22.8 us
  matrix products: 36.9 us -> 8.64 us
  Pallas kernels: 0 us -> 27.2 us
  between operations: 14.6 us -> 1.07 us
  starting transfers between devices: 13 us -> 26.1 us
  blocking collectives: 12.4 us -> 0 us
  other arithmetic: 5.75 us -> 13.9 us
  local copies, waits for them, and re-layouts: 9.09 us -> 15.6 us
    all_gather x3 -> x0, waiting for transfers between devices: 109 us -> none  [body(): gathered = lax.all_gather(local_rows, 'set', axis=0, tiled=True)]
    unnamed x5 -> x0, waiting for transfers between devices: 107 us -> none
    dot_general x9 -> x2, matrix products: 36.9 us -> 8.64 us  [the longest x1 8.43 us: body(): jnp.dot(scenarios.reshape(STEPS * ROWS, -1), projection, preferred_elemen...]
    pallas_call x0 -> x4, Pallas kernels: none -> 27.2 us  [net(): pl.pallas_call(net_kernel, in_specs=[vmem] * 5, out_specs=vmem, out_shape...]
    ppermute x0 -> x19, starting transfers between devices: none -> 26.1 us  [the longest x12 20.2 us: shift_by(): return lax.ppermute(value, 'set', ring_pairs(shift, stage))]
    ppermute x0 -> x19, waiting for transfers between devices: none -> 22.8 us  [the longest x12 17.8 us: shift_by(): return lax.ppermute(value, 'set', ring_pairs(shift, stage))]
    all_to_all x3 -> x0, starting transfers between devices: 12.8 us -> none  [body(): lax.all_to_all(gathered, 'rep', split_axis=1, concat_axis=0, tiled=True)]
    all_gather x1 -> x0, blocking collectives: 12.4 us -> none  [body(): per_replicate = lax.all_gather(stacked, 'rep', axis=2, tiled=True)]
  transfers between devices with their start and end apart: 7 -> 19, of which waited for: 5 -> 10; matrix products, arithmetic and copies ran while one was open for 10% -> 23% of each run, Pallas kernels for 0% -> 18%
where the time goes in v1:
time: 116 us; the launch traced here: 115 us
  Pallas kernels  27.2 us (23%)
  starting transfers between devices  26.1 us (22%)
  waiting for transfers between devices  22.8 us (20%)
  local copies, waits for them, and re-layouts  15.6 us (13%)
  other arithmetic  13.9 us (12%)
  matrix products  8.64 us (7%)
    pallas_call x4, Pallas kernels, net(): pl.pallas_call(net_kernel, in_specs=[vmem] * 5, out_specs=vmem, out_shape...  27.2 us
    ppermute x12, starting transfers between devices, shift_by(): return lax.ppermute(value, 'set', ring_pairs(shift, stage))  20.2 us
    ppermute x12, waiting for transfers between devices, shift_by(): return lax.ppermute(value, 'set', ring_pairs(shift, stage))  17.8 us
    dot_general x1, matrix products, body(): jnp.dot(scenarios.reshape(STEPS * ROWS, -1), projection, preferred_elemen...  8.43 us
    unnamed x23, local copies, waits for them, and re-layouts  7.15 us
    ppermute x3, starting transfers between devices, body(): lax.ppermute(sums, 'rep', [(i, (i + shift) % SIDE) for i in range(SIDE)])  5.22 us
    select_n x1, other arithmetic, body(): weights = jnp.where(live[None, None], coefs, 0).astype(BF16)  5 us
    another operation x4, other arithmetic  4.12 us
  transfers between devices with their start and end apart: 19, of which 10 were waited for; matrix products, arithmetic and copies ran while one was open for 23% of the time, Pallas kernels for 18%

profile of v1, /device:TPU:0, one launch (start us, length us, event | category | flops | bytes accessed | tf_op | source)
XLA Modules:
  0.0 115.3 jit_solution(13903990447305477042)
XLA Ops:
  0.7 8.4 %fusion = bf16[192,256]{1,0:T(8,128)(2,1)S(1)} fusion(bf16[192,20000]{1,0:T(8,128)(2,1)} %bitcast.242, bf16[20000,256]{1,0:T(8,128)(2,1)} %param.7), kind=kOutput, calls=%fused_computation.2 | convolution fusion | flops 1966129152 | bytes 18018304 | tf_op jit(solution)/shard_map/dot_general | solution.py:100
  9.1 1.7 %collective-permute-start.2 = (bf16[3,64,256]{2,1,0:T(8,128)(2,1)S(1)}, bf16[3,64,256]{2,1,0:T(8,128)(2,1)S(1)}, u32[]{:S(2)}, u32[]{:S(2)}) collective-permute-start(bf16[3,64,256]{2,1,0:T(8,128)(2,1)S(1)} %bitcast.249), channel_id=1, source_target_pairs={{0,2},{1,9},{2,4},{3,11},{4,6},{5,13},{6,0},{7,15},{8,10},{9,17},{... | collective-permute-start | bytes 294920 | tf_op jit(solution)/shard_map/ppermute | solution.py:42
  10.8 2.7 %collective-permute-start.1 = (bf16[3,64,256]{2,1,0:T(8,128)(2,1)S(1)}, bf16[3,64,256]{2,1,0:T(8,128)(2,1)S(1)}, u32[]{:S(2)}, u32[]{:S(2)}) collective-permute-start(bf16[3,64,256]{2,1,0:T(8,128)(2,1)S(1)} %bitcast.250), channel_id=1, source_target_pairs={{0,4},{1,17},{2,6},{3,19},{4,0},{5,21},{6,2},{7,23},{8,12},{9,25},... | collective-permute-start | bytes 294920 | tf_op jit(solution)/shard_map/ppermute | solution.py:42
  13.5 1.4 %collective-permute-start = (bf16[3,64,256]{2,1,0:T(8,128)(2,1)S(1)}, bf16[3,64,256]{2,1,0:T(8,128)(2,1)}, u32[]{:S(2)}, u32[]{:S(2)}) collective-permute-start(bf16[3,64,256]{2,1,0:T(8,128)(2,1)S(1)} %bitcast.251), channel_id=1, source_target_pairs={{0,6},{1,25},{2,0},{3,27},{4,2},{5,29},{6,4},{7,31},{8,14},{9,1},{... | collective-permute-start | bytes 294920 | tf_op jit(solution)/shard_map/ppermute | solution.py:42
  15.0 5.0 %copy_select_fusion = bf16[3,256,32,64]{1,2,3,0:T(8,128)(2,1)} fusion(bf16[3,256,32,64]{1,3,2,0:T(8,128)(2,1)S(1)} %copy-done.1, pred[32,64]{0,1:T(8,128)(4,1)S(1)} %iota_compare_fusion.1), kind=kLoop, calls=%fused_computation | loop fusion | flops 1572864 | bytes 6293504 | tf_op jit(solution)/shard_map/jit(_where)/select_n | solution.py:95
  20.0 3.2 %copy.48.mine_ref = bf16[3,256,2048]{2,1,0:T(8,128)(2,1)S(1)} copy(bf16[3,256,2048]{1,2,0:T(8,128)(2,1)} %bitcast.243) | data formatting | bytes 6291456 | tf_op jit(solution)/shard_map/reshape | solution.py:96
  28.2 1.5 %bitcast_dynamic-update-slice_fusion.4 = bf16[8,3,64,256]{3,2,1,0:T(8,128)(2,1)} fusion(bf16[8,3,64,256]{3,2,1,0:T(8,128)(2,1)} %constant_dynamic-update-slice_fusion.1, bf16[3,64,256]{2,1,0:T(8,128)(2,1)} %collective-permute-done), kind=kLoop, calls=%fused_computation.26 | loop fusion | bytes 196608
  31.7 1.5 %bitcast_dynamic-update-slice_fusion.5 = bf16[8,3,64,256]{3,2,1,0:T(8,128)(2,1)} fusion(bf16[8,3,64,256]{3,2,1,0:T(8,128)(2,1)} %constant_dynamic-update-slice_fusion, bf16[3,64,256]{2,1,0:T(8,128)(2,1)} %collective-permute-done), kind=kLoop, calls=%fused_computation.27 | loop fusion | bytes 196608
  34.5 1.0 constant_dynamic-slice_fusion.rows_ref
  35.6 4.1 %collective-permute-start.8 = (bf16[4,3,64,256]{3,2,1,0:T(8,128)(2,1)S(1)}, bf16[4,3,64,256]{3,2,1,0:T(8,128)(2,1)S(1)}, u32[]{:S(2)}, u32[]{:S(2)}) collective-permute-start(bf16[4,3,64,256]{3,2,1,0:T(8,128)(2,1)S(1)} %constant_dynamic-slice_fusion.rows_ref), channel_id=1, source_target_pairs={{0,24},{1,7},{2,26},{3,1},{4,28},{5,3},{6,30},{7,5},{8,0},{9,15},{... | collective-permute-start | bytes 1179656 | tf_op jit(solution)/shard_map/ppermute | solution.py:42
  40.4 1.4 %pad_maximum_fusion.3.floor_ref = f32[2,3,1,2048]{3,2,1,0:T(1,128)} fusion(f32[1,3,1,2048]{3,2,1,0:T(1,128)} %bitcast.10, f32[1,3,1,2048]{3,2,1,0:T(1,128)} %stack_reshape.9), kind=kLoop, calls=%fused_computation.28 | loop fusion | flops 12288 | bytes 98304 | tf_op jit(solution)/shard_map/stack | solution.py:124
  41.8 1.3 %collective-permute-start.6 = (bf16[4,3,64,256]{3,2,1,0:T(8,128)(2,1)S(1)}, bf16[4,3,64,256]{3,2,1,0:T(8,128)(2,1)}, u32[]{:S(2)}, u32[]{:S(2)}) collective-permute-start(bf16[4,3,64,256]{3,2,1,0:T(8,128)(2,1)S(1)} %constant_dynamic-slice_fusion.rows_ref), channel_id=1, source_target_pairs={{0,8},{1,3},{2,10},{3,5},{4,12},{5,7},{6,14},{7,1},{8,16},{9,11},{... | collective-permute-start | bytes 1179656 | tf_op jit(solution)/shard_map/ppermute | solution.py:42
  43.1 6.1 %collective-permute-done.8.rows_ref = bf16[4,3,64,256]{3,2,1,0:T(8,128)(2,1)S(1)} collective-permute-done((bf16[4,3,64,256]{3,2,1,0:T(8,128)(2,1)S(1)}, bf16[4,3,64,256]{3,2,1,0:T(8,128)(2,1)S(1)}, u32[]{:S(2)}, u32[]{:S(2)}) %collective-permute-start.8) | collective-permute-done | bytes 393248 | tf_op jit(solution)/shard_map/ppermute | solution.py:42
  50.0 6.8 %net.7 = f32[3,128,256]{2,1,0:T(8,128)} custom-call(bf16[4,3,64,256]{3,2,1,0:T(8,128)(2,1)} %copy-done.3, bf16[3,256,2048]{2,1,0:T(8,128)(2,1)} %copy-done, bf16[3,256,2048]{2,1,0:T(8,128)(2,1)} %collective-permute-done.3.other_ref, f32[2,3,1,2048]{3,2,1,0:T(1,128)} %pad_maximum_fusion.3.floor_ref, bf16[2,128,128]{2,1,0:T(8,128)(2,1)} %compare_convert_fusion.hot_ref), custom_call_target="tpu_custom_call" | custom-call | tf_op jit(solution)/shard_map/net/pallas_call | solution.py:81
  58.7 6.8 %net.5 = f32[3,128,256]{2,1,0:T(8,128)} custom-call(bf16[4,3,64,256]{3,2,1,0:T(8,128)(2,1)} %collective-permute-done.6.rows_ref, bf16[3,256,2048]{2,1,0:T(8,128)(2,1)} %copy-done, bf16[3,256,2048]{2,1,0:T(8,128)(2,1)} %collective-permute-done.3.other_ref, f32[2,3,1,2048]{3,2,1,0:T(1,128)} %pad_maximum_fusion.3.floor_ref, ...), custom_call_target="tpu_custom_call" | custom-call | tf_op jit(solution)/shard_map/net/pallas_call | solution.py:81
  65.5 1.0 copy_convert_fusion.1
  66.6 6.8 %net.4 = f32[3,128,256]{2,1,0:T(8,128)} custom-call(bf16[4,3,64,256]{3,2,1,0:T(8,128)(2,1)} %copy-done.2, bf16[3,256,2048]{2,1,0:T(8,128)(2,1)} %copy-done, bf16[3,256,2048]{2,1,0:T(8,128)(2,1)} %collective-permute-done.3.other_ref, f32[2,3,1,2048]{3,2,1,0:T(1,128)} %pad_maximum_fusion.3.floor_ref, bf16[2,128,128]{2,1,0:T(8,128)(2,1)} %compare_convert_fusion.hot_ref), custom_call_target="tpu_custom_call" | custom-call | tf_op jit(solution)/shard_map/net/pallas_call | solution.py:81
  73.4 1.0 copy_convert_fusion.2
  74.5 6.8 %net.6 = f32[3,128,256]{2,1,0:T(8,128)} custom-call(bf16[4,3,64,256]{3,2,1,0:T(8,128)(2,1)} %collective-permute-done.7.rows_ref, bf16[3,256,2048]{2,1,0:T(8,128)(2,1)} %copy-done, bf16[3,256,2048]{2,1,0:T(8,128)(2,1)} %collective-permute-done.3.other_ref, f32[2,3,1,2048]{3,2,1,0:T(1,128)} %pad_maximum_fusion.3.floor_ref, ...), custom_call_target="tpu_custom_call" | custom-call | tf_op jit(solution)/shard_map/net/pallas_call | solution.py:81
  81.3 1.0 copy_convert_fusion
  83.6 2.7 %collective-permute-start.10 = (f16[4,3,8,1024]{3,2,1,0:T(8,128)(2,1)S(1)}, f16[4,3,8,1024]{3,2,1,0:T(8,128)(2,1)S(1)}, u32[]{:S(2)}, u32[]{:S(2)}) collective-permute-start(f16[4,3,8,1024]{3,2,1,0:T(8,128)(2,1)S(1)} %pad_maximum_fusion.1), channel_id=1, source_target_pairs={{0,6},{1,25},{2,0},{3,27},{4,2},{5,29},{6,4},{7,31},{8,14},{9,1},{... | collective-permute-start | bytes 589832 | tf_op jit(solution)/shard_map/ppermute | solution.py:42
  86.7 3.0 %collective-permute-done.9 = f16[4,3,8,1024]{3,2,1,0:T(8,128)(2,1)S(1)} collective-permute-done((f16[4,3,8,1024]{3,2,1,0:T(8,128)(2,1)S(1)}, f16[4,3,8,1024]{3,2,1,0:T(8,128)(2,1)S(1)}, u32[]{:S(2)}, u32[]{:S(2)}) %collective-permute-start.9) | collective-permute-done | bytes 196640 | tf_op jit(solution)/shard_map/ppermute | solution.py:42
  89.7 1.9 %collective-permute-done.10 = f16[4,3,8,1024]{3,2,1,0:T(8,128)(2,1)S(1)} collective-permute-done((f16[4,3,8,1024]{3,2,1,0:T(8,128)(2,1)S(1)}, f16[4,3,8,1024]{3,2,1,0:T(8,128)(2,1)S(1)}, u32[]{:S(2)}, u32[]{:S(2)}) %collective-permute-start.10) | collective-permute-done | bytes 196640 | tf_op jit(solution)/shard_map/ppermute | solution.py:42
  91.7 2.1 %collective-permute-done.11 = f16[4,3,8,1024]{3,2,1,0:T(8,128)(2,1)S(1)} collective-permute-done((f16[4,3,8,1024]{3,2,1,0:T(8,128)(2,1)S(1)}, f16[4,3,8,1024]{3,2,1,0:T(8,128)(2,1)S(1)}, u32[]{:S(2)}, u32[]{:S(2)}) %collective-permute-start.11) | collective-permute-done | bytes 196640 | tf_op jit(solution)/shard_map/ppermute | solution.py:42
  94.0 5.2 %collective-permute-start.14 = (f32[3,8,1024]{2,1,0:T(8,128)S(1)}, f32[3,8,1024]{2,1,0:T(8,128)S(1)}, u32[]{:S(2)}, u32[]{:S(2)}) collective-permute-start(f32[3,8,1024]{2,1,0:T(8,128)S(1)} %get-tuple-element.5), channel_id=1, source_target_pairs={{0,16},{1,5},{2,18},{3,7},{4,20},{5,1},{6,22},{7,3},{8,24},{9,13},... | collective-permute-start | bytes 294920 | tf_op jit(solution)/shard_map/ppermute | solution.py:42
  99.2 1.1 collective-permute-done.12
  100.3 2.5 %collective-permute-done.14 = f32[3,8,1024]{2,1,0:T(8,128)S(1)} collective-permute-done((f32[3,8,1024]{2,1,0:T(8,128)S(1)}, f32[3,8,1024]{2,1,0:T(8,128)S(1)}, u32[]{:S(2)}, u32[]{:S(2)}) %collective-permute-start.14) | collective-permute-done | bytes 98336 | tf_op jit(solution)/shard_map/ppermute | solution.py:42
  104.2 1.1 collective-permute-done.15
  105.4 3.2 %collective-permute-start.18 = (f32[3,4,8]{2,1,0:T(4,128)S(1)}, f32[3,4,8]{2,1,0:T(4,128)S(1)}, u32[]{:S(2)}, u32[]{:S(2)}) collective-permute-start(f32[3,4,8]{2,1,0:T(4,128)S(1)} %bitcast_add_fusion), channel_id=1, source_target_pairs={{0,64},{32,96},{64,0},{96,32},{1,65},{33,97},{65,1},{97,33},{2,66}... | collective-permute-start | bytes 1160 | tf_op jit(solution)/shard_map/ppermute | solution.py:165
  108.6 1.1 collective-permute-start.17
  110.6 1.6 %collective-permute-done.17 = f32[3,4,8]{2,1,0:T(4,128)S(1)} collective-permute-done((f32[3,4,8]{2,1,0:T(4,128)S(1)}, f32[3,4,8]{2,1,0:T(4,128)S(1)}, u32[]{:S(2)}, u32[]{:S(2)}) %collective-permute-start.17) | collective-permute-done | bytes 416 | tf_op jit(solution)/shard_map/ppermute | solution.py:165
  112.2 2.3 %collective-permute-done.16 = f32[3,4,8]{2,1,0:T(4,128)S(1)} collective-permute-done((f32[3,4,8]{2,1,0:T(4,128)S(1)}, f32[3,4,8]{2,1,0:T(4,128)S(1)}, u32[]{:S(2)}, u32[]{:S(2)}) %collective-permute-start.16) | collective-permute-done | bytes 416 | tf_op jit(solution)/shard_map/ppermute | solution.py:165
  (97 shorter events, 16.6 us)
Async XLA Ops:
  0.6 14.3 %copy-start.7 = (s32[32]{0:T(128)S(1)}, s32[32]{0:T(128)}, u32[]{:S(2)}) copy-start(s32[32]{0:T(128)} %param.10) | copy-start | bytes 388
  0.6 14.3 %copy-start.6 = (s32[32]{0:T(128)S(1)}, s32[32]{0:T(128)}, u32[]{:S(2)}) copy-start(s32[32]{0:T(128)} %param.11) | copy-start | bytes 388
  0.7 14.3 %copy-start.1 = (bf16[3,256,32,64]{1,3,2,0:T(8,128)(2,1)S(1)}, bf16[3,256,32,64]{1,3,2,0:T(8,128)(2,1)}, u32[]{:S(2)}) copy-start(bf16[3,256,32,64]{1,3,2,0:T(8,128)(2,1)} %param.8) | copy-start | bytes 9437188
  9.1 21.3 %collective-permute-start.2 = (bf16[3,64,256]{2,1,0:T(8,128)(2,1)S(1)}, bf16[3,64,256]{2,1,0:T(8,128)(2,1)S(1)}, u32[]{:S(2)}, u32[]{:S(2)}) collective-permute-start(bf16[3,64,256]{2,1,0:T(8,128)(2,1)S(1)} %bitcast.249), channel_id=1, source_target_pairs={{0,2},{1,9},{2,4},{3,11},{4,6},{5,13},{6,0},{7,15},{8,10},{9,17},{... | collective-permute-start | bytes 294920 | tf_op jit(solution)/shard_map/ppermute | solution.py:42
  10.8 19.0 %collective-permute-start.1 = (bf16[3,64,256]{2,1,0:T(8,128)(2,1)S(1)}, bf16[3,64,256]{2,1,0:T(8,128)(2,1)S(1)}, u32[]{:S(2)}, u32[]{:S(2)}) collective-permute-start(bf16[3,64,256]{2,1,0:T(8,128)(2,1)S(1)} %bitcast.250), channel_id=1, source_target_pairs={{0,4},{1,17},{2,6},{3,19},{4,0},{5,21},{6,2},{7,23},{8,12},{9,25},... | collective-permute-start | bytes 294920 | tf_op jit(solution)/shard_map/ppermute | solution.py:42
  13.5 14.7 %collective-permute-start = (bf16[3,64,256]{2,1,0:T(8,128)(2,1)S(1)}, bf16[3,64,256]{2,1,0:T(8,128)(2,1)}, u32[]{:S(2)}, u32[]{:S(2)}) collective-permute-start(bf16[3,64,256]{2,1,0:T(8,128)(2,1)S(1)} %bitcast.251), channel_id=1, source_target_pairs={{0,6},{1,25},{2,0},{3,27},{4,2},{5,29},{6,4},{7,31},{8,14},{9,1},{... | collective-permute-start | bytes 294920 | tf_op jit(solution)/shard_map/ppermute | solution.py:42
  14.9 13.2 %collective-permute-start.5 = (s32[32]{0:T(128)S(1)}, s32[32]{0:T(128)S(1)}, u32[]{:S(2)}, u32[]{:S(2)}) collective-permute-start(s32[32]{0:T(128)S(1)} %copy-done.7), channel_id=1, source_target_pairs={{0,1},{1,0},{2,3},{3,2},{4,5},{5,4},{6,7},{7,6},{8,9},{9,8},{10,11... | collective-permute-start | bytes 392 | tf_op jit(solution)/shard_map/ppermute | solution.py:46
  20.0 3.9 %copy-start.4 = (f32[3,32,64]{2,1,0:T(8,128)S(1)}, f32[3,32,64]{2,1,0:T(8,128)}, u32[]{:S(2)}) copy-start(f32[3,32,64]{2,1,0:T(8,128)} %param.9) | copy-start | bytes 73732
  23.2 26.8 %copy-start = (bf16[3,256,2048]{2,1,0:T(8,128)(2,1)}, bf16[3,256,2048]{2,1,0:T(8,128)(2,1)S(1)}, u32[]{:S(2)}) copy-start(bf16[3,256,2048]{2,1,0:T(8,128)(2,1)S(1)} %copy.48.mine_ref) | copy-start | bytes 9437188
  23.2 26.8 %collective-permute-start.3 = (bf16[3,256,2048]{2,1,0:T(8,128)(2,1)S(1)}, bf16[3,256,2048]{2,1,0:T(8,128)(2,1)}, u32[]{:S(2)}, u32[]{:S(2)}) collective-permute-start(bf16[3,256,2048]{2,1,0:T(8,128)(2,1)S(1)} %copy.48.mine_ref), channel_id=1, source_target_pairs={{0,1},{1,0},{2,3},{3,2},{4,5},{5,4},{6,7},{7,6},{8,9},{9,8},{10,11... | collective-permute-start | bytes 9437192 | tf_op jit(solution)/shard_map/ppermute | solution.py:46
  28.1 12.3 %collective-permute-start.4 = (f32[3,1,2048]{2,1,0:T(1,128)}, f32[3,1,2048]{2,1,0:T(1,128)}, u32[]{:S(2)}, u32[]{:S(2)}) collective-permute-start(f32[3,1,2048]{2,1,0:T(1,128)} %reshape.208), channel_id=1, source_target_pairs={{0,1},{1,0},{2,3},{3,2},{4,5},{5,4},{6,7},{7,6},{8,9},{9,8},{10,11... | collective-permute-start | bytes 73736 | tf_op jit(solution)/shard_map/ppermute | solution.py:46
  35.6 21.2 %copy-start.2 = (bf16[4,3,64,256]{3,2,1,0:T(8,128)(2,1)}, bf16[4,3,64,256]{3,2,1,0:T(8,128)(2,1)S(1)}, u32[]{:S(2)}) copy-start(bf16[4,3,64,256]{3,2,1,0:T(8,128)(2,1)S(1)} %constant_dynamic-slice_fusion.rows_ref) | copy-start | bytes 1179652
  35.6 13.6 %collective-permute-start.8 = (bf16[4,3,64,256]{3,2,1,0:T(8,128)(2,1)S(1)}, bf16[4,3,64,256]{3,2,1,0:T(8,128)(2,1)S(1)}, u32[]{:S(2)}, u32[]{:S(2)}) collective-permute-start(bf16[4,3,64,256]{3,2,1,0:T(8,128)(2,1)S(1)} %constant_dynamic-slice_fusion.rows_ref), channel_id=1, source_target_pairs={{0,24},{1,7},{2,26},{3,1},{4,28},{5,3},{6,30},{7,5},{8,0},{9,15},{... | collective-permute-start | bytes 1179656 | tf_op jit(solution)/shard_map/ppermute | solution.py:42
  41.8 32.7 %collective-permute-start.7 = (bf16[4,3,64,256]{3,2,1,0:T(8,128)(2,1)S(1)}, bf16[4,3,64,256]{3,2,1,0:T(8,128)(2,1)}, u32[]{:S(2)}, u32[]{:S(2)}) collective-permute-start(bf16[4,3,64,256]{3,2,1,0:T(8,128)(2,1)S(1)} %constant_dynamic-slice_fusion.rows_ref), channel_id=1, source_target_pairs={{0,16},{1,5},{2,18},{3,7},{4,20},{5,1},{6,22},{7,3},{8,24},{9,13},... | collective-permute-start | bytes 1179656 | tf_op jit(solution)/shard_map/ppermute | solution.py:42
  41.8 16.9 %collective-permute-start.6 = (bf16[4,3,64,256]{3,2,1,0:T(8,128)(2,1)S(1)}, bf16[4,3,64,256]{3,2,1,0:T(8,128)(2,1)}, u32[]{:S(2)}, u32[]{:S(2)}) collective-permute-start(bf16[4,3,64,256]{3,2,1,0:T(8,128)(2,1)S(1)} %constant_dynamic-slice_fusion.rows_ref), channel_id=1, source_target_pairs={{0,8},{1,3},{2,10},{3,5},{4,12},{5,7},{6,14},{7,1},{8,16},{9,11},{... | collective-permute-start | bytes 1179656 | tf_op jit(solution)/shard_map/ppermute | solution.py:42
  49.2 0.8 copy-start.3
  82.6 7.2 %collective-permute-start.9 = (f16[4,3,8,1024]{3,2,1,0:T(8,128)(2,1)S(1)}, f16[4,3,8,1024]{3,2,1,0:T(8,128)(2,1)S(1)}, u32[]{:S(2)}, u32[]{:S(2)}) collective-permute-start(f16[4,3,8,1024]{3,2,1,0:T(8,128)(2,1)S(1)} %pad_maximum_fusion), channel_id=1, source_target_pairs={{0,2},{1,9},{2,4},{3,11},{4,6},{5,13},{6,0},{7,15},{8,10},{9,17},{... | collective-permute-start | bytes 589832 | tf_op jit(solution)/shard_map/ppermute | solution.py:42
  83.6 8.0 %collective-permute-start.10 = (f16[4,3,8,1024]{3,2,1,0:T(8,128)(2,1)S(1)}, f16[4,3,8,1024]{3,2,1,0:T(8,128)(2,1)S(1)}, u32[]{:S(2)}, u32[]{:S(2)}) collective-permute-start(f16[4,3,8,1024]{3,2,1,0:T(8,128)(2,1)S(1)} %pad_maximum_fusion.1), channel_id=1, source_target_pairs={{0,6},{1,25},{2,0},{3,27},{4,2},{5,29},{6,4},{7,31},{8,14},{9,1},{... | collective-permute-start | bytes 589832 | tf_op jit(solution)/shard_map/ppermute | solution.py:42
  86.5 7.3 %collective-permute-start.11 = (f16[4,3,8,1024]{3,2,1,0:T(8,128)(2,1)S(1)}, f16[4,3,8,1024]{3,2,1,0:T(8,128)(2,1)S(1)}, u32[]{:S(2)}, u32[]{:S(2)}) collective-permute-start(f16[4,3,8,1024]{3,2,1,0:T(8,128)(2,1)S(1)} %pad_maximum_fusion.2), channel_id=1, source_target_pairs={{0,4},{1,17},{2,6},{3,19},{4,0},{5,21},{6,2},{7,23},{8,12},{9,25},... | collective-permute-start | bytes 589832 | tf_op jit(solution)/shard_map/ppermute | solution.py:42
  93.9 6.4 %collective-permute-start.12 = (f32[3,8,1024]{2,1,0:T(8,128)S(1)}, f32[3,8,1024]{2,1,0:T(8,128)S(1)}, u32[]{:S(2)}, u32[]{:S(2)}) collective-permute-start(f32[3,8,1024]{2,1,0:T(8,128)S(1)} %get-tuple-element.4), channel_id=1, source_target_pairs={{0,8},{1,3},{2,10},{3,5},{4,12},{5,7},{6,14},{7,1},{8,16},{9,11},{... | collective-permute-start | bytes 294920 | tf_op jit(solution)/shard_map/ppermute | solution.py:42
  94.0 8.8 %collective-permute-start.14 = (f32[3,8,1024]{2,1,0:T(8,128)S(1)}, f32[3,8,1024]{2,1,0:T(8,128)S(1)}, u32[]{:S(2)}, u32[]{:S(2)}) collective-permute-start(f32[3,8,1024]{2,1,0:T(8,128)S(1)} %get-tuple-element.5), channel_id=1, source_target_pairs={{0,16},{1,5},{2,18},{3,7},{4,20},{5,1},{6,22},{7,3},{8,24},{9,13},... | collective-permute-start | bytes 294920 | tf_op jit(solution)/shard_map/ppermute | solution.py:42
  99.2 4.6 %collective-permute-start.13 = (f32[3,8,1024]{2,1,0:T(8,128)S(1)}, f32[3,8,1024]{2,1,0:T(8,128)S(1)}, u32[]{:S(2)}, u32[]{:S(2)}) collective-permute-start(f32[3,8,1024]{2,1,0:T(8,128)S(1)} %get-tuple-element.6), channel_id=1, source_target_pairs={{0,24},{1,7},{2,26},{3,1},{4,28},{5,3},{6,30},{7,5},{8,0},{9,15},{... | collective-permute-start | bytes 294920 | tf_op jit(solution)/shard_map/ppermute | solution.py:42
  104.1 1.2 %collective-permute-start.15 = (f32[3,4,8]{2,1,0:T(4,128)S(1)}, f32[3,4,8]{2,1,0:T(4,128)S(1)}, u32[]{:S(2)}, u32[]{:S(2)}) collective-permute-start(f32[3,4,8]{2,1,0:T(4,128)S(1)} %dynamic-slice_bitcast_fusion), channel_id=1, source_target_pairs={{0,1},{1,0},{2,3},{3,2},{4,5},{5,4},{6,7},{7,6},{8,9},{9,8},{10,11... | collective-permute-start | bytes 1160 | tf_op jit(solution)/shard_map/ppermute | solution.py:46
  105.4 5.2 %collective-permute-start.18 = (f32[3,4,8]{2,1,0:T(4,128)S(1)}, f32[3,4,8]{2,1,0:T(4,128)S(1)}, u32[]{:S(2)}, u32[]{:S(2)}) collective-permute-start(f32[3,4,8]{2,1,0:T(4,128)S(1)} %bitcast_add_fusion), channel_id=1, source_target_pairs={{0,64},{32,96},{64,0},{96,32},{1,65},{33,97},{65,1},{97,33},{2,66}... | collective-permute-start | bytes 1160 | tf_op jit(solution)/shard_map/ppermute | solution.py:165
  108.6 3.6 %collective-permute-start.17 = (f32[3,4,8]{2,1,0:T(4,128)S(1)}, f32[3,4,8]{2,1,0:T(4,128)S(1)}, u32[]{:S(2)}, u32[]{:S(2)}) collective-permute-start(f32[3,4,8]{2,1,0:T(4,128)S(1)} %bitcast_add_fusion), channel_id=1, source_target_pairs={{0,96},{32,0},{64,32},{96,64},{1,97},{33,1},{65,33},{97,65},{2,98}... | collective-permute-start | bytes 1160 | tf_op jit(solution)/shard_map/ppermute | solution.py:165
  109.6 4.8 %collective-permute-start.16 = (f32[3,4,8]{2,1,0:T(4,128)S(1)}, f32[3,4,8]{2,1,0:T(4,128)S(1)}, u32[]{:S(2)}, u32[]{:S(2)}) collective-permute-start(f32[3,4,8]{2,1,0:T(4,128)S(1)} %bitcast_add_fusion), channel_id=1, source_target_pairs={{0,32},{32,64},{64,96},{96,0},{1,33},{33,65},{65,97},{97,1},{2,34}... | collective-permute-start | bytes 1160 | tf_op jit(solution)/shard_map/ppermute | solution.py:165
  114.6 0.8 copy-start.5

commit v2 on v1

v2 whole, which is shorter than its diff:
```python
import functools

import jax
import jax.numpy as jnp
from jax import lax
from jax.experimental import pallas as pl
from jax.experimental.pallas import tpu as pltpu
from jax.sharding import PartitionSpec as P

STEPS = 3
PATHS = 1024
REPL = 8
SPD = 4
SIDE = 4
BPD = 32
TB = 64
BASIS = 256
ROWS = 64
CHUNK = SIDE * ROWS
OWN = 2 * SPD
GROUP = 4
F32 = jnp.float32
BF16 = jnp.bfloat16


def ring_pairs(shift, stage):
    pairs = []
    for z in range(SIDE):
        for x in range(SIDE):
            for core in range(2):
                if (core + stage) % 2 == 0:
                    to = (z, (x + shift) % SIDE, core)
                else:
                    to = ((z + shift) % SIDE, x, core)
                pairs.append((z * 8 + x * 2 + core, to[0] * 8 + to[1] * 2 + to[2]))
    return pairs


CORE_PAIRS = [(i, i ^ 1) for i in range(2 * SIDE * SIDE)]


def shift_by(value, shift, stage):
    return lax.ppermute(value, "set", ring_pairs(shift, stage))


def swap_core(value):
    return lax.ppermute(value, "set", CORE_PAIRS)


def dot(a, b, dims):
    return lax.dot_general(a, b, (dims, ((), ())), preferred_element_type=F32)


def net_kernel(
    live_ref, rows_ref, mine_ref, other_ref, floor_ref, hot_ref, out_ref, sums_ref, held_ref, sems
):
    copies = [
        [
            pltpu.make_async_copy(source.at[step], held_ref.at[step, half], sems.at[step, half])
            for half, source in enumerate((mine_ref, other_ref))
        ]
        for step in range(STEPS)
    ]
    for pair in copies:
        for copy in pair:
            copy.start()
    trade = lax.broadcasted_iota(jnp.int32, (TB, CHUNK), 0)
    for step in range(STEPS):
        rows = rows_ref[:, step].reshape(CHUNK, BASIS)
        for half in range(2):
            copies[step][half].wait()
            for first in range(0, BPD, GROUP):
                trades = slice(first * TB, (first + GROUP) * TB)
                values = dot(held_ref[step, half, trades, :], rows, ((1,), (1,)))
                for block in range(GROUP):
                    spot = half * BPD + first + block
                    floor = floor_ref[step, :, spot : spot + 1]
                    value = jnp.maximum(values[block * TB : (block + 1) * TB], floor)
                    value = jnp.where(trade < live_ref[spot], value, 0.0)
                    sums = value[:8]
                    for part in range(8, TB, 8):
                        sums = sums + value[part : part + 8]
                    sums_ref[spot * 8 : spot * 8 + 8, :] = sums
        sums = sums_ref[...]
        high = sums.astype(BF16)
        low = (sums - high.astype(F32)).astype(BF16)
        hot = hot_ref[...]
        out_ref[step] = dot(hot, high, ((1,), (0,))) + dot(hot, low, ((1,), (0,)))


VMEM = pl.BlockSpec(memory_space=pltpu.VMEM)
SMEM = pl.BlockSpec(memory_space=pltpu.SMEM)
ANY = pl.BlockSpec(memory_space=pl.ANY)


def net(rows, live, mine, other, floors, hot):
    mine = pltpu.with_memory_space_constraint(mine, pltpu.HBM)
    return pl.pallas_call(
        net_kernel,
        in_specs=[SMEM, VMEM, ANY, ANY, VMEM, VMEM],
        out_specs=VMEM,
        out_shape=jax.ShapeDtypeStruct((STEPS, SIDE * SIDE * OWN, CHUNK), F32),
        scratch_shapes=[
            pltpu.VMEM((2 * BPD * 8, CHUNK), F32),
            pltpu.VMEM((STEPS, 2, BPD * TB, BASIS), BF16),
            pltpu.SemaphoreType.DMA((STEPS, 2)),
        ],
        compiler_params=pltpu.CompilerParams(vmem_limit_bytes=20 << 20),
        cost_estimate=pl.CostEstimate(
            flops=4 * STEPS * CHUNK * BPD * TB * BASIS, bytes_accessed=1 << 20, transcendentals=0
        ),
        name="net",
    )(live, rows, mine, other, floors, hot)


def line_kernel(first_ref, *refs):
    out_ref = refs[-1]
    for step in range(SIDE):
        out_ref[lax.rem(first_ref[0] + step, SIDE)] = refs[step][...]


def make_line(first, parts):
    return pl.pallas_call(
        line_kernel,
        in_specs=[SMEM] + [pl.BlockSpec()] * SIDE,
        out_specs=pl.BlockSpec(),
        out_shape=jax.ShapeDtypeStruct((SIDE, STEPS, ROWS, BASIS), BF16),
        compiler_params=pltpu.CompilerParams(vmem_limit_bytes=4 << 20),
        name="line",
    )(first.reshape(1), *parts)


def body(scenarios, projection, coefs, exercise, block_set, block_live):
    place = lax.axis_index("set")
    z, x, core = place // 8, (place // 2) % SIDE, place % 2

    basis = jnp.tanh(
        jnp.dot(
            scenarios.reshape(STEPS * ROWS, -1), projection, preferred_element_type=F32
        )
    ).astype(BF16)
    basis = basis.reshape(STEPS, ROWS, BASIS)
    weights = jnp.transpose(coefs, (0, 2, 3, 1)).reshape(STEPS, BPD * TB, BASIS)

    first = jnp.where(core == 0, x, z)
    line = make_line(first, [basis] + [shift_by(basis, shift, 0) for shift in (3, 2, 1)])

    other_weights = swap_core(weights)
    other_floors = swap_core(exercise)
    blocks = jnp.stack([block_set, block_live])
    blocks = jnp.concatenate([blocks, swap_core(blocks)], axis=1)

    near = (first + jnp.arange(SIDE)) % SIDE
    second = jnp.where(core == 0, z, x)
    far = (second + jnp.arange(SIDE)) % SIDE
    chip = jnp.where(
        core == 0, far[None, :] * SIDE + near[:, None], near[:, None] * SIDE + far[None, :]
    )
    ids = (chip[:, :, None] * OWN + jnp.arange(OWN)).reshape(-1)
    owners = jnp.repeat(blocks[0], 8)
    hot = (ids[:, None] == owners[None, :]).astype(BF16)
    both_floors = jnp.swapaxes(jnp.concatenate([exercise, other_floors], axis=1), 1, 2)

    run = functools.partial(
        net, live=blocks[1], mine=weights, other=other_weights, floors=both_floors, hot=hot
    )
    arrived = {shift: shift_by(line, shift, 1) for shift in (1, 3, 2)}
    terms, sent = {}, {}
    rows = line
    for shift, following in ((0, 1), (1, 3), (3, 2), (2, None)):
        terms[shift] = run(rows).reshape(STEPS, SIDE, SIDE, OWN, CHUNK)
        sent[shift] = terms[shift][:, 1:].astype(jnp.float16)
        if following:
            rows, sent[shift] = lax.optimization_barrier((arrived[following], sent[shift]))

    def message(values, near_step):
        return jnp.stack(
            [
                jnp.concatenate(
                    [values[(spot - far_step) % SIDE][:, near_step, far_step] for spot in range(SIDE)],
                    axis=2,
                )
                for far_step in range(SIDE)
            ]
        )

    held = message(terms, 0)
    for shift in (1, 3, 2):
        held = held + shift_by(message(sent, shift - 1), shift, 0).astype(F32)
    netted = held[0]
    for shift in (1, 3, 2):
        half = (held[shift] * 0.5).astype(jnp.float16)
        netted = netted + shift_by(half, shift, 1).astype(F32) * 2.0

    positive = jnp.maximum(netted, 0.0).reshape(STEPS * OWN, SIDE * CHUNK)
    pick = (jnp.arange(SIDE * CHUNK)[:, None] % REPL == jnp.arange(REPL)[None, :]).astype(F32)
    sums = jnp.dot(positive, pick, precision=lax.Precision.HIGHEST).reshape(STEPS, 2, SPD, REPL)
    kept = lax.dynamic_index_in_dim(sums, core, 1, keepdims=False)
    given = lax.dynamic_index_in_dim(sums, 1 - core, 1, keepdims=False)
    sums = kept + swap_core(given)
    total = sums
    for shift in (1, 3, 2):
        total = total + lax.ppermute(
            sums, "rep", [(i, (i + shift) % SIDE) for i in range(SIDE)]
        )
    per_replicate = total * (1.0 / PATHS)
    exposure = jnp.mean(per_replicate, axis=2)
    deviation = per_replicate - exposure[:, :, None]
    spread = jnp.sqrt(
        PATHS * jnp.sum(deviation * deviation, axis=2) / ((REPL - 1) * REPL)
    )
    return (exposure, spread)


def solution(mesh):
    return jax.shard_map(
        body,
        mesh=mesh,
        in_specs=(
            P(None, ("rep", "set"), None),
            P(),
            P(None, None, "set", None),
            P(None, "set", None),
            P("set"),
            P("set"),
        ),
        out_specs=(P(None, "set"), P(None, "set")),
        check_vma=False,
    )
```

time: 116 us -> 86.8 us (0.75)
  local copies, waits for them, and re-layouts: 15.6 us -> 3.42 us
  other arithmetic: 13.9 us -> 4.2 us
  Pallas kernels: 27.2 us -> 22.9 us
  starting transfers between devices: 26.1 us -> 23.9 us
    unnamed x23 -> x19, local copies, waits for them, and re-layouts: 7.15 us -> 1.59 us
    select_n x1 -> x0, other arithmetic: 5 us -> none  [body(): weights = jnp.where(live[None, None], coefs, 0).astype(BF16)]
    another operation x25 -> x24, other arithmetic: 6.04 us -> 1.14 us  [the longest x1 0.57 us: body(): blocks = jnp.stack([block_set, block_live])]
    pallas_call x4 -> x5, Pallas kernels: 27.2 us -> 22.9 us  [the longest x4 22.9 us: net(): pl.pallas_call(net_kernel, in_specs=[SMEM, VMEM, ANY, ANY, VMEM, VMEM], o...]
    reshape x2 -> x0, local copies, waits for them, and re-layouts: 3.93 us -> none  [the longest x1 3.21 us: body(): weights = jnp.swapaxes(weights, 2, 3).reshape(STEPS, BASIS, TB * BPD)]
    ppermute x12, starting transfers between devices: 20.2 us -> 18 us  [shift_by(): return lax.ppermute(value, 'set', ring_pairs(shift, stage))]
    another operation x4 -> x0, local copies, waits for them, and re-layouts: 1.45 us -> none  [the longest x1 0.71 us: body(): both_floors = jnp.stack([floors, other_floors])]
  transfers between devices with their start and end apart: 19 -> 19, of which waited for: 10 -> 9; matrix products, arithmetic and copies ran while one was open for 23% -> 17% of each run, Pallas kernels for 18% -> 20%
where the time goes in v2:
time: 86.8 us; the launch traced here: 86.5 us
  starting transfers between devices  23.9 us (28%)
  Pallas kernels  22.9 us (26%)
  waiting for transfers between devices  22.2 us (26%)
  matrix products  8.67 us (10%)
  other arithmetic  4.2 us (5%)
  local copies, waits for them, and re-layouts  3.42 us (4%)
  between operations  1.19 us (1%)
    pallas_call x4, Pallas kernels, net(): pl.pallas_call(net_kernel, in_specs=[SMEM, VMEM, ANY, ANY, VMEM, VMEM], o...  22.9 us
    ppermute x12, starting transfers between devices, shift_by(): return lax.ppermute(value, 'set', ring_pairs(shift, stage))  18 us
    ppermute x12, waiting for transfers between devices, shift_by(): return lax.ppermute(value, 'set', ring_pairs(shift, stage))  17.2 us
    dot_general x1, matrix products, body(): jnp.dot(scenarios.reshape(STEPS * ROWS, -1), projection, preferred_elemen...  8.45 us
    ppermute x3, starting transfers between devices, body(): lax.ppermute(sums, 'rep', [(i, (i + shift) % SIDE) for i in range(SIDE)])  5.22 us
    ppermute x3, waiting for transfers between devices, body(): lax.ppermute(sums, 'rep', [(i, (i + shift) % SIDE) for i in range(SIDE)])  3.87 us
  transfers between devices with their start and end apart: 19, of which 9 were waited for; matrix products, arithmetic and copies ran while one was open for 17% of the time, Pallas kernels for 20%

profile of v2, /device:TPU:0, one launch (start us, length us, event | category | flops | bytes accessed | tf_op | source)
XLA Modules:
  0.0 86.5 jit_solution(1898409796449325266)
XLA Ops:
  0.7 8.5 %fusion = bf16[192,256]{1,0:T(8,128)(2,1)S(1)} fusion(bf16[192,20000]{1,0:T(8,128)(2,1)} %bitcast.265, bf16[20000,256]{1,0:T(8,128)(2,1)} %param.7), kind=kOutput, calls=%fused_computation.1 | convolution fusion | flops 1966129152 | bytes 18018304 | tf_op jit(solution)/shard_map/dot_general | solution.py:138
  9.2 1.7 %collective-permute-start.3 = (bf16[3,64,256]{2,1,0:T(8,128)(2,1)S(1)}, bf16[3,64,256]{2,1,0:T(8,128)(2,1)S(1)}, u32[]{:S(2)}, u32[]{:S(2)}) collective-permute-start(bf16[3,64,256]{2,1,0:T(8,128)(2,1)S(1)} %bitcast.256), channel_id=1, source_target_pairs={{0,2},{1,9},{2,4},{3,11},{4,6},{5,13},{6,0},{7,15},{8,10},{9,17},{... | collective-permute-start | bytes 294920 | tf_op jit(solution)/shard_map/ppermute | solution.py:43
  10.9 2.7 %collective-permute-start.2 = (bf16[3,64,256]{2,1,0:T(8,128)(2,1)S(1)}, bf16[3,64,256]{2,1,0:T(8,128)(2,1)S(1)}, u32[]{:S(2)}, u32[]{:S(2)}) collective-permute-start(bf16[3,64,256]{2,1,0:T(8,128)(2,1)S(1)} %bitcast.257), channel_id=1, source_target_pairs={{0,4},{1,17},{2,6},{3,19},{4,0},{5,21},{6,2},{7,23},{8,12},{9,25},... | collective-permute-start | bytes 294920 | tf_op jit(solution)/shard_map/ppermute | solution.py:43
  13.6 1.4 %collective-permute-start.1 = (bf16[3,64,256]{2,1,0:T(8,128)(2,1)S(1)}, bf16[3,64,256]{2,1,0:T(8,128)(2,1)S(1)}, u32[]{:S(2)}, u32[]{:S(2)}) collective-permute-start(bf16[3,64,256]{2,1,0:T(8,128)(2,1)S(1)} %bitcast.258), channel_id=1, source_target_pairs={{0,6},{1,25},{2,0},{3,27},{4,2},{5,29},{6,4},{7,31},{8,14},{9,1},{... | collective-permute-start | bytes 294920 | tf_op jit(solution)/shard_map/ppermute | solution.py:43
  16.4 1.5 %copy.41 = f32[3,32,64]{1,2,0:T(8,128)} copy(f32[3,32,64]{2,1,0:T(8,128)} %param.9) | data formatting | bytes 49152 | tf_op args[3]
  17.9 0.7 pad_add_fusion.1
  18.7 0.7 broadcast_in_dim.2
  19.4 0.8 eq.43
  20.3 1.0 %maximum_bitcast_fusion.floor_ref = f32[3,64,64]{2,1,0:T(8,128)S(1)} fusion(f32[3,32,64]{1,2,0:T(8,128)} %collective-permute-done.5, f32[3,32,64]{1,2,0:T(8,128)} %copy.41), kind=kLoop, calls=%fused_computation.23 | loop fusion | flops 12288 | bytes 98304 | tf_op jit(solution)/shard_map/transpose | solution.py:162
  21.4 4.1 %collective-permute-start.8 = (bf16[4,3,64,256]{3,2,1,0:T(8,128)(2,1)S(1)}, bf16[4,3,64,256]{3,2,1,0:T(8,128)(2,1)S(1)}, u32[]{:S(2)}, u32[]{:S(2)}) collective-permute-start(bf16[4,3,64,256]{3,2,1,0:T(8,128)(2,1)S(1)} %line.1.rows_ref), channel_id=1, source_target_pairs={{0,24},{1,7},{2,26},{3,1},{4,28},{5,3},{6,30},{7,5},{8,0},{9,15},{... | collective-permute-start | bytes 1179656 | tf_op jit(solution)/shard_map/ppermute | solution.py:43
  25.5 1.3 %collective-permute-start.6 = (bf16[4,3,64,256]{3,2,1,0:T(8,128)(2,1)S(1)}, bf16[4,3,64,256]{3,2,1,0:T(8,128)(2,1)S(1)}, u32[]{:S(2)}, u32[]{:S(2)}) collective-permute-start(bf16[4,3,64,256]{3,2,1,0:T(8,128)(2,1)S(1)} %line.1.rows_ref), channel_id=1, source_target_pairs={{0,8},{1,3},{2,10},{3,5},{4,12},{5,7},{6,14},{7,1},{8,16},{9,11},{... | collective-permute-start | bytes 1179656 | tf_op jit(solution)/shard_map/ppermute | solution.py:43
  26.8 5.7 %net.4 = f32[3,128,256]{2,1,0:T(8,128)S(1)} custom-call(s32[64]{0:T(128)S(1)} %get-tuple-element.84.live_ref, bf16[4,3,64,256]{3,2,1,0:T(8,128)(2,1)S(1)} %line.1.rows_ref, bf16[3,2048,256]{2,1,0:T(8,128)(2,1)} %bitcast.261, bf16[3,2048,256]{2,1,0:T(8,128)(2,1)S(1)} %collective-permute-done.4.other_ref, f32[3,64,64]{2,1,0:T(8,128)S(1)} %maximum_bitcast_fusion.floor_ref, ...), custom_call_target="tpu_custom_call" | custom-call | flops 1610612736 | bytes 1048576 | tf_op jit(solution)/shard_map/net/pallas_call | solution.py:98
  32.6 6.2 %collective-permute-done.6.rows_ref = bf16[4,3,64,256]{3,2,1,0:T(8,128)(2,1)S(1)} collective-permute-done((bf16[4,3,64,256]{3,2,1,0:T(8,128)(2,1)S(1)}, bf16[4,3,64,256]{3,2,1,0:T(8,128)(2,1)S(1)}, u32[]{:S(2)}, u32[]{:S(2)}) %collective-permute-start.6) | collective-permute-done | bytes 393248 | tf_op jit(solution)/shard_map/ppermute | solution.py:43
  38.7 5.7 %net.5 = f32[3,128,256]{2,1,0:T(8,128)S(1)} custom-call(s32[64]{0:T(128)S(1)} %get-tuple-element.84.live_ref, bf16[4,3,64,256]{3,2,1,0:T(8,128)(2,1)S(1)} %collective-permute-done.6.rows_ref, bf16[3,2048,256]{2,1,0:T(8,128)(2,1)} %bitcast.262, bf16[3,2048,256]{2,1,0:T(8,128)(2,1)S(1)} %collective-permute-done.4.other_ref, ...), custom_call_target="tpu_custom_call" | custom-call | flops 1610612736 | bytes 1048576 | tf_op jit(solution)/shard_map/net/pallas_call | solution.py:98
  44.5 5.7 %net.6 = f32[3,128,256]{2,1,0:T(8,128)S(1)} custom-call(s32[64]{0:T(128)S(1)} %get-tuple-element.84.live_ref, bf16[4,3,64,256]{3,2,1,0:T(8,128)(2,1)S(1)} %collective-permute-done.8.rows_ref, bf16[3,2048,256]{2,1,0:T(8,128)(2,1)} %bitcast.263, bf16[3,2048,256]{2,1,0:T(8,128)(2,1)S(1)} %collective-permute-done.4.other_ref, ...), custom_call_target="tpu_custom_call" | custom-call | flops 1610612736 | bytes 1048576 | tf_op jit(solution)/shard_map/net/pallas_call | solution.py:98
  50.3 5.7 %net.7 = f32[3,128,256]{2,1,0:T(8,128)S(1)} custom-call(s32[64]{0:T(128)S(1)} %get-tuple-element.84.live_ref, bf16[4,3,64,256]{3,2,1,0:T(8,128)(2,1)S(1)} %collective-permute-done.7.rows_ref, bf16[3,2048,256]{2,1,0:T(8,128)(2,1)} %bitcast.264, bf16[3,2048,256]{2,1,0:T(8,128)(2,1)S(1)} %collective-permute-done.4.other_ref, ...), custom_call_target="tpu_custom_call" | custom-call | flops 1610612736 | bytes 1048576 | tf_op jit(solution)/shard_map/net/pallas_call | solution.py:98
  56.6 0.7 collective-permute-start.9
  57.4 2.7 %collective-permute-start.10 = (f16[4,3,8,1024]{3,2,1,0:T(8,128)(2,1)S(1)}, f16[4,3,8,1024]{3,2,1,0:T(8,128)(2,1)S(1)}, u32[]{:S(2)}, u32[]{:S(2)}) collective-permute-start(f16[4,3,8,1024]{3,2,1,0:T(8,128)(2,1)S(1)} %pad_maximum_fusion.1), channel_id=1, source_target_pairs={{0,6},{1,25},{2,0},{3,27},{4,2},{5,29},{6,4},{7,31},{8,14},{9,1},{... | collective-permute-start | bytes 589832 | tf_op jit(solution)/shard_map/ppermute | solution.py:43
  60.5 3.0 %collective-permute-done.9 = f16[4,3,8,1024]{3,2,1,0:T(8,128)(2,1)S(1)} collective-permute-done((f16[4,3,8,1024]{3,2,1,0:T(8,128)(2,1)S(1)}, f16[4,3,8,1024]{3,2,1,0:T(8,128)(2,1)S(1)}, u32[]{:S(2)}, u32[]{:S(2)}) %collective-permute-start.9) | collective-permute-done | bytes 196640 | tf_op jit(solution)/shard_map/ppermute | solution.py:43
  63.6 1.9 %collective-permute-done.10 = f16[4,3,8,1024]{3,2,1,0:T(8,128)(2,1)S(1)} collective-permute-done((f16[4,3,8,1024]{3,2,1,0:T(8,128)(2,1)S(1)}, f16[4,3,8,1024]{3,2,1,0:T(8,128)(2,1)S(1)}, u32[]{:S(2)}, u32[]{:S(2)}) %collective-permute-start.10) | collective-permute-done | bytes 196640 | tf_op jit(solution)/shard_map/ppermute | solution.py:43
  65.5 2.6 %collective-permute-done.11 = f16[4,3,8,1024]{3,2,1,0:T(8,128)(2,1)S(1)} collective-permute-done((f16[4,3,8,1024]{3,2,1,0:T(8,128)(2,1)S(1)}, f16[4,3,8,1024]{3,2,1,0:T(8,128)(2,1)S(1)}, u32[]{:S(2)}, u32[]{:S(2)}) %collective-permute-start.11) | collective-permute-done | bytes 196640 | tf_op jit(solution)/shard_map/ppermute | solution.py:43
  68.3 1.9 %collective-permute-start.14 = (f16[3,8,1024]{2,1,0:T(8,128)(2,1)S(1)}, f16[3,8,1024]{2,1,0:T(8,128)(2,1)S(1)}, u32[]{:S(2)}, u32[]{:S(2)}) collective-permute-start(f16[3,8,1024]{2,1,0:T(8,128)(2,1)S(1)} %get-tuple-element.17), channel_id=1, source_target_pairs={{0,16},{1,5},{2,18},{3,7},{4,20},{5,1},{6,22},{7,3},{8,24},{9,13},... | collective-permute-start | bytes 147464 | tf_op jit(solution)/shard_map/ppermute | solution.py:43
  70.2 1.4 %collective-permute-start.13 = (f16[3,8,1024]{2,1,0:T(8,128)(2,1)S(1)}, f16[3,8,1024]{2,1,0:T(8,128)(2,1)S(1)}, u32[]{:S(2)}, u32[]{:S(2)}) collective-permute-start(f16[3,8,1024]{2,1,0:T(8,128)(2,1)S(1)} %get-tuple-element.18), channel_id=1, source_target_pairs={{0,24},{1,7},{2,26},{3,1},{4,28},{5,3},{6,30},{7,5},{8,0},{9,15},{... | collective-permute-start | bytes 147464 | tf_op jit(solution)/shard_map/ppermute | solution.py:43
  71.5 2.6 %collective-permute-done.12 = f16[3,8,1024]{2,1,0:T(8,128)(2,1)S(1)} collective-permute-done((f16[3,8,1024]{2,1,0:T(8,128)(2,1)S(1)}, f16[3,8,1024]{2,1,0:T(8,128)(2,1)S(1)}, u32[]{:S(2)}, u32[]{:S(2)}) %collective-permute-start.12) | collective-permute-done | bytes 49184 | tf_op jit(solution)/shard_map/ppermute | solution.py:43
  74.1 0.9 collective-permute-done.13
  75.4 1.1 %collective-permute-done.15 = f32[3,4,8]{2,1,0:T(4,128)S(1)} collective-permute-done((f32[3,4,8]{2,1,0:T(4,128)S(1)}, f32[3,4,8]{2,1,0:T(4,128)S(1)}, u32[]{:S(2)}, u32[]{:S(2)}) %collective-permute-start.15) | collective-permute-done | bytes 416 | tf_op jit(solution)/shard_map/ppermute | solution.py:47
  76.6 3.2 %collective-permute-start.18 = (f32[3,4,8]{2,1,0:T(4,128)S(1)}, f32[3,4,8]{2,1,0:T(4,128)S(1)}, u32[]{:S(2)}, u32[]{:S(2)}) collective-permute-start(f32[3,4,8]{2,1,0:T(4,128)S(1)} %bitcast_add_fusion), channel_id=1, source_target_pairs={{0,64},{32,96},{64,0},{96,32},{1,65},{33,97},{65,1},{97,33},{2,66}... | collective-permute-start | bytes 1160 | tf_op jit(solution)/shard_map/ppermute | solution.py:203
  79.7 1.1 %collective-permute-start.17 = (f32[3,4,8]{2,1,0:T(4,128)S(1)}, f32[3,4,8]{2,1,0:T(4,128)S(1)}, u32[]{:S(2)}, u32[]{:S(2)}) collective-permute-start(f32[3,4,8]{2,1,0:T(4,128)S(1)} %bitcast_add_fusion), channel_id=1, source_target_pairs={{0,96},{32,0},{64,32},{96,64},{1,97},{33,1},{65,33},{97,65},{2,98}... | collective-permute-start | bytes 1160 | tf_op jit(solution)/shard_map/ppermute | solution.py:203
  80.8 1.0 %collective-permute-start.16 = (f32[3,4,8]{2,1,0:T(4,128)S(1)}, f32[3,4,8]{2,1,0:T(4,128)S(1)}, u32[]{:S(2)}, u32[]{:S(2)}) collective-permute-start(f32[3,4,8]{2,1,0:T(4,128)S(1)} %bitcast_add_fusion), channel_id=1, source_target_pairs={{0,32},{32,64},{64,96},{96,0},{1,33},{33,65},{65,97},{97,1},{2,34}... | collective-permute-start | bytes 1160 | tf_op jit(solution)/shard_map/ppermute | solution.py:203
  81.8 1.6 %collective-permute-done.17 = f32[3,4,8]{2,1,0:T(4,128)S(1)} collective-permute-done((f32[3,4,8]{2,1,0:T(4,128)S(1)}, f32[3,4,8]{2,1,0:T(4,128)S(1)}, u32[]{:S(2)}, u32[]{:S(2)}) %collective-permute-start.17) | collective-permute-done | bytes 416 | tf_op jit(solution)/shard_map/ppermute | solution.py:203
  83.4 2.3 %collective-permute-done.16 = f32[3,4,8]{2,1,0:T(4,128)S(1)} collective-permute-done((f32[3,4,8]{2,1,0:T(4,128)S(1)}, f32[3,4,8]{2,1,0:T(4,128)S(1)}, u32[]{:S(2)}, u32[]{:S(2)}) %collective-permute-start.16) | collective-permute-done | bytes 416 | tf_op jit(solution)/shard_map/ppermute | solution.py:203
  85.9 0.6 multiply_sqrt_fusion
  (86 shorter events, 3.3 us)
Async XLA Ops:
  0.6 26.2 %collective-permute-start.4 = (bf16[3,2048,256]{2,1,0:T(8,128)(2,1)}, bf16[3,2048,256]{2,1,0:T(8,128)(2,1)S(1)}, u32[]{:S(2)}, u32[]{:S(2)}) collective-permute-start(bf16[3,2048,256]{2,1,0:T(8,128)(2,1)} %bitcast.260), channel_id=1, source_target_pairs={{0,1},{1,0},{2,3},{3,2},{4,5},{5,4},{6,7},{7,6},{8,9},{9,8},{10,11... | collective-permute-start | bytes 9437192 | tf_op jit(solution)/shard_map/ppermute | solution.py:47
  0.7 14.3 %copy-start.1 = (s32[32]{0:T(128)S(1)}, s32[32]{0:T(128)}, u32[]{:S(2)}) copy-start(s32[32]{0:T(128)} %param.11) | copy-start | bytes 388
  0.7 14.3 %copy-start.2 = (s32[32]{0:T(128)S(1)}, s32[32]{0:T(128)}, u32[]{:S(2)}) copy-start(s32[32]{0:T(128)} %param.10) | copy-start | bytes 388
  9.2 12.2 %collective-permute-start.3 = (bf16[3,64,256]{2,1,0:T(8,128)(2,1)S(1)}, bf16[3,64,256]{2,1,0:T(8,128)(2,1)S(1)}, u32[]{:S(2)}, u32[]{:S(2)}) collective-permute-start(bf16[3,64,256]{2,1,0:T(8,128)(2,1)S(1)} %bitcast.256), channel_id=1, source_target_pairs={{0,2},{1,9},{2,4},{3,11},{4,6},{5,13},{6,0},{7,15},{8,10},{9,17},{... | collective-permute-start | bytes 294920 | tf_op jit(solution)/shard_map/ppermute | solution.py:43
  10.9 10.5 %collective-permute-start.2 = (bf16[3,64,256]{2,1,0:T(8,128)(2,1)S(1)}, bf16[3,64,256]{2,1,0:T(8,128)(2,1)S(1)}, u32[]{:S(2)}, u32[]{:S(2)}) collective-permute-start(bf16[3,64,256]{2,1,0:T(8,128)(2,1)S(1)} %bitcast.257), channel_id=1, source_target_pairs={{0,4},{1,17},{2,6},{3,19},{4,0},{5,21},{6,2},{7,23},{8,12},{9,25},... | collective-permute-start | bytes 294920 | tf_op jit(solution)/shard_map/ppermute | solution.py:43
  13.6 7.8 %collective-permute-start.1 = (bf16[3,64,256]{2,1,0:T(8,128)(2,1)S(1)}, bf16[3,64,256]{2,1,0:T(8,128)(2,1)S(1)}, u32[]{:S(2)}, u32[]{:S(2)}) collective-permute-start(bf16[3,64,256]{2,1,0:T(8,128)(2,1)S(1)} %bitcast.258), channel_id=1, source_target_pairs={{0,6},{1,25},{2,0},{3,27},{4,2},{5,29},{6,4},{7,31},{8,14},{9,1},{... | collective-permute-start | bytes 294920 | tf_op jit(solution)/shard_map/ppermute | solution.py:43
  15.6 2.3 %collective-permute-start = (s32[2,32]{1,0:T(2,128)}, s32[2,32]{1,0:T(2,128)}, u32[]{:S(2)}, u32[]{:S(2)}) collective-permute-start(s32[2,32]{1,0:T(2,128)} %pad_add_fusion), channel_id=1, source_target_pairs={{0,1},{1,0},{2,3},{3,2},{4,5},{5,4},{6,7},{7,6},{8,9},{9,8},{10,11... | collective-permute-start | bytes 776 | tf_op jit(solution)/shard_map/ppermute | solution.py:47
  17.9 2.4 %collective-permute-start.5 = (f32[3,32,64]{1,2,0:T(8,128)}, f32[3,32,64]{1,2,0:T(8,128)}, u32[]{:S(2)}, u32[]{:S(2)}) collective-permute-start(f32[3,32,64]{1,2,0:T(8,128)} %copy.41), channel_id=1, source_target_pairs={{0,1},{1,0},{2,3},{3,2},{4,5},{5,4},{6,7},{7,6},{8,9},{9,8},{10,11... | collective-permute-start | bytes 73736 | tf_op jit(solution)/shard_map/ppermute | solution.py:47
  21.4 23.1 %collective-permute-start.8 = (bf16[4,3,64,256]{3,2,1,0:T(8,128)(2,1)S(1)}, bf16[4,3,64,256]{3,2,1,0:T(8,128)(2,1)S(1)}, u32[]{:S(2)}, u32[]{:S(2)}) collective-permute-start(bf16[4,3,64,256]{3,2,1,0:T(8,128)(2,1)S(1)} %line.1.rows_ref), channel_id=1, source_target_pairs={{0,24},{1,7},{2,26},{3,1},{4,28},{5,3},{6,30},{7,5},{8,0},{9,15},{... | collective-permute-start | bytes 1179656 | tf_op jit(solution)/shard_map/ppermute | solution.py:43
  25.5 24.8 %collective-permute-start.7 = (bf16[4,3,64,256]{3,2,1,0:T(8,128)(2,1)S(1)}, bf16[4,3,64,256]{3,2,1,0:T(8,128)(2,1)S(1)}, u32[]{:S(2)}, u32[]{:S(2)}) collective-permute-start(bf16[4,3,64,256]{3,2,1,0:T(8,128)(2,1)S(1)} %line.1.rows_ref), channel_id=1, source_target_pairs={{0,16},{1,5},{2,18},{3,7},{4,20},{5,1},{6,22},{7,3},{8,24},{9,13},... | collective-permute-start | bytes 1179656 | tf_op jit(solution)/shard_map/ppermute | solution.py:43
  25.5 13.2 %collective-permute-start.6 = (bf16[4,3,64,256]{3,2,1,0:T(8,128)(2,1)S(1)}, bf16[4,3,64,256]{3,2,1,0:T(8,128)(2,1)S(1)}, u32[]{:S(2)}, u32[]{:S(2)}) collective-permute-start(bf16[4,3,64,256]{3,2,1,0:T(8,128)(2,1)S(1)} %line.1.rows_ref), channel_id=1, source_target_pairs={{0,8},{1,3},{2,10},{3,5},{4,12},{5,7},{6,14},{7,1},{8,16},{9,11},{... | collective-permute-start | bytes 1179656 | tf_op jit(solution)/shard_map/ppermute | solution.py:43
  56.6 6.9 %collective-permute-start.9 = (f16[4,3,8,1024]{3,2,1,0:T(8,128)(2,1)S(1)}, f16[4,3,8,1024]{3,2,1,0:T(8,128)(2,1)S(1)}, u32[]{:S(2)}, u32[]{:S(2)}) collective-permute-start(f16[4,3,8,1024]{3,2,1,0:T(8,128)(2,1)S(1)} %pad_maximum_fusion), channel_id=1, source_target_pairs={{0,2},{1,9},{2,4},{3,11},{4,6},{5,13},{6,0},{7,15},{8,10},{9,17},{... | collective-permute-start | bytes 589832 | tf_op jit(solution)/shard_map/ppermute | solution.py:43
  57.4 8.0 %collective-permute-start.10 = (f16[4,3,8,1024]{3,2,1,0:T(8,128)(2,1)S(1)}, f16[4,3,8,1024]{3,2,1,0:T(8,128)(2,1)S(1)}, u32[]{:S(2)}, u32[]{:S(2)}) collective-permute-start(f16[4,3,8,1024]{3,2,1,0:T(8,128)(2,1)S(1)} %pad_maximum_fusion.1), channel_id=1, source_target_pairs={{0,6},{1,25},{2,0},{3,27},{4,2},{5,29},{6,4},{7,31},{8,14},{9,1},{... | collective-permute-start | bytes 589832 | tf_op jit(solution)/shard_map/ppermute | solution.py:43
  60.3 7.7 %collective-permute-start.11 = (f16[4,3,8,1024]{3,2,1,0:T(8,128)(2,1)S(1)}, f16[4,3,8,1024]{3,2,1,0:T(8,128)(2,1)S(1)}, u32[]{:S(2)}, u32[]{:S(2)}) collective-permute-start(f16[4,3,8,1024]{3,2,1,0:T(8,128)(2,1)S(1)} %pad_maximum_fusion.2), channel_id=1, source_target_pairs={{0,4},{1,17},{2,6},{3,19},{4,0},{5,21},{6,2},{7,23},{8,12},{9,25},... | collective-permute-start | bytes 589832 | tf_op jit(solution)/shard_map/ppermute | solution.py:43
  68.2 5.9 %collective-permute-start.12 = (f16[3,8,1024]{2,1,0:T(8,128)(2,1)S(1)}, f16[3,8,1024]{2,1,0:T(8,128)(2,1)S(1)}, u32[]{:S(2)}, u32[]{:S(2)}) collective-permute-start(f16[3,8,1024]{2,1,0:T(8,128)(2,1)S(1)} %get-tuple-element.16), channel_id=1, source_target_pairs={{0,8},{1,3},{2,10},{3,5},{4,12},{5,7},{6,14},{7,1},{8,16},{9,11},{... | collective-permute-start | bytes 147464 | tf_op jit(solution)/shard_map/ppermute | solution.py:43
  68.3 5.8 %collective-permute-start.14 = (f16[3,8,1024]{2,1,0:T(8,128)(2,1)S(1)}, f16[3,8,1024]{2,1,0:T(8,128)(2,1)S(1)}, u32[]{:S(2)}, u32[]{:S(2)}) collective-permute-start(f16[3,8,1024]{2,1,0:T(8,128)(2,1)S(1)} %get-tuple-element.17), channel_id=1, source_target_pairs={{0,16},{1,5},{2,18},{3,7},{4,20},{5,1},{6,22},{7,3},{8,24},{9,13},... | collective-permute-start | bytes 147464 | tf_op jit(solution)/shard_map/ppermute | solution.py:43
  70.2 4.8 %collective-permute-start.13 = (f16[3,8,1024]{2,1,0:T(8,128)(2,1)S(1)}, f16[3,8,1024]{2,1,0:T(8,128)(2,1)S(1)}, u32[]{:S(2)}, u32[]{:S(2)}) collective-permute-start(f16[3,8,1024]{2,1,0:T(8,128)(2,1)S(1)} %get-tuple-element.18), channel_id=1, source_target_pairs={{0,24},{1,7},{2,26},{3,1},{4,28},{5,3},{6,30},{7,5},{8,0},{9,15},{... | collective-permute-start | bytes 147464 | tf_op jit(solution)/shard_map/ppermute | solution.py:43
  75.3 1.2 %collective-permute-start.15 = (f32[3,4,8]{2,1,0:T(4,128)S(1)}, f32[3,4,8]{2,1,0:T(4,128)S(1)}, u32[]{:S(2)}, u32[]{:S(2)}) collective-permute-start(f32[3,4,8]{2,1,0:T(4,128)S(1)} %dynamic-slice_bitcast_fusion), channel_id=1, source_target_pairs={{0,1},{1,0},{2,3},{3,2},{4,5},{5,4},{6,7},{7,6},{8,9},{9,8},{10,11... | collective-permute-start | bytes 1160 | tf_op jit(solution)/shard_map/ppermute | solution.py:47
  76.6 5.2 %collective-permute-start.18 = (f32[3,4,8]{2,1,0:T(4,128)S(1)}, f32[3,4,8]{2,1,0:T(4,128)S(1)}, u32[]{:S(2)}, u32[]{:S(2)}) collective-permute-start(f32[3,4,8]{2,1,0:T(4,128)S(1)} %bitcast_add_fusion), channel_id=1, source_target_pairs={{0,64},{32,96},{64,0},{96,32},{1,65},{33,97},{65,1},{97,33},{2,66}... | collective-permute-start | bytes 1160 | tf_op jit(solution)/shard_map/ppermute | solution.py:203
  79.7 3.6 %collective-permute-start.17 = (f32[3,4,8]{2,1,0:T(4,128)S(1)}, f32[3,4,8]{2,1,0:T(4,128)S(1)}, u32[]{:S(2)}, u32[]{:S(2)}) collective-permute-start(f32[3,4,8]{2,1,0:T(4,128)S(1)} %bitcast_add_fusion), channel_id=1, source_target_pairs={{0,96},{32,0},{64,32},{96,64},{1,97},{33,1},{65,33},{97,65},{2,98}... | collective-permute-start | bytes 1160 | tf_op jit(solution)/shard_map/ppermute | solution.py:203
  80.8 4.8 %collective-permute-start.16 = (f32[3,4,8]{2,1,0:T(4,128)S(1)}, f32[3,4,8]{2,1,0:T(4,128)S(1)}, u32[]{:S(2)}, u32[]{:S(2)}) collective-permute-start(f32[3,4,8]{2,1,0:T(4,128)S(1)} %bitcast_add_fusion), channel_id=1, source_target_pairs={{0,32},{32,64},{64,96},{96,0},{1,33},{33,65},{65,97},{97,1},{2,34}... | collective-permute-start | bytes 1160 | tf_op jit(solution)/shard_map/ppermute | solution.py:203
  85.7 0.8 copy-start

commit v3 on v2

--- a/solution.py
+++ b/solution.py
@@ -1,5 +1,3 @@
-import functools
-
 import jax
 import jax.numpy as jnp
 from jax import lax
@@ -51,24 +49,13 @@
     return lax.dot_general(a, b, (dims, ((), ())), preferred_element_type=F32)
 
 
-def net_kernel(
-    live_ref, rows_ref, mine_ref, other_ref, floor_ref, hot_ref, out_ref, sums_ref, held_ref, sems
-):
-    copies = [
-        [
-            pltpu.make_async_copy(source.at[step], held_ref.at[step, half], sems.at[step, half])
-            for half, source in enumerate((mine_ref, other_ref))
-        ]
-        for step in range(STEPS)
-    ]
-    for pair in copies:
-        for copy in pair:
-            copy.start()
+def net_rows(live_ref, rows_ref, floor_ref, hot_ref, held_ref, out_ref, sums_ref, copies=None):
     trade = lax.broadcasted_iota(jnp.int32, (TB, CHUNK), 0)
     for step in range(STEPS):
         rows = rows_ref[:, step].reshape(CHUNK, BASIS)
         for half in range(2):
-            copies[step][half].wait()
+            if copies:
+                copies[step][half].wait()
             for first in range(0, BPD, GROUP):
                 trades = slice(first * TB, (first + GROUP) * TB)
                 values = dot(held_ref[step, half, trades, :], rows, ((1,), (1,)))
@@ -88,29 +75,62 @@
         out_ref[step] = dot(hot, high, ((1,), (0,))) + dot(hot, low, ((1,), (0,)))
 
 
+def net_first_kernel(
+    live_ref, rows_ref, mine_ref, other_ref, floor_ref, hot_ref, out_ref, held_ref, sums_ref, sems
+):
+    copies = [
+        [
+            pltpu.make_async_copy(source.at[step], held_ref.at[step, half], sems.at[step, half])
+            for half, source in enumerate((mine_ref, other_ref))
+        ]
+        for step in range(STEPS)
+    ]
+    for pair in copies:
+        for copy in pair:
+            copy.start()
+    net_rows(live_ref, rows_ref, floor_ref, hot_ref, held_ref, out_ref, sums_ref, copies)
+
+
+def net_next_kernel(live_ref, rows_ref, held_ref, floor_ref, hot_ref, out_ref, sums_ref):
+    net_rows(live_ref, rows_ref, floor_ref, hot_ref, held_ref, out_ref, sums_ref)
+
+
 VMEM = pl.BlockSpec(memory_space=pltpu.VMEM)
 SMEM = pl.BlockSpec(memory_space=pltpu.SMEM)
 ANY = pl.BlockSpec(memory_space=pl.ANY)
 
 
-def net(rows, live, mine, other, floors, hot):
+TERMS = (STEPS, SIDE * SIDE * OWN, CHUNK)
+HELD = (STEPS, 2, BPD * TB, BASIS)
+
+
+def net_first(rows, live, mine, other, floors, hot):
     mine = pltpu.with_memory_space_constraint(mine, pltpu.HBM)
     return pl.pallas_call(
-        net_kernel,
+        net_first_kernel,
         in_specs=[SMEM, VMEM, ANY, ANY, VMEM, VMEM],
-        out_specs=VMEM,
-        out_shape=jax.ShapeDtypeStruct((STEPS, SIDE * SIDE * OWN, CHUNK), F32),
+        out_specs=(VMEM, VMEM),
+        out_shape=(jax.ShapeDtypeStruct(TERMS, F32), pltpu.VMEM(HELD, BF16)),
         scratch_shapes=[
             pltpu.VMEM((2 * BPD * 8, CHUNK), F32),
-            pltpu.VMEM((STEPS, 2, BPD * TB, BASIS), BF16),
             pltpu.SemaphoreType.DMA((STEPS, 2)),
         ],
         compiler_params=pltpu.CompilerParams(vmem_limit_bytes=20 << 20),
-        cost_estimate=pl.CostEstimate(
-            flops=4 * STEPS * CHUNK * BPD * TB * BASIS, bytes_accessed=1 << 20, transcendentals=0
-        ),
-        name="net",
+        name="net_first",
     )(live, rows, mine, other, floors, hot)
+
+
+def net_next(rows, live, held, floors, hot):
+    held = pltpu.with_memory_space_constraint(held, pltpu.VMEM)
+    return pl.pallas_call(
+        net_next_kernel,
+        in_specs=[SMEM, VMEM, VMEM, VMEM, VMEM],
+        out_specs=VMEM,
+        out_shape=jax.ShapeDtypeStruct(TERMS, F32),
+        scratch_shapes=[pltpu.VMEM((2 * BPD * 8, CHUNK), F32)],
+        compiler_params=pltpu.CompilerParams(vmem_limit_bytes=12 << 20),
+        name="net_next",
+    )(live, rows, held, floors, hot)
 
 
 def line_kernel(first_ref, *refs):
@@ -161,14 +181,15 @@
     hot = (ids[:, None] == owners[None, :]).astype(BF16)
     both_floors = jnp.swapaxes(jnp.concatenate([exercise, other_floors], axis=1), 1, 2)
 
-    run = functools.partial(
-        net, live=blocks[1], mine=weights, other=other_weights, floors=both_floors, hot=hot
-    )
     arrived = {shift: shift_by(line, shift, 1) for shift in (1, 3, 2)}
     terms, sent = {}, {}
     rows = line
     for shift, following in ((0, 1), (1, 3), (3, 2), (2, None)):
-        terms[shift] = run(rows).reshape(STEPS, SIDE, SIDE, OWN, CHUNK)
+        if shift == 0:
+            term, held = net_first(rows, blocks[1], weights, other_weights, both_floors, hot)
+        else:
+            term = net_next(rows, blocks[1], held, both_floors, hot)
+        terms[shift] = term.reshape(STEPS, SIDE, SIDE, OWN, CHUNK)
         sent[shift] = terms[shift][:, 1:].astype(jnp.float16)
         if following:
             rows, sent[shift] = lax.optimization_barrier((arrived[following], sent[shift]))

time: 86.8 us -> 73.8 us (0.85)
  Pallas kernels: 22.9 us -> 15.3 us
  waiting for transfers between devices: 22.2 us -> 16.2 us
    pallas_call x4, Pallas kernels: 22.9 us -> 15.3 us  [the longest x3 9.59 us: net_next(): pl.pallas_call(net_next_kernel, in_specs=[SMEM, VMEM, VMEM, VMEM, VMEM],...]
    ppermute x12, waiting for transfers between devices: 17.2 us -> 11.9 us  [shift_by(): return lax.ppermute(value, 'set', ring_pairs(shift, stage))]
  transfers between devices with their start and end apart: 19 -> 19, of which waited for: 9 -> 8; matrix products, arithmetic and copies ran while one was open for 17% -> 20% of each run, Pallas kernels for 20% -> 17%
where the time goes in v3:
time: 73.8 us; the launch traced here: 73.5 us
  starting transfers between devices  24.5 us (33%)
  waiting for transfers between devices  16.2 us (22%)
  Pallas kernels  15.3 us (21%)
  matrix products  8.67 us (12%)
  other arithmetic  4.19 us (6%)
  local copies, waits for them, and re-layouts  3.43 us (5%)
  between operations  1.15 us (2%)
    ppermute x12, starting transfers between devices, shift_by(): return lax.ppermute(value, 'set', ring_pairs(shift, stage))  18.6 us
    ppermute x12, waiting for transfers between devices, shift_by(): return lax.ppermute(value, 'set', ring_pairs(shift, stage))  11.9 us
    pallas_call x3, Pallas kernels, net_next(): pl.pallas_call(net_next_kernel, in_specs=[SMEM, VMEM, VMEM, VMEM, VMEM],...  9.59 us
    dot_general x1, matrix products, body(): jnp.dot(scenarios.reshape(STEPS * ROWS, -1), projection, preferred_elemen...  8.45 us
    pallas_call x1, Pallas kernels, net_first(): pl.pallas_call(net_first_kernel, in_specs=[SMEM, VMEM, ANY, ANY, VMEM, VM...  5.73 us
    ppermute x3, starting transfers between devices, body(): lax.ppermute(sums, 'rep', [(i, (i + shift) % SIDE) for i in range(SIDE)])  5.23 us
    ppermute x3, waiting for transfers between devices, body(): lax.ppermute(sums, 'rep', [(i, (i + shift) % SIDE) for i in range(SIDE)])  3.14 us
    unnamed x19, local copies, waits for them, and re-layouts  1.6 us
  transfers between devices with their start and end apart: 19, of which 8 were waited for; matrix products, arithmetic and copies ran while one was open for 20% of the time, Pallas kernels for 17%

profile of v3, /device:TPU:0, one launch (start us, length us, event | category | flops | bytes accessed | tf_op | source)
XLA Modules:
  0.0 73.5 jit_solution(15026780691882033221)
XLA Ops:
  0.7 8.5 %fusion = bf16[192,256]{1,0:T(8,128)(2,1)S(1)} fusion(bf16[192,20000]{1,0:T(8,128)(2,1)} %bitcast.260, bf16[20000,256]{1,0:T(8,128)(2,1)} %param.7), kind=kOutput, calls=%fused_computation.1 | convolution fusion | flops 1966129152 | bytes 18018304 | tf_op jit(solution)/shard_map/dot_general | solution.py:158
  9.2 2.9 %collective-permute-start.1 = (bf16[3,64,256]{2,1,0:T(8,128)(2,1)S(1)}, bf16[3,64,256]{2,1,0:T(8,128)(2,1)S(1)}, u32[]{:S(2)}, u32[]{:S(2)}) collective-permute-start(bf16[3,64,256]{2,1,0:T(8,128)(2,1)S(1)} %bitcast.254), channel_id=1, source_target_pairs={{0,6},{1,25},{2,0},{3,27},{4,2},{5,29},{6,4},{7,31},{8,14},{9,1},{... | collective-permute-start | bytes 294920 | tf_op jit(solution)/shard_map/ppermute | solution.py:41
  12.1 0.8 %collective-permute-start.2 = (bf16[3,64,256]{2,1,0:T(8,128)(2,1)S(1)}, bf16[3,64,256]{2,1,0:T(8,128)(2,1)S(1)}, u32[]{:S(2)}, u32[]{:S(2)}) collective-permute-start(bf16[3,64,256]{2,1,0:T(8,128)(2,1)S(1)} %bitcast.255), channel_id=1, source_target_pairs={{0,4},{1,17},{2,6},{3,19},{4,0},{5,21},{6,2},{7,23},{8,12},{9,25},... | collective-permute-start | bytes 294920 | tf_op jit(solution)/shard_map/ppermute | solution.py:41
  12.9 0.9 %collective-permute-start.3 = (bf16[3,64,256]{2,1,0:T(8,128)(2,1)S(1)}, bf16[3,64,256]{2,1,0:T(8,128)(2,1)S(1)}, u32[]{:S(2)}, u32[]{:S(2)}) collective-permute-start(bf16[3,64,256]{2,1,0:T(8,128)(2,1)S(1)} %bitcast.256), channel_id=1, source_target_pairs={{0,2},{1,9},{2,4},{3,11},{4,6},{5,13},{6,0},{7,15},{8,10},{9,17},{... | collective-permute-start | bytes 294920 | tf_op jit(solution)/shard_map/ppermute | solution.py:41
  13.8 0.6 pad_add_fusion
  15.2 1.5 %copy.41 = f32[3,32,64]{1,2,0:T(8,128)} copy(f32[3,32,64]{2,1,0:T(8,128)} %param.9) | data formatting | bytes 49152 | tf_op args[3]
  16.7 0.7 pad_add_fusion.1
  17.5 0.7 broadcast_in_dim.2
  18.2 0.8 %eq.43 = s32[512]{0:T(512)S(1)} reshape(s32[64,8]{1,0:T(8,128)} %broadcast_in_dim.2) | data formatting | bytes 4096 | tf_op jit(solution)/shard_map/eq | solution.py:181
  19.4 2.0 %collective-permute-start.6 = (bf16[4,3,64,256]{3,2,1,0:T(8,128)(2,1)S(1)}, bf16[4,3,64,256]{3,2,1,0:T(8,128)(2,1)S(1)}, u32[]{:S(2)}, u32[]{:S(2)}) collective-permute-start(bf16[4,3,64,256]{3,2,1,0:T(8,128)(2,1)S(1)} %line.1.rows_ref), channel_id=1, source_target_pairs={{0,8},{1,3},{2,10},{3,5},{4,12},{5,7},{6,14},{7,1},{8,16},{9,11},{... | collective-permute-start | bytes 1179656 | tf_op jit(solution)/shard_map/ppermute | solution.py:41
  21.5 1.0 %maximum_bitcast_fusion.floor_ref = f32[3,64,64]{2,1,0:T(8,128)S(1)} fusion(f32[3,32,64]{1,2,0:T(8,128)} %collective-permute-done.5, f32[3,32,64]{1,2,0:T(8,128)} %copy.41), kind=kLoop, calls=%fused_computation.23 | loop fusion | flops 12288 | bytes 98304 | tf_op jit(solution)/shard_map/transpose | solution.py:182
  22.5 2.2 %collective-permute-start.8 = (bf16[4,3,64,256]{3,2,1,0:T(8,128)(2,1)S(1)}, bf16[4,3,64,256]{3,2,1,0:T(8,128)(2,1)S(1)}, u32[]{:S(2)}, u32[]{:S(2)}) collective-permute-start(bf16[4,3,64,256]{3,2,1,0:T(8,128)(2,1)S(1)} %line.1.rows_ref), channel_id=1, source_target_pairs={{0,24},{1,7},{2,26},{3,1},{4,28},{5,3},{6,30},{7,5},{8,0},{9,15},{... | collective-permute-start | bytes 1179656 | tf_op jit(solution)/shard_map/ppermute | solution.py:41
  24.7 1.9 %collective-permute-start.7 = (bf16[4,3,64,256]{3,2,1,0:T(8,128)(2,1)S(1)}, bf16[4,3,64,256]{3,2,1,0:T(8,128)(2,1)S(1)}, u32[]{:S(2)}, u32[]{:S(2)}) collective-permute-start(bf16[4,3,64,256]{3,2,1,0:T(8,128)(2,1)S(1)} %line.1.rows_ref), channel_id=1, source_target_pairs={{0,16},{1,5},{2,18},{3,7},{4,20},{5,1},{6,22},{7,3},{8,24},{9,13},... | collective-permute-start | bytes 1179656 | tf_op jit(solution)/shard_map/ppermute | solution.py:41
  26.5 5.7 %net_first.1 = (f32[3,128,256]{2,1,0:T(8,128)S(1)}, bf16[3,2,2048,256]{3,2,1,0:T(8,128)(2,1)S(1)}) custom-call(s32[64]{0:T(128)S(1)} %get-tuple-element.88.live_ref, bf16[4,3,64,256]{3,2,1,0:T(8,128)(2,1)S(1)} %line.1.rows_ref, bf16[3,2048,256]{2,1,0:T(8,128)(2,1)} %bitcast.262, bf16[3,2048,256]{2,1,0:T(8,128)(2,1)S(1)} %collective-permute-done.4.other_ref, ...), custom_call_target="tpu_custom_call" | custom-call | tf_op jit(solution)/shard_map/net_first/pallas_call | solution.py:109
  32.3 3.2 %net_next.3 = f32[3,128,256]{2,1,0:T(8,128)S(1)} custom-call(s32[64]{0:T(128)S(1)} %get-tuple-element.88.live_ref, bf16[4,3,64,256]{3,2,1,0:T(8,128)(2,1)S(1)} %collective-permute-done.6.rows_ref, bf16[3,2,2048,256]{3,2,1,0:T(8,128)(2,1)S(1)} %get-tuple-element.12.held_ref, f32[3,64,64]{2,1,0:T(8,128)S(1)} %maximum_bitcast_fusion.floor_ref, ...), custom_call_target="tpu_custom_call" | custom-call | tf_op jit(solution)/shard_map/net_next/pallas_call | solution.py:125
  35.6 3.2 %net_next.4 = f32[3,128,256]{2,1,0:T(8,128)S(1)} custom-call(s32[64]{0:T(128)S(1)} %get-tuple-element.88.live_ref, bf16[4,3,64,256]{3,2,1,0:T(8,128)(2,1)S(1)} %collective-permute-done.8.rows_ref, bf16[3,2,2048,256]{3,2,1,0:T(8,128)(2,1)S(1)} %get-tuple-element.12.held_ref, f32[3,64,64]{2,1,0:T(8,128)S(1)} %maximum_bitcast_fusion.floor_ref, ...), custom_call_target="tpu_custom_call" | custom-call | tf_op jit(solution)/shard_map/net_next/pallas_call | solution.py:125
  38.8 3.2 %net_next.5 = f32[3,128,256]{2,1,0:T(8,128)S(1)} custom-call(s32[64]{0:T(128)S(1)} %get-tuple-element.88.live_ref, bf16[4,3,64,256]{3,2,1,0:T(8,128)(2,1)S(1)} %collective-permute-done.7.rows_ref, bf16[3,2,2048,256]{3,2,1,0:T(8,128)(2,1)S(1)} %get-tuple-element.12.held_ref, f32[3,64,64]{2,1,0:T(8,128)S(1)} %maximum_bitcast_fusion.floor_ref, ...), custom_call_target="tpu_custom_call" | custom-call | tf_op jit(solution)/shard_map/net_next/pallas_call | solution.py:125
  42.5 1.8 %collective-permute-start.9 = (f16[4,3,8,1024]{3,2,1,0:T(8,128)(2,1)S(1)}, f16[4,3,8,1024]{3,2,1,0:T(8,128)(2,1)S(1)}, u32[]{:S(2)}, u32[]{:S(2)}) collective-permute-start(f16[4,3,8,1024]{3,2,1,0:T(8,128)(2,1)S(1)} %pad_maximum_fusion), channel_id=1, source_target_pairs={{0,2},{1,9},{2,4},{3,11},{4,6},{5,13},{6,0},{7,15},{8,10},{9,17},{... | collective-permute-start | bytes 589832 | tf_op jit(solution)/shard_map/ppermute | solution.py:41
  44.5 1.8 %collective-permute-start.10 = (f16[4,3,8,1024]{3,2,1,0:T(8,128)(2,1)S(1)}, f16[4,3,8,1024]{3,2,1,0:T(8,128)(2,1)S(1)}, u32[]{:S(2)}, u32[]{:S(2)}) collective-permute-start(f16[4,3,8,1024]{3,2,1,0:T(8,128)(2,1)S(1)} %pad_maximum_fusion.1), channel_id=1, source_target_pairs={{0,6},{1,25},{2,0},{3,27},{4,2},{5,29},{6,4},{7,31},{8,14},{9,1},{... | collective-permute-start | bytes 589832 | tf_op jit(solution)/shard_map/ppermute | solution.py:41
  47.1 2.5 %collective-permute-done.9 = f16[4,3,8,1024]{3,2,1,0:T(8,128)(2,1)S(1)} collective-permute-done((f16[4,3,8,1024]{3,2,1,0:T(8,128)(2,1)S(1)}, f16[4,3,8,1024]{3,2,1,0:T(8,128)(2,1)S(1)}, u32[]{:S(2)}, u32[]{:S(2)}) %collective-permute-start.9) | collective-permute-done | bytes 196640 | tf_op jit(solution)/shard_map/ppermute | solution.py:41
  49.6 0.6 collective-permute-done.10
  50.2 3.5 %collective-permute-done.11 = f16[4,3,8,1024]{3,2,1,0:T(8,128)(2,1)S(1)} collective-permute-done((f16[4,3,8,1024]{3,2,1,0:T(8,128)(2,1)S(1)}, f16[4,3,8,1024]{3,2,1,0:T(8,128)(2,1)S(1)}, u32[]{:S(2)}, u32[]{:S(2)}) %collective-permute-start.11) | collective-permute-done | bytes 196640 | tf_op jit(solution)/shard_map/ppermute | solution.py:41
  53.8 1.1 %collective-permute-start.12 = (f16[3,8,1024]{2,1,0:T(8,128)(2,1)S(1)}, f16[3,8,1024]{2,1,0:T(8,128)(2,1)S(1)}, u32[]{:S(2)}, u32[]{:S(2)}) collective-permute-start(f16[3,8,1024]{2,1,0:T(8,128)(2,1)S(1)} %get-tuple-element.20), channel_id=1, source_target_pairs={{0,8},{1,3},{2,10},{3,5},{4,12},{5,7},{6,14},{7,1},{8,16},{9,11},{... | collective-permute-start | bytes 147464 | tf_op jit(solution)/shard_map/ppermute | solution.py:41
  54.9 2.2 %collective-permute-start.13 = (f16[3,8,1024]{2,1,0:T(8,128)(2,1)S(1)}, f16[3,8,1024]{2,1,0:T(8,128)(2,1)S(1)}, u32[]{:S(2)}, u32[]{:S(2)}) collective-permute-start(f16[3,8,1024]{2,1,0:T(8,128)(2,1)S(1)} %get-tuple-element.22), channel_id=1, source_target_pairs={{0,24},{1,7},{2,26},{3,1},{4,28},{5,3},{6,30},{7,5},{8,0},{9,15},{... | collective-permute-start | bytes 147464 | tf_op jit(solution)/shard_map/ppermute | solution.py:41
  57.7 1.5 %collective-permute-done.12 = f16[3,8,1024]{2,1,0:T(8,128)(2,1)S(1)} collective-permute-done((f16[3,8,1024]{2,1,0:T(8,128)(2,1)S(1)}, f16[3,8,1024]{2,1,0:T(8,128)(2,1)S(1)}, u32[]{:S(2)}, u32[]{:S(2)}) %collective-permute-start.12) | collective-permute-done | bytes 49184 | tf_op jit(solution)/shard_map/ppermute | solution.py:41
  59.2 3.5 %collective-permute-done.14 = f16[3,8,1024]{2,1,0:T(8,128)(2,1)S(1)} collective-permute-done((f16[3,8,1024]{2,1,0:T(8,128)(2,1)S(1)}, f16[3,8,1024]{2,1,0:T(8,128)(2,1)S(1)}, u32[]{:S(2)}, u32[]{:S(2)}) %collective-permute-start.14) | collective-permute-done | bytes 49184 | tf_op jit(solution)/shard_map/ppermute | solution.py:41
  63.1 1.1 %collective-permute-done.15 = f32[3,4,8]{2,1,0:T(4,128)S(1)} collective-permute-done((f32[3,4,8]{2,1,0:T(4,128)S(1)}, f32[3,4,8]{2,1,0:T(4,128)S(1)}, u32[]{:S(2)}, u32[]{:S(2)}) %collective-permute-start.15) | collective-permute-done | bytes 416 | tf_op jit(solution)/shard_map/ppermute | solution.py:45
  64.3 1.6 %collective-permute-start.16 = (f32[3,4,8]{2,1,0:T(4,128)S(1)}, f32[3,4,8]{2,1,0:T(4,128)S(1)}, u32[]{:S(2)}, u32[]{:S(2)}) collective-permute-start(f32[3,4,8]{2,1,0:T(4,128)S(1)} %bitcast_add_fusion), channel_id=1, source_target_pairs={{0,32},{32,64},{64,96},{96,0},{1,33},{33,65},{65,97},{97,1},{2,34}... | collective-permute-start | bytes 1160 | tf_op jit(solution)/shard_map/ppermute | solution.py:224
  65.9 1.7 %collective-permute-start.17 = (f32[3,4,8]{2,1,0:T(4,128)S(1)}, f32[3,4,8]{2,1,0:T(4,128)S(1)}, u32[]{:S(2)}, u32[]{:S(2)}) collective-permute-start(f32[3,4,8]{2,1,0:T(4,128)S(1)} %bitcast_add_fusion), channel_id=1, source_target_pairs={{0,96},{32,0},{64,32},{96,64},{1,97},{33,1},{65,33},{97,65},{2,98}... | collective-permute-start | bytes 1160 | tf_op jit(solution)/shard_map/ppermute | solution.py:224
  67.5 2.0 %collective-permute-start.18 = (f32[3,4,8]{2,1,0:T(4,128)S(1)}, f32[3,4,8]{2,1,0:T(4,128)S(1)}, u32[]{:S(2)}, u32[]{:S(2)}) collective-permute-start(f32[3,4,8]{2,1,0:T(4,128)S(1)} %bitcast_add_fusion), channel_id=1, source_target_pairs={{0,64},{32,96},{64,0},{96,32},{1,65},{33,97},{65,1},{97,33},{2,66}... | collective-permute-start | bytes 1160 | tf_op jit(solution)/shard_map/ppermute | solution.py:224
  69.5 3.1 %collective-permute-done.18 = f32[3,4,8]{2,1,0:T(4,128)S(1)} collective-permute-done((f32[3,4,8]{2,1,0:T(4,128)S(1)}, f32[3,4,8]{2,1,0:T(4,128)S(1)}, u32[]{:S(2)}, u32[]{:S(2)}) %collective-permute-start.18) | collective-permute-done | bytes 416 | tf_op jit(solution)/shard_map/ppermute | solution.py:224
  72.9 0.6 multiply_sqrt_fusion
  (86 shorter events, 3.9 us)
Async XLA Ops:
  0.6 25.9 %collective-permute-start.4 = (bf16[3,2048,256]{2,1,0:T(8,128)(2,1)}, bf16[3,2048,256]{2,1,0:T(8,128)(2,1)S(1)}, u32[]{:S(2)}, u32[]{:S(2)}) collective-permute-start(bf16[3,2048,256]{2,1,0:T(8,128)(2,1)} %bitcast.261), channel_id=1, source_target_pairs={{0,1},{1,0},{2,3},{3,2},{4,5},{5,4},{6,7},{7,6},{8,9},{9,8},{10,11... | collective-permute-start | bytes 9437192 | tf_op jit(solution)/shard_map/ppermute | solution.py:45
  0.7 13.1 %copy-start.1 = (s32[32]{0:T(128)S(1)}, s32[32]{0:T(128)}, u32[]{:S(2)}) copy-start(s32[32]{0:T(128)} %param.11) | copy-start | bytes 388
  0.7 13.1 %copy-start.2 = (s32[32]{0:T(128)S(1)}, s32[32]{0:T(128)}, u32[]{:S(2)}) copy-start(s32[32]{0:T(128)} %param.10) | copy-start | bytes 388
  9.2 9.8 %collective-permute-start.1 = (bf16[3,64,256]{2,1,0:T(8,128)(2,1)S(1)}, bf16[3,64,256]{2,1,0:T(8,128)(2,1)S(1)}, u32[]{:S(2)}, u32[]{:S(2)}) collective-permute-start(bf16[3,64,256]{2,1,0:T(8,128)(2,1)S(1)} %bitcast.254), channel_id=1, source_target_pairs={{0,6},{1,25},{2,0},{3,27},{4,2},{5,29},{6,4},{7,31},{8,14},{9,1},{... | collective-permute-start | bytes 294920 | tf_op jit(solution)/shard_map/ppermute | solution.py:41
  12.1 6.9 %collective-permute-start.2 = (bf16[3,64,256]{2,1,0:T(8,128)(2,1)S(1)}, bf16[3,64,256]{2,1,0:T(8,128)(2,1)S(1)}, u32[]{:S(2)}, u32[]{:S(2)}) collective-permute-start(bf16[3,64,256]{2,1,0:T(8,128)(2,1)S(1)} %bitcast.255), channel_id=1, source_target_pairs={{0,4},{1,17},{2,6},{3,19},{4,0},{5,21},{6,2},{7,23},{8,12},{9,25},... | collective-permute-start | bytes 294920 | tf_op jit(solution)/shard_map/ppermute | solution.py:41
  12.9 6.4 %collective-permute-start.3 = (bf16[3,64,256]{2,1,0:T(8,128)(2,1)S(1)}, bf16[3,64,256]{2,1,0:T(8,128)(2,1)S(1)}, u32[]{:S(2)}, u32[]{:S(2)}) collective-permute-start(bf16[3,64,256]{2,1,0:T(8,128)(2,1)S(1)} %bitcast.256), channel_id=1, source_target_pairs={{0,2},{1,9},{2,4},{3,11},{4,6},{5,13},{6,0},{7,15},{8,10},{9,17},{... | collective-permute-start | bytes 294920 | tf_op jit(solution)/shard_map/ppermute | solution.py:41
  14.4 2.3 %collective-permute-start = (s32[2,32]{1,0:T(2,128)}, s32[2,32]{1,0:T(2,128)}, u32[]{:S(2)}, u32[]{:S(2)}) collective-permute-start(s32[2,32]{1,0:T(2,128)} %pad_add_fusion), channel_id=1, source_target_pairs={{0,1},{1,0},{2,3},{3,2},{4,5},{5,4},{6,7},{7,6},{8,9},{9,8},{10,11... | collective-permute-start | bytes 776 | tf_op jit(solution)/shard_map/ppermute | solution.py:45
  16.7 4.7 %collective-permute-start.5 = (f32[3,32,64]{1,2,0:T(8,128)}, f32[3,32,64]{1,2,0:T(8,128)}, u32[]{:S(2)}, u32[]{:S(2)}) collective-permute-start(f32[3,32,64]{1,2,0:T(8,128)} %copy.41), channel_id=1, source_target_pairs={{0,1},{1,0},{2,3},{3,2},{4,5},{5,4},{6,7},{7,6},{8,9},{9,8},{10,11... | collective-permute-start | bytes 73736 | tf_op jit(solution)/shard_map/ppermute | solution.py:45
  19.4 13.0 %collective-permute-start.6 = (bf16[4,3,64,256]{3,2,1,0:T(8,128)(2,1)S(1)}, bf16[4,3,64,256]{3,2,1,0:T(8,128)(2,1)S(1)}, u32[]{:S(2)}, u32[]{:S(2)}) collective-permute-start(bf16[4,3,64,256]{3,2,1,0:T(8,128)(2,1)S(1)} %line.1.rows_ref), channel_id=1, source_target_pairs={{0,8},{1,3},{2,10},{3,5},{4,12},{5,7},{6,14},{7,1},{8,16},{9,11},{... | collective-permute-start | bytes 1179656 | tf_op jit(solution)/shard_map/ppermute | solution.py:41
  22.5 13.0 %collective-permute-start.8 = (bf16[4,3,64,256]{3,2,1,0:T(8,128)(2,1)S(1)}, bf16[4,3,64,256]{3,2,1,0:T(8,128)(2,1)S(1)}, u32[]{:S(2)}, u32[]{:S(2)}) collective-permute-start(bf16[4,3,64,256]{3,2,1,0:T(8,128)(2,1)S(1)} %line.1.rows_ref), channel_id=1, source_target_pairs={{0,24},{1,7},{2,26},{3,1},{4,28},{5,3},{6,30},{7,5},{8,0},{9,15},{... | collective-permute-start | bytes 1179656 | tf_op jit(solution)/shard_map/ppermute | solution.py:41
  24.7 14.1 %collective-permute-start.7 = (bf16[4,3,64,256]{3,2,1,0:T(8,128)(2,1)S(1)}, bf16[4,3,64,256]{3,2,1,0:T(8,128)(2,1)S(1)}, u32[]{:S(2)}, u32[]{:S(2)}) collective-permute-start(bf16[4,3,64,256]{3,2,1,0:T(8,128)(2,1)S(1)} %line.1.rows_ref), channel_id=1, source_target_pairs={{0,16},{1,5},{2,18},{3,7},{4,20},{5,1},{6,22},{7,3},{8,24},{9,13},... | collective-permute-start | bytes 1179656 | tf_op jit(solution)/shard_map/ppermute | solution.py:41
  42.5 7.2 %collective-permute-start.9 = (f16[4,3,8,1024]{3,2,1,0:T(8,128)(2,1)S(1)}, f16[4,3,8,1024]{3,2,1,0:T(8,128)(2,1)S(1)}, u32[]{:S(2)}, u32[]{:S(2)}) collective-permute-start(f16[4,3,8,1024]{3,2,1,0:T(8,128)(2,1)S(1)} %pad_maximum_fusion), channel_id=1, source_target_pairs={{0,2},{1,9},{2,4},{3,11},{4,6},{5,13},{6,0},{7,15},{8,10},{9,17},{... | collective-permute-start | bytes 589832 | tf_op jit(solution)/shard_map/ppermute | solution.py:41
  44.5 5.7 %collective-permute-start.10 = (f16[4,3,8,1024]{3,2,1,0:T(8,128)(2,1)S(1)}, f16[4,3,8,1024]{3,2,1,0:T(8,128)(2,1)S(1)}, u32[]{:S(2)}, u32[]{:S(2)}) collective-permute-start(f16[4,3,8,1024]{3,2,1,0:T(8,128)(2,1)S(1)} %pad_maximum_fusion.1), channel_id=1, source_target_pairs={{0,6},{1,25},{2,0},{3,27},{4,2},{5,29},{6,4},{7,31},{8,14},{9,1},{... | collective-permute-start | bytes 589832 | tf_op jit(solution)/shard_map/ppermute | solution.py:41
  46.4 7.3 %collective-permute-start.11 = (f16[4,3,8,1024]{3,2,1,0:T(8,128)(2,1)S(1)}, f16[4,3,8,1024]{3,2,1,0:T(8,128)(2,1)S(1)}, u32[]{:S(2)}, u32[]{:S(2)}) collective-permute-start(f16[4,3,8,1024]{3,2,1,0:T(8,128)(2,1)S(1)} %pad_maximum_fusion.2), channel_id=1, source_target_pairs={{0,4},{1,17},{2,6},{3,19},{4,0},{5,21},{6,2},{7,23},{8,12},{9,25},... | collective-permute-start | bytes 589832 | tf_op jit(solution)/shard_map/ppermute | solution.py:41
  53.8 5.4 %collective-permute-start.12 = (f16[3,8,1024]{2,1,0:T(8,128)(2,1)S(1)}, f16[3,8,1024]{2,1,0:T(8,128)(2,1)S(1)}, u32[]{:S(2)}, u32[]{:S(2)}) collective-permute-start(f16[3,8,1024]{2,1,0:T(8,128)(2,1)S(1)} %get-tuple-element.20), channel_id=1, source_target_pairs={{0,8},{1,3},{2,10},{3,5},{4,12},{5,7},{6,14},{7,1},{8,16},{9,11},{... | collective-permute-start | bytes 147464 | tf_op jit(solution)/shard_map/ppermute | solution.py:41
  54.9 4.3 %collective-permute-start.13 = (f16[3,8,1024]{2,1,0:T(8,128)(2,1)S(1)}, f16[3,8,1024]{2,1,0:T(8,128)(2,1)S(1)}, u32[]{:S(2)}, u32[]{:S(2)}) collective-permute-start(f16[3,8,1024]{2,1,0:T(8,128)(2,1)S(1)} %get-tuple-element.22), channel_id=1, source_target_pairs={{0,24},{1,7},{2,26},{3,1},{4,28},{5,3},{6,30},{7,5},{8,0},{9,15},{... | collective-permute-start | bytes 147464 | tf_op jit(solution)/shard_map/ppermute | solution.py:41
  57.1 5.6 %collective-permute-start.14 = (f16[3,8,1024]{2,1,0:T(8,128)(2,1)S(1)}, f16[3,8,1024]{2,1,0:T(8,128)(2,1)S(1)}, u32[]{:S(2)}, u32[]{:S(2)}) collective-permute-start(f16[3,8,1024]{2,1,0:T(8,128)(2,1)S(1)} %get-tuple-element.21), channel_id=1, source_target_pairs={{0,16},{1,5},{2,18},{3,7},{4,20},{5,1},{6,22},{7,3},{8,24},{9,13},... | collective-permute-start | bytes 147464 | tf_op jit(solution)/shard_map/ppermute | solution.py:41
  63.0 1.2 %collective-permute-start.15 = (f32[3,4,8]{2,1,0:T(4,128)S(1)}, f32[3,4,8]{2,1,0:T(4,128)S(1)}, u32[]{:S(2)}, u32[]{:S(2)}) collective-permute-start(f32[3,4,8]{2,1,0:T(4,128)S(1)} %dynamic-slice_bitcast_fusion), channel_id=1, source_target_pairs={{0,1},{1,0},{2,3},{3,2},{4,5},{5,4},{6,7},{7,6},{8,9},{9,8},{10,11... | collective-permute-start | bytes 1160 | tf_op jit(solution)/shard_map/ppermute | solution.py:45
  64.3 5.2 %collective-permute-start.16 = (f32[3,4,8]{2,1,0:T(4,128)S(1)}, f32[3,4,8]{2,1,0:T(4,128)S(1)}, u32[]{:S(2)}, u32[]{:S(2)}) collective-permute-start(f32[3,4,8]{2,1,0:T(4,128)S(1)} %bitcast_add_fusion), channel_id=1, source_target_pairs={{0,32},{32,64},{64,96},{96,0},{1,33},{33,65},{65,97},{97,1},{2,34}... | collective-permute-start | bytes 1160 | tf_op jit(solution)/shard_map/ppermute | solution.py:224
  65.9 3.7 %collective-permute-start.17 = (f32[3,4,8]{2,1,0:T(4,128)S(1)}, f32[3,4,8]{2,1,0:T(4,128)S(1)}, u32[]{:S(2)}, u32[]{:S(2)}) collective-permute-start(f32[3,4,8]{2,1,0:T(4,128)S(1)} %bitcast_add_fusion), channel_id=1, source_target_pairs={{0,96},{32,0},{64,32},{96,64},{1,97},{33,1},{65,33},{97,65},{2,98}... | collective-permute-start | bytes 1160 | tf_op jit(solution)/shard_map/ppermute | solution.py:224
  67.5 5.1 %collective-permute-start.18 = (f32[3,4,8]{2,1,0:T(4,128)S(1)}, f32[3,4,8]{2,1,0:T(4,128)S(1)}, u32[]{:S(2)}, u32[]{:S(2)}) collective-permute-start(f32[3,4,8]{2,1,0:T(4,128)S(1)} %bitcast_add_fusion), channel_id=1, source_target_pairs={{0,64},{32,96},{64,0},{96,32},{1,65},{33,97},{65,1},{97,33},{2,66}... | collective-permute-start | bytes 1160 | tf_op jit(solution)/shard_map/ppermute | solution.py:224
  72.8 0.8 %copy-start = (f32[3,4]{1,0:T(4,128)}, f32[3,4]{1,0:T(4,128)S(1)}, u32[]{:S(2)}) copy-start(f32[3,4]{1,0:T(4,128)S(1)} %broadcast_multiply_fusion) | copy-start | bytes 148

commit v4 on v3

--- a/solution.py
+++ b/solution.py
@@ -49,11 +49,17 @@
     return lax.dot_general(a, b, (dims, ((), ())), preferred_element_type=F32)
 
 
-def net_rows(live_ref, rows_ref, floor_ref, hot_ref, held_ref, out_ref, sums_ref, copies=None):
+def net_rows(
+    live_ref, rows_ref, floor_refs, hot_ref, held_ref, out_ref, sums_ref, copies=None
+):
     trade = lax.broadcasted_iota(jnp.int32, (TB, CHUNK), 0)
     for step in range(STEPS):
         rows = rows_ref[:, step].reshape(CHUNK, BASIS)
+        if copies and step + 1 < STEPS:
+            for copy in copies[step + 1]:
+                copy.start()
         for half in range(2):
+            floors = jnp.transpose(floor_refs[half][step])
             if copies:
                 copies[step][half].wait()
             for first in range(0, BPD, GROUP):
@@ -61,7 +67,7 @@
                 values = dot(held_ref[step, half, trades, :], rows, ((1,), (1,)))
                 for block in range(GROUP):
                     spot = half * BPD + first + block
-                    floor = floor_ref[step, :, spot : spot + 1]
+                    floor = floors[:, first + block : first + block + 1]
                     value = jnp.maximum(values[block * TB : (block + 1) * TB], floor)
                     value = jnp.where(trade < live_ref[spot], value, 0.0)
                     sums = value[:8]
@@ -76,7 +82,17 @@
 
 
 def net_first_kernel(
-    live_ref, rows_ref, mine_ref, other_ref, floor_ref, hot_ref, out_ref, held_ref, sums_ref, sems
+    live_ref,
+    rows_ref,
+    mine_ref,
+    other_ref,
+    my_floor_ref,
+    other_floor_ref,
+    hot_ref,
+    out_ref,
+    held_ref,
+    sums_ref,
+    sems,
 ):
     copies = [
         [
@@ -85,14 +101,17 @@
         ]
         for step in range(STEPS)
     ]
-    for pair in copies:
-        for copy in pair:
-            copy.start()
-    net_rows(live_ref, rows_ref, floor_ref, hot_ref, held_ref, out_ref, sums_ref, copies)
-
-
-def net_next_kernel(live_ref, rows_ref, held_ref, floor_ref, hot_ref, out_ref, sums_ref):
-    net_rows(live_ref, rows_ref, floor_ref, hot_ref, held_ref, out_ref, sums_ref)
+    for copy in copies[0]:
+        copy.start()
+    floors = (my_floor_ref, other_floor_ref)
+    net_rows(live_ref, rows_ref, floors, hot_ref, held_ref, out_ref, sums_ref, copies)
+
+
+def net_next_kernel(
+    live_ref, rows_ref, held_ref, my_floor_ref, other_floor_ref, hot_ref, out_ref, sums_ref
+):
+    floors = (my_floor_ref, other_floor_ref)
+    net_rows(live_ref, rows_ref, floors, hot_ref, held_ref, out_ref, sums_ref)
 
 
 VMEM = pl.BlockSpec(memory_space=pltpu.VMEM)
@@ -108,7 +127,7 @@
     mine = pltpu.with_memory_space_constraint(mine, pltpu.HBM)
     return pl.pallas_call(
         net_first_kernel,
-        in_specs=[SMEM, VMEM, ANY, ANY, VMEM, VMEM],
+        in_specs=[SMEM, VMEM, ANY, ANY, VMEM, VMEM, VMEM],
         out_specs=(VMEM, VMEM),
         out_shape=(jax.ShapeDtypeStruct(TERMS, F32), pltpu.VMEM(HELD, BF16)),
         scratch_shapes=[
@@ -117,20 +136,20 @@
         ],
         compiler_params=pltpu.CompilerParams(vmem_limit_bytes=20 << 20),
         name="net_first",
-    )(live, rows, mine, other, floors, hot)
+    )(live, rows, mine, other, *floors, hot)
 
 
 def net_next(rows, live, held, floors, hot):
     held = pltpu.with_memory_space_constraint(held, pltpu.VMEM)
     return pl.pallas_call(
         net_next_kernel,
-        in_specs=[SMEM, VMEM, VMEM, VMEM, VMEM],
+        in_specs=[SMEM] + [VMEM] * 5,
         out_specs=VMEM,
         out_shape=jax.ShapeDtypeStruct(TERMS, F32),
         scratch_shapes=[pltpu.VMEM((2 * BPD * 8, CHUNK), F32)],
         compiler_params=pltpu.CompilerParams(vmem_limit_bytes=12 << 20),
         name="net_next",
-    )(live, rows, held, floors, hot)
+    )(live, rows, held, *floors, hot)
 
 
 def line_kernel(first_ref, *refs):
@@ -179,7 +198,7 @@
     ids = (chip[:, :, None] * OWN + jnp.arange(OWN)).reshape(-1)
     owners = jnp.repeat(blocks[0], 8)
     hot = (ids[:, None] == owners[None, :]).astype(BF16)
-    both_floors = jnp.swapaxes(jnp.concatenate([exercise, other_floors], axis=1), 1, 2)
+    both_floors = (exercise, other_floors)
 
     arrived = {shift: shift_by(line, shift, 1) for shift in (1, 3, 2)}
     terms, sent = {}, {}

time: 73.8 us -> 74.4 us (level)
  other arithmetic: 4.19 us -> 1.94 us
  starting transfers between devices: 24.5 us -> 26.6 us
  Pallas kernels: 15.3 us -> 16.9 us
  local copies, waits for them, and re-layouts: 3.43 us -> 1.89 us
    ppermute x12, starting transfers between devices: 18.6 us -> 20.3 us  [shift_by(): return lax.ppermute(value, 'set', ring_pairs(shift, stage))]
    unnamed x19 -> x20, local copies, waits for them, and re-layouts: 1.6 us -> 0.06 us
    transpose x1 -> x0, other arithmetic: 1.03 us -> none  [body(): jnp.swapaxes(jnp.concatenate([exercise, other_floors], axis=1), 1, 2)]
    pallas_call x1, Pallas kernels: 0.03 us -> 0.92 us  [make_line(): pl.pallas_call(line_kernel, in_specs=[SMEM] + [pl.BlockSpec()] * SIDE, ou...]
  transfers between devices with their start and end apart: 19 -> 19, of which waited for: 8 -> 10; matrix products, arithmetic and copies ran while one was open for 20% -> 15% of each run, Pallas kernels for 17% -> 18%
where the time goes in v4:
time: 74.4 us; the launch traced here: 74.2 us
  starting transfers between devices  26.6 us (36%)
  waiting for transfers between devices  16.9 us (23%)
  Pallas kernels  16.9 us (23%)
  matrix products  8.67 us (12%)
  other arithmetic  1.94 us (3%)
  local copies, waits for them, and re-layouts  1.89 us (3%)
  between operations  1.17 us (2%)
    ppermute x12, starting transfers between devices, shift_by(): return lax.ppermute(value, 'set', ring_pairs(shift, stage))  20.3 us
    ppermute x12, waiting for transfers between devices, shift_by(): return lax.ppermute(value, 'set', ring_pairs(shift, stage))  12.1 us
    pallas_call x3, Pallas kernels, net_next(): pl.pallas_call(net_next_kernel, in_specs=[SMEM] + [VMEM] * 5, out_specs=V...  10.2 us
    dot_general x1, matrix products, body(): jnp.dot(scenarios.reshape(STEPS * ROWS, -1), projection, preferred_elemen...  8.45 us
    pallas_call x1, Pallas kernels, net_first(): pl.pallas_call(net_first_kernel, in_specs=[SMEM, VMEM, ANY, ANY, VMEM, VM...  5.85 us
    ppermute x3, starting transfers between devices, body(): lax.ppermute(sums, 'rep', [(i, (i + shift) % SIDE) for i in range(SIDE)])  5.23 us
    ppermute x3, waiting for transfers between devices, body(): lax.ppermute(sums, 'rep', [(i, (i + shift) % SIDE) for i in range(SIDE)])  3.14 us
    ppermute x4, waiting for transfers between devices, swap_core(): return lax.ppermute(value, 'set', CORE_PAIRS)  1.7 us
  transfers between devices with their start and end apart: 19, of which 10 were waited for; matrix products, arithmetic and copies ran while one was open for 15% of the time, Pallas kernels for 18%

profile of v4, /device:TPU:0, one launch (start us, length us, event | category | flops | bytes accessed | tf_op | source)
XLA Modules:
  0.0 74.2 jit_solution(10498280951755205897)
XLA Ops:
  0.8 8.5 %fusion = bf16[192,256]{1,0:T(8,128)(2,1)S(1)} fusion(bf16[192,20000]{1,0:T(8,128)(2,1)} %bitcast.258, bf16[20000,256]{1,0:T(8,128)(2,1)} %param.7), kind=kOutput, calls=%fused_computation.1 | convolution fusion | flops 1966129152 | bytes 18018304 | tf_op jit(solution)/shard_map/dot_general | solution.py:177
  9.2 2.9 %collective-permute-start.1 = (bf16[3,64,256]{2,1,0:T(8,128)(2,1)S(1)}, bf16[3,64,256]{2,1,0:T(8,128)(2,1)S(1)}, u32[]{:S(2)}, u32[]{:S(2)}) collective-permute-start(bf16[3,64,256]{2,1,0:T(8,128)(2,1)S(1)} %bitcast.252), channel_id=1, source_target_pairs={{0,6},{1,25},{2,0},{3,27},{4,2},{5,29},{6,4},{7,31},{8,14},{9,1},{... | collective-permute-start | bytes 294920 | tf_op jit(solution)/shard_map/ppermute | solution.py:41
  12.2 0.8 %collective-permute-start.2 = (bf16[3,64,256]{2,1,0:T(8,128)(2,1)S(1)}, bf16[3,64,256]{2,1,0:T(8,128)(2,1)S(1)}, u32[]{:S(2)}, u32[]{:S(2)}) collective-permute-start(bf16[3,64,256]{2,1,0:T(8,128)(2,1)S(1)} %bitcast.253), channel_id=1, source_target_pairs={{0,4},{1,17},{2,6},{3,19},{4,0},{5,21},{6,2},{7,23},{8,12},{9,25},... | collective-permute-start | bytes 294920 | tf_op jit(solution)/shard_map/ppermute | solution.py:41
  13.0 0.9 %collective-permute-start.3 = (bf16[3,64,256]{2,1,0:T(8,128)(2,1)S(1)}, bf16[3,64,256]{2,1,0:T(8,128)(2,1)}, u32[]{:S(2)}, u32[]{:S(2)}) collective-permute-start(bf16[3,64,256]{2,1,0:T(8,128)(2,1)S(1)} %bitcast.254), channel_id=1, source_target_pairs={{0,2},{1,9},{2,4},{3,11},{4,6},{5,13},{6,0},{7,15},{8,10},{9,17},{... | collective-permute-start | bytes 294920 | tf_op jit(solution)/shard_map/ppermute | solution.py:41
  13.9 0.6 collective-permute-start
  14.7 0.5 collective-permute-done
  15.7 0.7 broadcast_in_dim.2
  16.3 0.8 %eq.43 = s32[512]{0:T(512)S(1)} reshape(s32[64,8]{1,0:T(8,128)} %broadcast_in_dim.2) | data formatting | bytes 4096 | tf_op jit(solution)/shard_map/eq | solution.py:200
  17.2 1.1 %collective-permute-done.2.refs_2_ = bf16[3,64,256]{2,1,0:T(8,128)(2,1)S(1)} collective-permute-done((bf16[3,64,256]{2,1,0:T(8,128)(2,1)S(1)}, bf16[3,64,256]{2,1,0:T(8,128)(2,1)S(1)}, u32[]{:S(2)}, u32[]{:S(2)}) %collective-permute-start.2) | collective-permute-done | bytes 98336 | tf_op jit(solution)/shard_map/ppermute | solution.py:41
  18.3 1.1 %collective-permute-done.3.refs_3_ = bf16[3,64,256]{2,1,0:T(8,128)(2,1)} collective-permute-done((bf16[3,64,256]{2,1,0:T(8,128)(2,1)S(1)}, bf16[3,64,256]{2,1,0:T(8,128)(2,1)}, u32[]{:S(2)}, u32[]{:S(2)}) %collective-permute-start.3) | collective-permute-done | bytes 98336 | tf_op jit(solution)/shard_map/ppermute | solution.py:41
  19.4 0.9 %line.1.rows_ref = bf16[4,3,64,256]{3,2,1,0:T(8,128)(2,1)S(1)} custom-call(s32[1]{0:T(128)} %bitcast.3.first_ref, bf16[3,64,256]{2,1,0:T(8,128)(2,1)S(1)} %bitcast.255, bf16[3,64,256]{2,1,0:T(8,128)(2,1)S(1)} %collective-permute-done.1.refs_1_, bf16[3,64,256]{2,1,0:T(8,128)(2,1)S(1)} %collective-permute-done.2.refs_2_, ...), custom_call_target="tpu_custom_call" | custom-call | tf_op jit(solution)/shard_map/line/pallas_call | solution.py:162
  20.4 2.0 %collective-permute-start.6 = (bf16[4,3,64,256]{3,2,1,0:T(8,128)(2,1)S(1)}, bf16[4,3,64,256]{3,2,1,0:T(8,128)(2,1)S(1)}, u32[]{:S(2)}, u32[]{:S(2)}) collective-permute-start(bf16[4,3,64,256]{3,2,1,0:T(8,128)(2,1)S(1)} %line.1.rows_ref), channel_id=1, source_target_pairs={{0,8},{1,3},{2,10},{3,5},{4,12},{5,7},{6,14},{7,1},{8,16},{9,11},{... | collective-permute-start | bytes 1179656 | tf_op jit(solution)/shard_map/ppermute | solution.py:41
  22.4 2.2 %collective-permute-start.8 = (bf16[4,3,64,256]{3,2,1,0:T(8,128)(2,1)S(1)}, bf16[4,3,64,256]{3,2,1,0:T(8,128)(2,1)S(1)}, u32[]{:S(2)}, u32[]{:S(2)}) collective-permute-start(bf16[4,3,64,256]{3,2,1,0:T(8,128)(2,1)S(1)} %line.1.rows_ref), channel_id=1, source_target_pairs={{0,24},{1,7},{2,26},{3,1},{4,28},{5,3},{6,30},{7,5},{8,0},{9,15},{... | collective-permute-start | bytes 1179656 | tf_op jit(solution)/shard_map/ppermute | solution.py:41
  24.6 1.9 %collective-permute-start.7 = (bf16[4,3,64,256]{3,2,1,0:T(8,128)(2,1)S(1)}, bf16[4,3,64,256]{3,2,1,0:T(8,128)(2,1)S(1)}, u32[]{:S(2)}, u32[]{:S(2)}) collective-permute-start(bf16[4,3,64,256]{3,2,1,0:T(8,128)(2,1)S(1)} %line.1.rows_ref), channel_id=1, source_target_pairs={{0,16},{1,5},{2,18},{3,7},{4,20},{5,1},{6,22},{7,3},{8,24},{9,13},... | collective-permute-start | bytes 1179656 | tf_op jit(solution)/shard_map/ppermute | solution.py:41
  26.5 5.8 %net_first.1 = (f32[3,128,256]{2,1,0:T(8,128)S(1)}, bf16[3,2,2048,256]{3,2,1,0:T(8,128)(2,1)S(1)}) custom-call(s32[64]{0:T(128)S(1)} %get-tuple-element.88.live_ref, bf16[4,3,64,256]{3,2,1,0:T(8,128)(2,1)S(1)} %line.1.rows_ref, bf16[3,2048,256]{2,1,0:T(8,128)(2,1)} %bitcast.260, bf16[3,2048,256]{2,1,0:T(8,128)(2,1)S(1)} %collective-permute-done.4.other_ref, ...), custom_call_target="tpu_custom_call" | custom-call | tf_op jit(solution)/shard_map/net_first/pallas_call | solution.py:128
  32.4 3.4 %net_next.3 = f32[3,128,256]{2,1,0:T(8,128)S(1)} custom-call(s32[64]{0:T(128)S(1)} %get-tuple-element.88.live_ref, bf16[4,3,64,256]{3,2,1,0:T(8,128)(2,1)S(1)} %collective-permute-done.6.rows_ref, bf16[3,2,2048,256]{3,2,1,0:T(8,128)(2,1)S(1)} %get-tuple-element.12.held_ref, f32[3,32,64]{2,1,0:T(8,128)S(1)} %copy-done, ...), custom_call_target="tpu_custom_call" | custom-call | tf_op jit(solution)/shard_map/net_next/pallas_call | solution.py:144
  35.8 3.4 %net_next.4 = f32[3,128,256]{2,1,0:T(8,128)S(1)} custom-call(s32[64]{0:T(128)S(1)} %get-tuple-element.88.live_ref, bf16[4,3,64,256]{3,2,1,0:T(8,128)(2,1)S(1)} %collective-permute-done.8.rows_ref, bf16[3,2,2048,256]{3,2,1,0:T(8,128)(2,1)S(1)} %get-tuple-element.12.held_ref, f32[3,32,64]{2,1,0:T(8,128)S(1)} %copy-done, ...), custom_call_target="tpu_custom_call" | custom-call | tf_op jit(solution)/shard_map/net_next/pallas_call | solution.py:144
  39.3 3.4 %net_next.5 = f32[3,128,256]{2,1,0:T(8,128)S(1)} custom-call(s32[64]{0:T(128)S(1)} %get-tuple-element.88.live_ref, bf16[4,3,64,256]{3,2,1,0:T(8,128)(2,1)S(1)} %collective-permute-done.7.rows_ref, bf16[3,2,2048,256]{3,2,1,0:T(8,128)(2,1)S(1)} %get-tuple-element.12.held_ref, f32[3,32,64]{2,1,0:T(8,128)S(1)} %copy-done, ...), custom_call_target="tpu_custom_call" | custom-call | tf_op jit(solution)/shard_map/net_next/pallas_call | solution.py:144
  43.6 3.3 %collective-permute-start.10 = (f16[4,3,8,1024]{3,2,1,0:T(8,128)(2,1)S(1)}, f16[4,3,8,1024]{3,2,1,0:T(8,128)(2,1)S(1)}, u32[]{:S(2)}, u32[]{:S(2)}) collective-permute-start(f16[4,3,8,1024]{3,2,1,0:T(8,128)(2,1)S(1)} %pad_maximum_fusion.1), channel_id=1, source_target_pairs={{0,6},{1,25},{2,0},{3,27},{4,2},{5,29},{6,4},{7,31},{8,14},{9,1},{... | collective-permute-start | bytes 589832 | tf_op jit(solution)/shard_map/ppermute | solution.py:41
  47.4 2.9 %collective-permute-done.9 = f16[4,3,8,1024]{3,2,1,0:T(8,128)(2,1)S(1)} collective-permute-done((f16[4,3,8,1024]{3,2,1,0:T(8,128)(2,1)S(1)}, f16[4,3,8,1024]{3,2,1,0:T(8,128)(2,1)S(1)}, u32[]{:S(2)}, u32[]{:S(2)}) %collective-permute-start.9) | collective-permute-done | bytes 196640 | tf_op jit(solution)/shard_map/ppermute | solution.py:41
  50.3 1.9 %collective-permute-done.10 = f16[4,3,8,1024]{3,2,1,0:T(8,128)(2,1)S(1)} collective-permute-done((f16[4,3,8,1024]{3,2,1,0:T(8,128)(2,1)S(1)}, f16[4,3,8,1024]{3,2,1,0:T(8,128)(2,1)S(1)}, u32[]{:S(2)}, u32[]{:S(2)}) %collective-permute-start.10) | collective-permute-done | bytes 196640 | tf_op jit(solution)/shard_map/ppermute | solution.py:41
  52.2 2.1 %collective-permute-done.11 = f16[4,3,8,1024]{3,2,1,0:T(8,128)(2,1)S(1)} collective-permute-done((f16[4,3,8,1024]{3,2,1,0:T(8,128)(2,1)S(1)}, f16[4,3,8,1024]{3,2,1,0:T(8,128)(2,1)S(1)}, u32[]{:S(2)}, u32[]{:S(2)}) %collective-permute-start.11) | collective-permute-done | bytes 196640 | tf_op jit(solution)/shard_map/ppermute | solution.py:41
  54.5 2.1 %collective-permute-start.12 = (f16[3,8,1024]{2,1,0:T(8,128)(2,1)S(1)}, f16[3,8,1024]{2,1,0:T(8,128)(2,1)S(1)}, u32[]{:S(2)}, u32[]{:S(2)}) collective-permute-start(f16[3,8,1024]{2,1,0:T(8,128)(2,1)S(1)} %get-tuple-element.20), channel_id=1, source_target_pairs={{0,8},{1,3},{2,10},{3,5},{4,12},{5,7},{6,14},{7,1},{8,16},{9,11},{... | collective-permute-start | bytes 147464 | tf_op jit(solution)/shard_map/ppermute | solution.py:41
  56.6 1.2 %collective-permute-start.13 = (f16[3,8,1024]{2,1,0:T(8,128)(2,1)S(1)}, f16[3,8,1024]{2,1,0:T(8,128)(2,1)S(1)}, u32[]{:S(2)}, u32[]{:S(2)}) collective-permute-start(f16[3,8,1024]{2,1,0:T(8,128)(2,1)S(1)} %get-tuple-element.22), channel_id=1, source_target_pairs={{0,24},{1,7},{2,26},{3,1},{4,28},{5,3},{6,30},{7,5},{8,0},{9,15},{... | collective-permute-start | bytes 147464 | tf_op jit(solution)/shard_map/ppermute | solution.py:41
  57.8 2.7 %collective-permute-start.14 = (f16[3,8,1024]{2,1,0:T(8,128)(2,1)S(1)}, f16[3,8,1024]{2,1,0:T(8,128)(2,1)S(1)}, u32[]{:S(2)}, u32[]{:S(2)}) collective-permute-start(f16[3,8,1024]{2,1,0:T(8,128)(2,1)S(1)} %get-tuple-element.21), channel_id=1, source_target_pairs={{0,16},{1,5},{2,18},{3,7},{4,20},{5,1},{6,22},{7,3},{8,24},{9,13},... | collective-permute-start | bytes 147464 | tf_op jit(solution)/shard_map/ppermute | solution.py:41
  60.7 2.7 %collective-permute-done.14 = f16[3,8,1024]{2,1,0:T(8,128)(2,1)S(1)} collective-permute-done((f16[3,8,1024]{2,1,0:T(8,128)(2,1)S(1)}, f16[3,8,1024]{2,1,0:T(8,128)(2,1)S(1)}, u32[]{:S(2)}, u32[]{:S(2)}) %collective-permute-start.14) | collective-permute-done | bytes 49184 | tf_op jit(solution)/shard_map/ppermute | solution.py:41
  63.8 1.1 %collective-permute-done.15 = f32[3,4,8]{2,1,0:T(4,128)S(1)} collective-permute-done((f32[3,4,8]{2,1,0:T(4,128)S(1)}, f32[3,4,8]{2,1,0:T(4,128)S(1)}, u32[]{:S(2)}, u32[]{:S(2)}) %collective-permute-start.15) | collective-permute-done | bytes 416 | tf_op jit(solution)/shard_map/ppermute | solution.py:45
  64.9 1.6 %collective-permute-start.16 = (f32[3,4,8]{2,1,0:T(4,128)S(1)}, f32[3,4,8]{2,1,0:T(4,128)S(1)}, u32[]{:S(2)}, u32[]{:S(2)}) collective-permute-start(f32[3,4,8]{2,1,0:T(4,128)S(1)} %bitcast_add_fusion), channel_id=1, source_target_pairs={{0,32},{32,64},{64,96},{96,0},{1,33},{33,65},{65,97},{97,1},{2,34}... | collective-permute-start | bytes 1160 | tf_op jit(solution)/shard_map/ppermute | solution.py:243
  66.5 1.6 %collective-permute-start.17 = (f32[3,4,8]{2,1,0:T(4,128)S(1)}, f32[3,4,8]{2,1,0:T(4,128)S(1)}, u32[]{:S(2)}, u32[]{:S(2)}) collective-permute-start(f32[3,4,8]{2,1,0:T(4,128)S(1)} %bitcast_add_fusion), channel_id=1, source_target_pairs={{0,96},{32,0},{64,32},{96,64},{1,97},{33,1},{65,33},{97,65},{2,98}... | collective-permute-start | bytes 1160 | tf_op jit(solution)/shard_map/ppermute | solution.py:243
  68.2 2.0 %collective-permute-start.18 = (f32[3,4,8]{2,1,0:T(4,128)S(1)}, f32[3,4,8]{2,1,0:T(4,128)S(1)}, u32[]{:S(2)}, u32[]{:S(2)}) collective-permute-start(f32[3,4,8]{2,1,0:T(4,128)S(1)} %bitcast_add_fusion), channel_id=1, source_target_pairs={{0,64},{32,96},{64,0},{96,32},{1,65},{33,97},{65,1},{97,33},{2,66}... | collective-permute-start | bytes 1160 | tf_op jit(solution)/shard_map/ppermute | solution.py:243
  70.2 3.1 %collective-permute-done.18 = f32[3,4,8]{2,1,0:T(4,128)S(1)} collective-permute-done((f32[3,4,8]{2,1,0:T(4,128)S(1)}, f32[3,4,8]{2,1,0:T(4,128)S(1)}, u32[]{:S(2)}, u32[]{:S(2)}) %collective-permute-start.18) | collective-permute-done | bytes 416 | tf_op jit(solution)/shard_map/ppermute | solution.py:243
  73.6 0.6 multiply_sqrt_fusion
  (86 shorter events, 3.0 us)
Async XLA Ops:
  0.6 25.9 %collective-permute-start.4 = (bf16[3,2048,256]{2,1,0:T(8,128)(2,1)}, bf16[3,2048,256]{2,1,0:T(8,128)(2,1)S(1)}, u32[]{:S(2)}, u32[]{:S(2)}) collective-permute-start(bf16[3,2048,256]{2,1,0:T(8,128)(2,1)} %bitcast.259), channel_id=1, source_target_pairs={{0,1},{1,0},{2,3},{3,2},{4,5},{5,4},{6,7},{7,6},{8,9},{9,8},{10,11... | collective-permute-start | bytes 9437192 | tf_op jit(solution)/shard_map/ppermute | solution.py:45
  0.7 13.1 %copy-start.2 = (s32[32]{0:T(128)S(1)}, s32[32]{0:T(128)}, u32[]{:S(2)}) copy-start(s32[32]{0:T(128)} %param.11) | copy-start | bytes 388
  0.7 13.1 %copy-start.3 = (s32[32]{0:T(128)S(1)}, s32[32]{0:T(128)}, u32[]{:S(2)}) copy-start(s32[32]{0:T(128)} %param.10) | copy-start | bytes 388
  0.7 14.5 %copy-start = (f32[3,32,64]{2,1,0:T(8,128)S(1)}, f32[3,32,64]{2,1,0:T(8,128)}, u32[]{:S(2)}) copy-start(f32[3,32,64]{2,1,0:T(8,128)} %my_floor_ref.7) | copy-start | bytes 73732
  9.2 8.0 %collective-permute-start.1 = (bf16[3,64,256]{2,1,0:T(8,128)(2,1)S(1)}, bf16[3,64,256]{2,1,0:T(8,128)(2,1)S(1)}, u32[]{:S(2)}, u32[]{:S(2)}) collective-permute-start(bf16[3,64,256]{2,1,0:T(8,128)(2,1)S(1)} %bitcast.252), channel_id=1, source_target_pairs={{0,6},{1,25},{2,0},{3,27},{4,2},{5,29},{6,4},{7,31},{8,14},{9,1},{... | collective-permute-start | bytes 294920 | tf_op jit(solution)/shard_map/ppermute | solution.py:41
  12.2 6.2 %collective-permute-start.2 = (bf16[3,64,256]{2,1,0:T(8,128)(2,1)S(1)}, bf16[3,64,256]{2,1,0:T(8,128)(2,1)S(1)}, u32[]{:S(2)}, u32[]{:S(2)}) collective-permute-start(bf16[3,64,256]{2,1,0:T(8,128)(2,1)S(1)} %bitcast.253), channel_id=1, source_target_pairs={{0,4},{1,17},{2,6},{3,19},{4,0},{5,21},{6,2},{7,23},{8,12},{9,25},... | collective-permute-start | bytes 294920 | tf_op jit(solution)/shard_map/ppermute | solution.py:41
  13.0 6.5 %collective-permute-start.3 = (bf16[3,64,256]{2,1,0:T(8,128)(2,1)S(1)}, bf16[3,64,256]{2,1,0:T(8,128)(2,1)}, u32[]{:S(2)}, u32[]{:S(2)}) collective-permute-start(bf16[3,64,256]{2,1,0:T(8,128)(2,1)S(1)} %bitcast.254), channel_id=1, source_target_pairs={{0,2},{1,9},{2,4},{3,11},{4,6},{5,13},{6,0},{7,15},{8,10},{9,17},{... | collective-permute-start | bytes 294920 | tf_op jit(solution)/shard_map/ppermute | solution.py:41
  13.9 1.4 %collective-permute-start = (s32[2,32]{1,0:T(2,128)S(1)}, s32[2,32]{1,0:T(2,128)S(1)}, u32[]{:S(2)}, u32[]{:S(2)}) collective-permute-start(s32[2,32]{1,0:T(2,128)S(1)} %pad_add_fusion), channel_id=1, source_target_pairs={{0,1},{1,0},{2,3},{3,2},{4,5},{5,4},{6,7},{7,6},{8,9},{9,8},{10,11... | collective-permute-start | bytes 776 | tf_op jit(solution)/shard_map/ppermute | solution.py:45
  15.2 11.3 %collective-permute-start.5 = (f32[3,32,64]{2,1,0:T(8,128)S(1)}, f32[3,32,64]{2,1,0:T(8,128)S(1)}, u32[]{:S(2)}, u32[]{:S(2)}) collective-permute-start(f32[3,32,64]{2,1,0:T(8,128)S(1)} %copy-done), channel_id=1, source_target_pairs={{0,1},{1,0},{2,3},{3,2},{4,5},{5,4},{6,7},{7,6},{8,9},{9,8},{10,11... | collective-permute-start | bytes 73736 | tf_op jit(solution)/shard_map/ppermute | solution.py:45
  20.4 12.0 %collective-permute-start.6 = (bf16[4,3,64,256]{3,2,1,0:T(8,128)(2,1)S(1)}, bf16[4,3,64,256]{3,2,1,0:T(8,128)(2,1)S(1)}, u32[]{:S(2)}, u32[]{:S(2)}) collective-permute-start(bf16[4,3,64,256]{3,2,1,0:T(8,128)(2,1)S(1)} %line.1.rows_ref), channel_id=1, source_target_pairs={{0,8},{1,3},{2,10},{3,5},{4,12},{5,7},{6,14},{7,1},{8,16},{9,11},{... | collective-permute-start | bytes 1179656 | tf_op jit(solution)/shard_map/ppermute | solution.py:41
  22.4 13.4 %collective-permute-start.8 = (bf16[4,3,64,256]{3,2,1,0:T(8,128)(2,1)S(1)}, bf16[4,3,64,256]{3,2,1,0:T(8,128)(2,1)S(1)}, u32[]{:S(2)}, u32[]{:S(2)}) collective-permute-start(bf16[4,3,64,256]{3,2,1,0:T(8,128)(2,1)S(1)} %line.1.rows_ref), channel_id=1, source_target_pairs={{0,24},{1,7},{2,26},{3,1},{4,28},{5,3},{6,30},{7,5},{8,0},{9,15},{... | collective-permute-start | bytes 1179656 | tf_op jit(solution)/shard_map/ppermute | solution.py:41
  24.6 14.6 %collective-permute-start.7 = (bf16[4,3,64,256]{3,2,1,0:T(8,128)(2,1)S(1)}, bf16[4,3,64,256]{3,2,1,0:T(8,128)(2,1)S(1)}, u32[]{:S(2)}, u32[]{:S(2)}) collective-permute-start(bf16[4,3,64,256]{3,2,1,0:T(8,128)(2,1)S(1)} %line.1.rows_ref), channel_id=1, source_target_pairs={{0,16},{1,5},{2,18},{3,7},{4,20},{5,1},{6,22},{7,3},{8,24},{9,13},... | collective-permute-start | bytes 1179656 | tf_op jit(solution)/shard_map/ppermute | solution.py:41
  43.1 7.2 %collective-permute-start.9 = (f16[4,3,8,1024]{3,2,1,0:T(8,128)(2,1)S(1)}, f16[4,3,8,1024]{3,2,1,0:T(8,128)(2,1)S(1)}, u32[]{:S(2)}, u32[]{:S(2)}) collective-permute-start(f16[4,3,8,1024]{3,2,1,0:T(8,128)(2,1)S(1)} %pad_maximum_fusion), channel_id=1, source_target_pairs={{0,2},{1,9},{2,4},{3,11},{4,6},{5,13},{6,0},{7,15},{8,10},{9,17},{... | collective-permute-start | bytes 589832 | tf_op jit(solution)/shard_map/ppermute | solution.py:41
  43.6 8.6 %collective-permute-start.10 = (f16[4,3,8,1024]{3,2,1,0:T(8,128)(2,1)S(1)}, f16[4,3,8,1024]{3,2,1,0:T(8,128)(2,1)S(1)}, u32[]{:S(2)}, u32[]{:S(2)}) collective-permute-start(f16[4,3,8,1024]{3,2,1,0:T(8,128)(2,1)S(1)} %pad_maximum_fusion.1), channel_id=1, source_target_pairs={{0,6},{1,25},{2,0},{3,27},{4,2},{5,29},{6,4},{7,31},{8,14},{9,1},{... | collective-permute-start | bytes 589832 | tf_op jit(solution)/shard_map/ppermute | solution.py:41
  47.1 7.3 %collective-permute-start.11 = (f16[4,3,8,1024]{3,2,1,0:T(8,128)(2,1)S(1)}, f16[4,3,8,1024]{3,2,1,0:T(8,128)(2,1)S(1)}, u32[]{:S(2)}, u32[]{:S(2)}) collective-permute-start(f16[4,3,8,1024]{3,2,1,0:T(8,128)(2,1)S(1)} %pad_maximum_fusion.2), channel_id=1, source_target_pairs={{0,4},{1,17},{2,6},{3,19},{4,0},{5,21},{6,2},{7,23},{8,12},{9,25},... | collective-permute-start | bytes 589832 | tf_op jit(solution)/shard_map/ppermute | solution.py:41
  54.5 6.0 %collective-permute-start.12 = (f16[3,8,1024]{2,1,0:T(8,128)(2,1)S(1)}, f16[3,8,1024]{2,1,0:T(8,128)(2,1)S(1)}, u32[]{:S(2)}, u32[]{:S(2)}) collective-permute-start(f16[3,8,1024]{2,1,0:T(8,128)(2,1)S(1)} %get-tuple-element.20), channel_id=1, source_target_pairs={{0,8},{1,3},{2,10},{3,5},{4,12},{5,7},{6,14},{7,1},{8,16},{9,11},{... | collective-permute-start | bytes 147464 | tf_op jit(solution)/shard_map/ppermute | solution.py:41
  56.6 4.1 %collective-permute-start.13 = (f16[3,8,1024]{2,1,0:T(8,128)(2,1)S(1)}, f16[3,8,1024]{2,1,0:T(8,128)(2,1)S(1)}, u32[]{:S(2)}, u32[]{:S(2)}) collective-permute-start(f16[3,8,1024]{2,1,0:T(8,128)(2,1)S(1)} %get-tuple-element.22), channel_id=1, source_target_pairs={{0,24},{1,7},{2,26},{3,1},{4,28},{5,3},{6,30},{7,5},{8,0},{9,15},{... | collective-permute-start | bytes 147464 | tf_op jit(solution)/shard_map/ppermute | solution.py:41
  57.8 5.6 %collective-permute-start.14 = (f16[3,8,1024]{2,1,0:T(8,128)(2,1)S(1)}, f16[3,8,1024]{2,1,0:T(8,128)(2,1)S(1)}, u32[]{:S(2)}, u32[]{:S(2)}) collective-permute-start(f16[3,8,1024]{2,1,0:T(8,128)(2,1)S(1)} %get-tuple-element.21), channel_id=1, source_target_pairs={{0,16},{1,5},{2,18},{3,7},{4,20},{5,1},{6,22},{7,3},{8,24},{9,13},... | collective-permute-start | bytes 147464 | tf_op jit(solution)/shard_map/ppermute | solution.py:41
  63.7 1.2 %collective-permute-start.15 = (f32[3,4,8]{2,1,0:T(4,128)S(1)}, f32[3,4,8]{2,1,0:T(4,128)S(1)}, u32[]{:S(2)}, u32[]{:S(2)}) collective-permute-start(f32[3,4,8]{2,1,0:T(4,128)S(1)} %dynamic-slice_bitcast_fusion), channel_id=1, source_target_pairs={{0,1},{1,0},{2,3},{3,2},{4,5},{5,4},{6,7},{7,6},{8,9},{9,8},{10,11... | collective-permute-start | bytes 1160 | tf_op jit(solution)/shard_map/ppermute | solution.py:45
  64.9 5.2 %collective-permute-start.16 = (f32[3,4,8]{2,1,0:T(4,128)S(1)}, f32[3,4,8]{2,1,0:T(4,128)S(1)}, u32[]{:S(2)}, u32[]{:S(2)}) collective-permute-start(f32[3,4,8]{2,1,0:T(4,128)S(1)} %bitcast_add_fusion), channel_id=1, source_target_pairs={{0,32},{32,64},{64,96},{96,0},{1,33},{33,65},{65,97},{97,1},{2,34}... | collective-permute-start | bytes 1160 | tf_op jit(solution)/shard_map/ppermute | solution.py:243
  66.5 3.6 %collective-permute-start.17 = (f32[3,4,8]{2,1,0:T(4,128)S(1)}, f32[3,4,8]{2,1,0:T(4,128)S(1)}, u32[]{:S(2)}, u32[]{:S(2)}) collective-permute-start(f32[3,4,8]{2,1,0:T(4,128)S(1)} %bitcast_add_fusion), channel_id=1, source_target_pairs={{0,96},{32,0},{64,32},{96,64},{1,97},{33,1},{65,33},{97,65},{2,98}... | collective-permute-start | bytes 1160 | tf_op jit(solution)/shard_map/ppermute | solution.py:243
  68.2 5.1 %collective-permute-start.18 = (f32[3,4,8]{2,1,0:T(4,128)S(1)}, f32[3,4,8]{2,1,0:T(4,128)S(1)}, u32[]{:S(2)}, u32[]{:S(2)}) collective-permute-start(f32[3,4,8]{2,1,0:T(4,128)S(1)} %bitcast_add_fusion), channel_id=1, source_target_pairs={{0,64},{32,96},{64,0},{96,32},{1,65},{33,97},{65,1},{97,33},{2,66}... | collective-permute-start | bytes 1160 | tf_op jit(solution)/shard_map/ppermute | solution.py:243
  73.4 0.8 %copy-start.1 = (f32[3,4]{1,0:T(4,128)}, f32[3,4]{1,0:T(4,128)S(1)}, u32[]{:S(2)}) copy-start(f32[3,4]{1,0:T(4,128)S(1)} %broadcast_multiply_fusion) | copy-start | bytes 148

commit v5 on v3

--- a/solution.py
+++ b/solution.py
@@ -13,6 +13,8 @@
 BPD = 32
 TB = 64
 BASIS = 256
+FACTORS = 20000
+FACTOR_TILE = 6784
 ROWS = 64
 CHUNK = SIDE * ROWS
 OWN = 2 * SPD
@@ -49,19 +51,25 @@
     return lax.dot_general(a, b, (dims, ((), ())), preferred_element_type=F32)
 
 
-def net_rows(live_ref, rows_ref, floor_ref, hot_ref, held_ref, out_ref, sums_ref, copies=None):
+def net_rows(
+    live_ref, rows_ref, held_ref, other_ref, my_floor_ref, other_floor_ref, hot_ref, out_ref, sums_ref,
+    copies=None,
+):
     trade = lax.broadcasted_iota(jnp.int32, (TB, CHUNK), 0)
     for step in range(STEPS):
         rows = rows_ref[:, step].reshape(CHUNK, BASIS)
-        for half in range(2):
-            if copies:
-                copies[step][half].wait()
+        for half, (weights, floors) in enumerate(
+            ((held_ref, my_floor_ref), (other_ref, other_floor_ref))
+        ):
+            if copies and half == 0:
+                copies[step].wait()
+            floors = jnp.transpose(floors[step])
             for first in range(0, BPD, GROUP):
                 trades = slice(first * TB, (first + GROUP) * TB)
-                values = dot(held_ref[step, half, trades, :], rows, ((1,), (1,)))
+                values = dot(weights[step, trades, :], rows, ((1,), (1,)))
                 for block in range(GROUP):
                     spot = half * BPD + first + block
-                    floor = floor_ref[step, :, spot : spot + 1]
+                    floor = floors[:, first + block : first + block + 1]
                     value = jnp.maximum(values[block * TB : (block + 1) * TB], floor)
                     value = jnp.where(trade < live_ref[spot], value, 0.0)
                     sums = value[:8]
@@ -76,61 +84,103 @@
 
 
 def net_first_kernel(
-    live_ref, rows_ref, mine_ref, other_ref, floor_ref, hot_ref, out_ref, held_ref, sums_ref, sems
+    live_ref, rows_ref, mine_ref, other_ref, my_floor_ref, other_floor_ref, hot_ref, out_ref, held_ref,
+    sums_ref, sems,
 ):
     copies = [
-        [
-            pltpu.make_async_copy(source.at[step], held_ref.at[step, half], sems.at[step, half])
-            for half, source in enumerate((mine_ref, other_ref))
-        ]
+        pltpu.make_async_copy(mine_ref.at[step], held_ref.at[step], sems.at[step])
         for step in range(STEPS)
     ]
-    for pair in copies:
-        for copy in pair:
-            copy.start()
-    net_rows(live_ref, rows_ref, floor_ref, hot_ref, held_ref, out_ref, sums_ref, copies)
-
-
-def net_next_kernel(live_ref, rows_ref, held_ref, floor_ref, hot_ref, out_ref, sums_ref):
-    net_rows(live_ref, rows_ref, floor_ref, hot_ref, held_ref, out_ref, sums_ref)
+    for copy in copies:
+        copy.start()
+    net_rows(
+        live_ref, rows_ref, held_ref, other_ref, my_floor_ref, other_floor_ref, hot_ref, out_ref,
+        sums_ref, copies,
+    )
+
+
+def net_next_kernel(*refs):
+    net_rows(*refs)
 
 
 VMEM = pl.BlockSpec(memory_space=pltpu.VMEM)
 SMEM = pl.BlockSpec(memory_space=pltpu.SMEM)
-ANY = pl.BlockSpec(memory_space=pl.ANY)
+HBM = pl.BlockSpec(memory_space=pltpu.HBM)
 
 
 TERMS = (STEPS, SIDE * SIDE * OWN, CHUNK)
-HELD = (STEPS, 2, BPD * TB, BASIS)
-
-
-def net_first(rows, live, mine, other, floors, hot):
+HELD = (STEPS, BPD * TB, BASIS)
+
+
+def net_first(rows, live, mine, other, my_floors, other_floors, hot):
     mine = pltpu.with_memory_space_constraint(mine, pltpu.HBM)
+    other = pltpu.with_memory_space_constraint(other, pltpu.VMEM)
     return pl.pallas_call(
         net_first_kernel,
-        in_specs=[SMEM, VMEM, ANY, ANY, VMEM, VMEM],
+        in_specs=[SMEM, VMEM, HBM, VMEM, VMEM, VMEM, VMEM],
         out_specs=(VMEM, VMEM),
         out_shape=(jax.ShapeDtypeStruct(TERMS, F32), pltpu.VMEM(HELD, BF16)),
         scratch_shapes=[
             pltpu.VMEM((2 * BPD * 8, CHUNK), F32),
-            pltpu.SemaphoreType.DMA((STEPS, 2)),
+            pltpu.SemaphoreType.DMA((STEPS,)),
         ],
-        compiler_params=pltpu.CompilerParams(vmem_limit_bytes=20 << 20),
+        compiler_params=pltpu.CompilerParams(vmem_limit_bytes=12 << 20),
         name="net_first",
-    )(live, rows, mine, other, floors, hot)
-
-
-def net_next(rows, live, held, floors, hot):
+    )(live, rows, mine, other, my_floors, other_floors, hot)
+
+
+def net_next(rows, live, held, other, my_floors, other_floors, hot):
     held = pltpu.with_memory_space_constraint(held, pltpu.VMEM)
+    other = pltpu.with_memory_space_constraint(other, pltpu.VMEM)
     return pl.pallas_call(
         net_next_kernel,
-        in_specs=[SMEM, VMEM, VMEM, VMEM, VMEM],
+        in_specs=[SMEM] + [VMEM] * 6,
         out_specs=VMEM,
         out_shape=jax.ShapeDtypeStruct(TERMS, F32),
         scratch_shapes=[pltpu.VMEM((2 * BPD * 8, CHUNK), F32)],
         compiler_params=pltpu.CompilerParams(vmem_limit_bytes=12 << 20),
         name="net_next",
-    )(live, rows, held, floors, hot)
+    )(live, rows, held, other, my_floors, other_floors, hot)
+
+
+def basis_kernel(scenarios_ref, projection_ref, out_ref, sums_ref):
+    step = pl.program_id(0)
+    last = pl.num_programs(0) - 1
+    width = FACTORS - (-(-FACTORS // FACTOR_TILE) - 1) * FACTOR_TILE
+    rows = STEPS * ROWS
+
+    @pl.when(step == 0)
+    def _():
+        sums_ref[...] = jnp.zeros_like(sums_ref)
+
+    @pl.when(step < last)
+    def _():
+        tile = scenarios_ref[...].reshape(rows, FACTOR_TILE)
+        sums_ref[...] += dot(tile, projection_ref[...], ((1,), (0,)))
+
+    @pl.when(step == last)
+    def _():
+        tile = scenarios_ref[:, :, :width].reshape(rows, width)
+        sums = sums_ref[...] + dot(tile, projection_ref[:width, :], ((1,), (0,)))
+        out_ref[...] = jnp.tanh(sums).astype(BF16).reshape(STEPS, ROWS, BASIS)
+
+
+def make_basis(scenarios, projection):
+    scenarios = pltpu.with_memory_space_constraint(scenarios, pltpu.HBM)
+    projection = pltpu.with_memory_space_constraint(projection, pltpu.HBM)
+    return pl.pallas_call(
+        basis_kernel,
+        grid=(-(-FACTORS // FACTOR_TILE),),
+        in_specs=[
+            pl.BlockSpec((STEPS, ROWS, FACTOR_TILE), lambda k: (0, 0, k)),
+            pl.BlockSpec((FACTOR_TILE, BASIS), lambda k: (k, 0)),
+        ],
+        out_specs=pl.BlockSpec((STEPS, ROWS, BASIS), lambda k: (0, 0, 0)),
+        out_shape=jax.ShapeDtypeStruct((STEPS, ROWS, BASIS), BF16),
+        scratch_shapes=[pltpu.VMEM((STEPS * ROWS, BASIS), F32)],
+        compiler_params=pltpu.CompilerParams(vmem_limit_bytes=24 << 20),
+        name="basis",
+    )(scenarios, projection)
 
 
 def line_kernel(first_ref, *refs):
@@ -154,12 +204,7 @@
     place = lax.axis_index("set")
     z, x, core = place // 8, (place // 2) % SIDE, place % 2
 
-    basis = jnp.tanh(
-        jnp.dot(
-            scenarios.reshape(STEPS * ROWS, -1), projection, preferred_element_type=F32
-        )
-    ).astype(BF16)
-    basis = basis.reshape(STEPS, ROWS, BASIS)
+    basis = make_basis(scenarios, projection)
     weights = jnp.transpose(coefs, (0, 2, 3, 1)).reshape(STEPS, BPD * TB, BASIS)
 
     first = jnp.where(core == 0, x, z)
@@ -179,16 +224,16 @@
     ids = (chip[:, :, None] * OWN + jnp.arange(OWN)).reshape(-1)
     owners = jnp.repeat(blocks[0], 8)
     hot = (ids[:, None] == owners[None, :]).astype(BF16)
-    both_floors = jnp.swapaxes(jnp.concatenate([exercise, other_floors], axis=1), 1, 2)
 
     arrived = {shift: shift_by(line, shift, 1) for shift in (1, 3, 2)}
     terms, sent = {}, {}
     rows = line
-    for shift, following in ((0, 1), (1, 3), (3, 2), (2, None)):
+    for shift, following in ((0, 3), (3, 2), (2, 1), (1, None)):
+        fixed = (other_weights, exercise, other_floors, hot)
         if shift == 0:
-            term, held = net_first(rows, blocks[1], weights, other_weights, both_floors, hot)
+            term, held = net_first(rows, blocks[1], weights, *fixed)
         else:
-            term = net_next(rows, blocks[1], held, both_floors, hot)
+            term = net_next(rows, blocks[1], held, *fixed)
         terms[shift] = term.reshape(STEPS, SIDE, SIDE, OWN, CHUNK)
         sent[shift] = terms[shift][:, 1:].astype(jnp.float16)
         if following:

time: 73.8 us -> 75.1 us (1.018)
  Pallas kernels: 15.3 us -> 23.9 us
  matrix products: 8.67 us -> 0.21 us
  waiting for transfers between devices: 16.2 us -> 20.9 us
  other arithmetic: 4.19 us -> 1.94 us
  local copies, waits for them, and re-layouts: 3.43 us -> 1.89 us
    dot_general x1 -> x0, matrix products: 8.45 us -> none  [body(): jnp.dot(scenarios.reshape(STEPS * ROWS, -1), projection, preferred_elemen...]
    pallas_call x4 -> x5, Pallas kernels: 15.3 us -> 23 us  [the longest x3 10.2 us: net_next(): pl.pallas_call(net_next_kernel, in_specs=[SMEM] + [VMEM] * 6, out_specs=V...]
    ppermute x12, waiting for transfers between devices: 11.9 us -> 15.3 us  [shift_by(): return lax.ppermute(value, 'set', ring_pairs(shift, stage))]
    unnamed x19 -> x20, local copies, waits for them, and re-layouts: 1.6 us -> 0.06 us
    transpose x1 -> x0, other arithmetic: 1.03 us -> none  [body(): jnp.swapaxes(jnp.concatenate([exercise, other_floors], axis=1), 1, 2)]
    pallas_call x1, Pallas kernels: 0.03 us -> 0.92 us  [make_line(): pl.pallas_call(line_kernel, in_specs=[SMEM] + [pl.BlockSpec()] * SIDE, ou...]
  transfers between devices with their start and end apart: 19 -> 19, of which waited for: 8 -> 12; matrix products, arithmetic and copies ran while one was open for 20% -> 3% of each run, Pallas kernels for 17% -> 27%
where the time goes in v5:
time: 75.1 us; the launch traced here: 74.9 us
  starting transfers between devices  24.9 us (33%)
  Pallas kernels  23.9 us (32%)
  waiting for transfers between devices  20.9 us (28%)
  other arithmetic  1.94 us (3%)
  local copies, waits for them, and re-layouts  1.89 us (3%)
  between operations  1.15 us (2%)
    ppermute x12, starting transfers between devices, shift_by(): return lax.ppermute(value, 'set', ring_pairs(shift, stage))  18.6 us
    ppermute x12, waiting for transfers between devices, shift_by(): return lax.ppermute(value, 'set', ring_pairs(shift, stage))  15.3 us
    pallas_call x3, Pallas kernels, net_next(): pl.pallas_call(net_next_kernel, in_specs=[SMEM] + [VMEM] * 6, out_specs=V...  10.2 us
    pallas_call x1, Pallas kernels, make_basis(): pl.pallas_call(basis_kernel, grid=(-(-FACTORS // FACTOR_TILE),), in_specs...  7.43 us
    pallas_call x1, Pallas kernels, net_first(): pl.pallas_call(net_first_kernel, in_specs=[SMEM, VMEM, HBM, VMEM, VMEM, V...  5.41 us
    ppermute x3, starting transfers between devices, body(): lax.ppermute(sums, 'rep', [(i, (i + shift) % SIDE) for i in range(SIDE)])  5.22 us
    ppermute x3, waiting for transfers between devices, body(): lax.ppermute(sums, 'rep', [(i, (i + shift) % SIDE) for i in range(SIDE)])  3.86 us
    ppermute x4, waiting for transfers between devices, swap_core(): return lax.ppermute(value, 'set', CORE_PAIRS)  1.7 us
  transfers between devices with their start and end apart: 19, of which 12 were waited for; matrix products, arithmetic and copies ran while one was open for 3% of the time, Pallas kernels for 27%

profile of v5, /device:TPU:0, one launch (start us, length us, event | category | flops | bytes accessed | tf_op | source)
XLA Modules:
  0.0 74.9 jit_solution(1469565110437908306)
XLA Ops:
  0.8 7.4 %basis.1.refs_0_ = bf16[3,64,256]{2,1,0:T(8,128)(2,1)S(1)} custom-call(bf16[3,64,20000]{2,1,0:T(8,128)(2,1)} %scenarios_ref.1, bf16[20000,256]{1,0:T(8,128)(2,1)} %projection_ref.1), custom_call_target="tpu_custom_call" | custom-call | tf_op jit(solution)/shard_map/basis/pallas_call | solution.py:171
  8.2 2.9 %collective-permute-start.1 = (bf16[3,64,256]{2,1,0:T(8,128)(2,1)S(1)}, bf16[3,64,256]{2,1,0:T(8,128)(2,1)S(1)}, u32[]{:S(2)}, u32[]{:S(2)}) collective-permute-start(bf16[3,64,256]{2,1,0:T(8,128)(2,1)S(1)} %basis.1.refs_0_), channel_id=1, source_target_pairs={{0,6},{1,25},{2,0},{3,27},{4,2},{5,29},{6,4},{7,31},{8,14},{9,1},{... | collective-permute-start | bytes 294920 | tf_op jit(solution)/shard_map/ppermute | solution.py:43
  11.1 0.8 %collective-permute-start.2 = (bf16[3,64,256]{2,1,0:T(8,128)(2,1)S(1)}, bf16[3,64,256]{2,1,0:T(8,128)(2,1)S(1)}, u32[]{:S(2)}, u32[]{:S(2)}) collective-permute-start(bf16[3,64,256]{2,1,0:T(8,128)(2,1)S(1)} %basis.1.refs_0_), channel_id=1, source_target_pairs={{0,4},{1,17},{2,6},{3,19},{4,0},{5,21},{6,2},{7,23},{8,12},{9,25},... | collective-permute-start | bytes 294920 | tf_op jit(solution)/shard_map/ppermute | solution.py:43
  11.9 0.9 %collective-permute-start.3 = (bf16[3,64,256]{2,1,0:T(8,128)(2,1)S(1)}, bf16[3,64,256]{2,1,0:T(8,128)(2,1)}, u32[]{:S(2)}, u32[]{:S(2)}) collective-permute-start(bf16[3,64,256]{2,1,0:T(8,128)(2,1)S(1)} %basis.1.refs_0_), channel_id=1, source_target_pairs={{0,2},{1,9},{2,4},{3,11},{4,6},{5,13},{6,0},{7,15},{8,10},{9,17},{... | collective-permute-start | bytes 294920 | tf_op jit(solution)/shard_map/ppermute | solution.py:43
  14.7 0.7 broadcast_in_dim.2
  15.3 0.8 %eq.43 = s32[512]{0:T(512)S(1)} reshape(s32[64,8]{1,0:T(8,128)} %broadcast_in_dim.2) | data formatting | bytes 4096 | tf_op jit(solution)/shard_map/eq | solution.py:226
  16.3 1.0 %collective-permute-done.2.refs_2_ = bf16[3,64,256]{2,1,0:T(8,128)(2,1)S(1)} collective-permute-done((bf16[3,64,256]{2,1,0:T(8,128)(2,1)S(1)}, bf16[3,64,256]{2,1,0:T(8,128)(2,1)S(1)}, u32[]{:S(2)}, u32[]{:S(2)}) %collective-permute-start.2) | collective-permute-done | bytes 98336 | tf_op jit(solution)/shard_map/ppermute | solution.py:43
  17.3 1.1 %collective-permute-done.3.refs_3_ = bf16[3,64,256]{2,1,0:T(8,128)(2,1)} collective-permute-done((bf16[3,64,256]{2,1,0:T(8,128)(2,1)S(1)}, bf16[3,64,256]{2,1,0:T(8,128)(2,1)}, u32[]{:S(2)}, u32[]{:S(2)}) %collective-permute-start.3) | collective-permute-done | bytes 98336 | tf_op jit(solution)/shard_map/ppermute | solution.py:43
  18.4 0.9 %line.1.rows_ref = bf16[4,3,64,256]{3,2,1,0:T(8,128)(2,1)S(1)} custom-call(s32[1]{0:T(128)} %bitcast.3.first_ref, bf16[3,64,256]{2,1,0:T(8,128)(2,1)S(1)} %basis.1.refs_0_, bf16[3,64,256]{2,1,0:T(8,128)(2,1)S(1)} %collective-permute-done.1.refs_1_, bf16[3,64,256]{2,1,0:T(8,128)(2,1)S(1)} %collective-permute-done.2.refs_2_, ...), custom_call_target="tpu_custom_call" | custom-call | tf_op jit(solution)/shard_map/line/pallas_call | solution.py:193
  19.3 4.1 %collective-permute-start.8 = (bf16[4,3,64,256]{3,2,1,0:T(8,128)(2,1)S(1)}, bf16[4,3,64,256]{3,2,1,0:T(8,128)(2,1)S(1)}, u32[]{:S(2)}, u32[]{:S(2)}) collective-permute-start(bf16[4,3,64,256]{3,2,1,0:T(8,128)(2,1)S(1)} %line.1.rows_ref), channel_id=1, source_target_pairs={{0,24},{1,7},{2,26},{3,1},{4,28},{5,3},{6,30},{7,5},{8,0},{9,15},{... | collective-permute-start | bytes 1179656 | tf_op jit(solution)/shard_map/ppermute | solution.py:43
  23.4 1.3 %collective-permute-start.6 = (bf16[4,3,64,256]{3,2,1,0:T(8,128)(2,1)S(1)}, bf16[4,3,64,256]{3,2,1,0:T(8,128)(2,1)S(1)}, u32[]{:S(2)}, u32[]{:S(2)}) collective-permute-start(bf16[4,3,64,256]{3,2,1,0:T(8,128)(2,1)S(1)} %line.1.rows_ref), channel_id=1, source_target_pairs={{0,8},{1,3},{2,10},{3,5},{4,12},{5,7},{6,14},{7,1},{8,16},{9,11},{... | collective-permute-start | bytes 1179656 | tf_op jit(solution)/shard_map/ppermute | solution.py:43
  24.7 5.4 %net_first.1 = (f32[3,128,256]{2,1,0:T(8,128)S(1)}, bf16[3,2048,256]{2,1,0:T(8,128)(2,1)S(1)}) custom-call(s32[64]{0:T(128)S(1)} %get-tuple-element.88.live_ref.refs_0_, bf16[4,3,64,256]{3,2,1,0:T(8,128)(2,1)S(1)} %line.1.rows_ref, bf16[3,2048,256]{2,1,0:T(8,128)(2,1)} %bitcast.251, bf16[3,2048,256]{2,1,0:T(8,128)(2,1)S(1)} %collective-permute-done.4.other_ref.refs_3_, ...), custom_call_target="tpu_custom_call" | custom-call | tf_op jit(solution)/shard_map/net_first/pallas_call | solution.py:118
  30.2 2.8 %collective-permute-done.8.refs_1_ = bf16[4,3,64,256]{3,2,1,0:T(8,128)(2,1)S(1)} collective-permute-done((bf16[4,3,64,256]{3,2,1,0:T(8,128)(2,1)S(1)}, bf16[4,3,64,256]{3,2,1,0:T(8,128)(2,1)S(1)}, u32[]{:S(2)}, u32[]{:S(2)}) %collective-permute-start.8) | collective-permute-done | bytes 393248 | tf_op jit(solution)/shard_map/ppermute | solution.py:43
  33.0 3.4 %net_next.3 = f32[3,128,256]{2,1,0:T(8,128)S(1)} custom-call(s32[64]{0:T(128)S(1)} %get-tuple-element.88.live_ref.refs_0_, bf16[4,3,64,256]{3,2,1,0:T(8,128)(2,1)S(1)} %collective-permute-done.8.refs_1_, bf16[3,2048,256]{2,1,0:T(8,128)(2,1)S(1)} %get-tuple-element.12.refs_2_, bf16[3,2048,256]{2,1,0:T(8,128)(2,1)S(1)} %collective-permute-done.4.other_ref.refs_3_, ...), custom_call_target="tpu_custom_call" | custom-call | tf_op jit(solution)/shard_map/net_next/pallas_call | solution.py:135
  36.4 3.4 %net_next.4 = f32[3,128,256]{2,1,0:T(8,128)S(1)} custom-call(s32[64]{0:T(128)S(1)} %get-tuple-element.88.live_ref.refs_0_, bf16[4,3,64,256]{3,2,1,0:T(8,128)(2,1)S(1)} %collective-permute-done.7.refs_1_, bf16[3,2048,256]{2,1,0:T(8,128)(2,1)S(1)} %get-tuple-element.12.refs_2_, bf16[3,2048,256]{2,1,0:T(8,128)(2,1)S(1)} %collective-permute-done.4.other_ref.refs_3_, ...), custom_call_target="tpu_custom_call" | custom-call | tf_op jit(solution)/shard_map/net_next/pallas_call | solution.py:135
  39.8 3.4 %net_next.5 = f32[3,128,256]{2,1,0:T(8,128)S(1)} custom-call(s32[64]{0:T(128)S(1)} %get-tuple-element.88.live_ref.refs_0_, bf16[4,3,64,256]{3,2,1,0:T(8,128)(2,1)S(1)} %collective-permute-done.6.refs_1_, bf16[3,2048,256]{2,1,0:T(8,128)(2,1)S(1)} %get-tuple-element.12.refs_2_, bf16[3,2048,256]{2,1,0:T(8,128)(2,1)S(1)} %collective-permute-done.4.other_ref.refs_3_, ...), custom_call_target="tpu_custom_call" | custom-call | tf_op jit(solution)/shard_map/net_next/pallas_call | solution.py:135
  43.8 1.3 %collective-permute-start.11 = (f16[4,3,8,1024]{3,2,1,0:T(8,128)(2,1)S(1)}, f16[4,3,8,1024]{3,2,1,0:T(8,128)(2,1)S(1)}, u32[]{:S(2)}, u32[]{:S(2)}) collective-permute-start(f16[4,3,8,1024]{3,2,1,0:T(8,128)(2,1)S(1)} %pad_maximum_fusion.2), channel_id=1, source_target_pairs={{0,4},{1,17},{2,6},{3,19},{4,0},{5,21},{6,2},{7,23},{8,12},{9,25},... | collective-permute-start | bytes 589832 | tf_op jit(solution)/shard_map/ppermute | solution.py:43
  45.2 1.2 %collective-permute-start.10 = (f16[4,3,8,1024]{3,2,1,0:T(8,128)(2,1)S(1)}, f16[4,3,8,1024]{3,2,1,0:T(8,128)(2,1)S(1)}, u32[]{:S(2)}, u32[]{:S(2)}) collective-permute-start(f16[4,3,8,1024]{3,2,1,0:T(8,128)(2,1)S(1)} %pad_maximum_fusion.1), channel_id=1, source_target_pairs={{0,6},{1,25},{2,0},{3,27},{4,2},{5,29},{6,4},{7,31},{8,14},{9,1},{... | collective-permute-start | bytes 589832 | tf_op jit(solution)/shard_map/ppermute | solution.py:43
  46.6 1.0 %collective-permute-start.9 = (f16[4,3,8,1024]{3,2,1,0:T(8,128)(2,1)S(1)}, f16[4,3,8,1024]{3,2,1,0:T(8,128)(2,1)S(1)}, u32[]{:S(2)}, u32[]{:S(2)}) collective-permute-start(f16[4,3,8,1024]{3,2,1,0:T(8,128)(2,1)S(1)} %pad_maximum_fusion), channel_id=1, source_target_pairs={{0,2},{1,9},{2,4},{3,11},{4,6},{5,13},{6,0},{7,15},{8,10},{9,17},{... | collective-permute-start | bytes 589832 | tf_op jit(solution)/shard_map/ppermute | solution.py:43
  47.6 3.6 %collective-permute-done.11 = f16[4,3,8,1024]{3,2,1,0:T(8,128)(2,1)S(1)} collective-permute-done((f16[4,3,8,1024]{3,2,1,0:T(8,128)(2,1)S(1)}, f16[4,3,8,1024]{3,2,1,0:T(8,128)(2,1)S(1)}, u32[]{:S(2)}, u32[]{:S(2)}) %collective-permute-start.11) | collective-permute-done | bytes 196640 | tf_op jit(solution)/shard_map/ppermute | solution.py:43
  51.3 2.3 %collective-permute-done.9 = f16[4,3,8,1024]{3,2,1,0:T(8,128)(2,1)S(1)} collective-permute-done((f16[4,3,8,1024]{3,2,1,0:T(8,128)(2,1)S(1)}, f16[4,3,8,1024]{3,2,1,0:T(8,128)(2,1)S(1)}, u32[]{:S(2)}, u32[]{:S(2)}) %collective-permute-start.9) | collective-permute-done | bytes 196640 | tf_op jit(solution)/shard_map/ppermute | solution.py:43
  53.8 4.3 %collective-permute-start.13 = (f16[3,8,1024]{2,1,0:T(8,128)(2,1)S(1)}, f16[3,8,1024]{2,1,0:T(8,128)(2,1)S(1)}, u32[]{:S(2)}, u32[]{:S(2)}) collective-permute-start(f16[3,8,1024]{2,1,0:T(8,128)(2,1)S(1)} %get-tuple-element.22), channel_id=1, source_target_pairs={{0,24},{1,7},{2,26},{3,1},{4,28},{5,3},{6,30},{7,5},{8,0},{9,15},{... | collective-permute-start | bytes 147464 | tf_op jit(solution)/shard_map/ppermute | solution.py:43
  58.1 0.8 %collective-permute-start.12 = (f16[3,8,1024]{2,1,0:T(8,128)(2,1)S(1)}, f16[3,8,1024]{2,1,0:T(8,128)(2,1)S(1)}, u32[]{:S(2)}, u32[]{:S(2)}) collective-permute-start(f16[3,8,1024]{2,1,0:T(8,128)(2,1)S(1)} %get-tuple-element.20), channel_id=1, source_target_pairs={{0,8},{1,3},{2,10},{3,5},{4,12},{5,7},{6,14},{7,1},{8,16},{9,11},{... | collective-permute-start | bytes 147464 | tf_op jit(solution)/shard_map/ppermute | solution.py:43
  59.3 2.1 %collective-permute-done.13 = f16[3,8,1024]{2,1,0:T(8,128)(2,1)S(1)} collective-permute-done((f16[3,8,1024]{2,1,0:T(8,128)(2,1)S(1)}, f16[3,8,1024]{2,1,0:T(8,128)(2,1)S(1)}, u32[]{:S(2)}, u32[]{:S(2)}) %collective-permute-start.13) | collective-permute-done | bytes 49184 | tf_op jit(solution)/shard_map/ppermute | solution.py:43
  61.4 1.9 %collective-permute-done.12 = f16[3,8,1024]{2,1,0:T(8,128)(2,1)S(1)} collective-permute-done((f16[3,8,1024]{2,1,0:T(8,128)(2,1)S(1)}, f16[3,8,1024]{2,1,0:T(8,128)(2,1)S(1)}, u32[]{:S(2)}, u32[]{:S(2)}) %collective-permute-start.12) | collective-permute-done | bytes 49184 | tf_op jit(solution)/shard_map/ppermute | solution.py:43
  63.8 1.1 %collective-permute-done.15 = f32[3,4,8]{2,1,0:T(4,128)S(1)} collective-permute-done((f32[3,4,8]{2,1,0:T(4,128)S(1)}, f32[3,4,8]{2,1,0:T(4,128)S(1)}, u32[]{:S(2)}, u32[]{:S(2)}) %collective-permute-start.15) | collective-permute-done | bytes 416 | tf_op jit(solution)/shard_map/ppermute | solution.py:47
  64.9 3.2 %collective-permute-start.18 = (f32[3,4,8]{2,1,0:T(4,128)S(1)}, f32[3,4,8]{2,1,0:T(4,128)S(1)}, u32[]{:S(2)}, u32[]{:S(2)}) collective-permute-start(f32[3,4,8]{2,1,0:T(4,128)S(1)} %bitcast_add_fusion), channel_id=1, source_target_pairs={{0,64},{32,96},{64,0},{96,32},{1,65},{33,97},{65,1},{97,33},{2,66}... | collective-permute-start | bytes 1160 | tf_op jit(solution)/shard_map/ppermute | solution.py:269
  68.1 1.0 %collective-permute-start.17 = (f32[3,4,8]{2,1,0:T(4,128)S(1)}, f32[3,4,8]{2,1,0:T(4,128)S(1)}, u32[]{:S(2)}, u32[]{:S(2)}) collective-permute-start(f32[3,4,8]{2,1,0:T(4,128)S(1)} %bitcast_add_fusion), channel_id=1, source_target_pairs={{0,96},{32,0},{64,32},{96,64},{1,97},{33,1},{65,33},{97,65},{2,98}... | collective-permute-start | bytes 1160 | tf_op jit(solution)/shard_map/ppermute | solution.py:269
  69.2 1.0 %collective-permute-start.16 = (f32[3,4,8]{2,1,0:T(4,128)S(1)}, f32[3,4,8]{2,1,0:T(4,128)S(1)}, u32[]{:S(2)}, u32[]{:S(2)}) collective-permute-start(f32[3,4,8]{2,1,0:T(4,128)S(1)} %bitcast_add_fusion), channel_id=1, source_target_pairs={{0,32},{32,64},{64,96},{96,0},{1,33},{33,65},{65,97},{97,1},{2,34}... | collective-permute-start | bytes 1160 | tf_op jit(solution)/shard_map/ppermute | solution.py:269
  70.1 1.6 %collective-permute-done.17 = f32[3,4,8]{2,1,0:T(4,128)S(1)} collective-permute-done((f32[3,4,8]{2,1,0:T(4,128)S(1)}, f32[3,4,8]{2,1,0:T(4,128)S(1)}, u32[]{:S(2)}, u32[]{:S(2)}) %collective-permute-start.17) | collective-permute-done | bytes 416 | tf_op jit(solution)/shard_map/ppermute | solution.py:269
  71.7 2.3 %collective-permute-done.16 = f32[3,4,8]{2,1,0:T(4,128)S(1)} collective-permute-done((f32[3,4,8]{2,1,0:T(4,128)S(1)}, f32[3,4,8]{2,1,0:T(4,128)S(1)}, u32[]{:S(2)}, u32[]{:S(2)}) %collective-permute-start.16) | collective-permute-done | bytes 416 | tf_op jit(solution)/shard_map/ppermute | solution.py:269
  74.3 0.6 multiply_sqrt_fusion
  (86 shorter events, 4.2 us)
Async XLA Ops:
  0.6 12.2 %copy-start.2 = (s32[32]{0:T(128)S(1)}, s32[32]{0:T(128)}, u32[]{:S(2)}) copy-start(s32[32]{0:T(128)} %param.11) | copy-start | bytes 388
  0.6 12.2 %copy-start.3 = (s32[32]{0:T(128)S(1)}, s32[32]{0:T(128)}, u32[]{:S(2)}) copy-start(s32[32]{0:T(128)} %param.10) | copy-start | bytes 388
  0.7 13.6 %copy-start = (f32[3,32,64]{2,1,0:T(8,128)S(1)}, f32[3,32,64]{2,1,0:T(8,128)}, u32[]{:S(2)}) copy-start(f32[3,32,64]{2,1,0:T(8,128)} %refs_4_.5) | copy-start | bytes 73732
  0.7 24.1 %collective-permute-start.4 = (bf16[3,2048,256]{2,1,0:T(8,128)(2,1)}, bf16[3,2048,256]{2,1,0:T(8,128)(2,1)S(1)}, u32[]{:S(2)}, u32[]{:S(2)}) collective-permute-start(bf16[3,2048,256]{2,1,0:T(8,128)(2,1)} %bitcast.250), channel_id=1, source_target_pairs={{0,1},{1,0},{2,3},{3,2},{4,5},{5,4},{6,7},{7,6},{8,9},{9,8},{10,11... | collective-permute-start | bytes 9437192 | tf_op jit(solution)/shard_map/ppermute | solution.py:47
  8.2 8.1 %collective-permute-start.1 = (bf16[3,64,256]{2,1,0:T(8,128)(2,1)S(1)}, bf16[3,64,256]{2,1,0:T(8,128)(2,1)S(1)}, u32[]{:S(2)}, u32[]{:S(2)}) collective-permute-start(bf16[3,64,256]{2,1,0:T(8,128)(2,1)S(1)} %basis.1.refs_0_), channel_id=1, source_target_pairs={{0,6},{1,25},{2,0},{3,27},{4,2},{5,29},{6,4},{7,31},{8,14},{9,1},{... | collective-permute-start | bytes 294920 | tf_op jit(solution)/shard_map/ppermute | solution.py:43
  11.1 6.2 %collective-permute-start.2 = (bf16[3,64,256]{2,1,0:T(8,128)(2,1)S(1)}, bf16[3,64,256]{2,1,0:T(8,128)(2,1)S(1)}, u32[]{:S(2)}, u32[]{:S(2)}) collective-permute-start(bf16[3,64,256]{2,1,0:T(8,128)(2,1)S(1)} %basis.1.refs_0_), channel_id=1, source_target_pairs={{0,4},{1,17},{2,6},{3,19},{4,0},{5,21},{6,2},{7,23},{8,12},{9,25},... | collective-permute-start | bytes 294920 | tf_op jit(solution)/shard_map/ppermute | solution.py:43
  11.9 6.5 %collective-permute-start.3 = (bf16[3,64,256]{2,1,0:T(8,128)(2,1)S(1)}, bf16[3,64,256]{2,1,0:T(8,128)(2,1)}, u32[]{:S(2)}, u32[]{:S(2)}) collective-permute-start(bf16[3,64,256]{2,1,0:T(8,128)(2,1)S(1)} %basis.1.refs_0_), channel_id=1, source_target_pairs={{0,2},{1,9},{2,4},{3,11},{4,6},{5,13},{6,0},{7,15},{8,10},{9,17},{... | collective-permute-start | bytes 294920 | tf_op jit(solution)/shard_map/ppermute | solution.py:43
  12.8 1.4 %collective-permute-start = (s32[2,32]{1,0:T(2,128)S(1)}, s32[2,32]{1,0:T(2,128)S(1)}, u32[]{:S(2)}, u32[]{:S(2)}) collective-permute-start(s32[2,32]{1,0:T(2,128)S(1)} %pad_add_fusion), channel_id=1, source_target_pairs={{0,1},{1,0},{2,3},{3,2},{4,5},{5,4},{6,7},{7,6},{8,9},{9,8},{10,11... | collective-permute-start | bytes 776 | tf_op jit(solution)/shard_map/ppermute | solution.py:47
  14.2 10.5 %collective-permute-start.5 = (f32[3,32,64]{2,1,0:T(8,128)S(1)}, f32[3,32,64]{2,1,0:T(8,128)S(1)}, u32[]{:S(2)}, u32[]{:S(2)}) collective-permute-start(f32[3,32,64]{2,1,0:T(8,128)S(1)} %copy-done), channel_id=1, source_target_pairs={{0,1},{1,0},{2,3},{3,2},{4,5},{5,4},{6,7},{7,6},{8,9},{9,8},{10,11... | collective-permute-start | bytes 73736 | tf_op jit(solution)/shard_map/ppermute | solution.py:47
  19.3 13.6 %collective-permute-start.8 = (bf16[4,3,64,256]{3,2,1,0:T(8,128)(2,1)S(1)}, bf16[4,3,64,256]{3,2,1,0:T(8,128)(2,1)S(1)}, u32[]{:S(2)}, u32[]{:S(2)}) collective-permute-start(bf16[4,3,64,256]{3,2,1,0:T(8,128)(2,1)S(1)} %line.1.rows_ref), channel_id=1, source_target_pairs={{0,24},{1,7},{2,26},{3,1},{4,28},{5,3},{6,30},{7,5},{8,0},{9,15},{... | collective-permute-start | bytes 1179656 | tf_op jit(solution)/shard_map/ppermute | solution.py:43
  23.4 12.9 %collective-permute-start.7 = (bf16[4,3,64,256]{3,2,1,0:T(8,128)(2,1)S(1)}, bf16[4,3,64,256]{3,2,1,0:T(8,128)(2,1)S(1)}, u32[]{:S(2)}, u32[]{:S(2)}) collective-permute-start(bf16[4,3,64,256]{3,2,1,0:T(8,128)(2,1)S(1)} %line.1.rows_ref), channel_id=1, source_target_pairs={{0,16},{1,5},{2,18},{3,7},{4,20},{5,1},{6,22},{7,3},{8,24},{9,13},... | collective-permute-start | bytes 1179656 | tf_op jit(solution)/shard_map/ppermute | solution.py:43
  23.4 16.4 %collective-permute-start.6 = (bf16[4,3,64,256]{3,2,1,0:T(8,128)(2,1)S(1)}, bf16[4,3,64,256]{3,2,1,0:T(8,128)(2,1)S(1)}, u32[]{:S(2)}, u32[]{:S(2)}) collective-permute-start(bf16[4,3,64,256]{3,2,1,0:T(8,128)(2,1)S(1)} %line.1.rows_ref), channel_id=1, source_target_pairs={{0,8},{1,3},{2,10},{3,5},{4,12},{5,7},{6,14},{7,1},{8,16},{9,11},{... | collective-permute-start | bytes 1179656 | tf_op jit(solution)/shard_map/ppermute | solution.py:43
  43.8 7.5 %collective-permute-start.11 = (f16[4,3,8,1024]{3,2,1,0:T(8,128)(2,1)S(1)}, f16[4,3,8,1024]{3,2,1,0:T(8,128)(2,1)S(1)}, u32[]{:S(2)}, u32[]{:S(2)}) collective-permute-start(f16[4,3,8,1024]{3,2,1,0:T(8,128)(2,1)S(1)} %pad_maximum_fusion.2), channel_id=1, source_target_pairs={{0,4},{1,17},{2,6},{3,19},{4,0},{5,21},{6,2},{7,23},{8,12},{9,25},... | collective-permute-start | bytes 589832 | tf_op jit(solution)/shard_map/ppermute | solution.py:43
  45.2 6.0 %collective-permute-start.10 = (f16[4,3,8,1024]{3,2,1,0:T(8,128)(2,1)S(1)}, f16[4,3,8,1024]{3,2,1,0:T(8,128)(2,1)S(1)}, u32[]{:S(2)}, u32[]{:S(2)}) collective-permute-start(f16[4,3,8,1024]{3,2,1,0:T(8,128)(2,1)S(1)} %pad_maximum_fusion.1), channel_id=1, source_target_pairs={{0,6},{1,25},{2,0},{3,27},{4,2},{5,29},{6,4},{7,31},{8,14},{9,1},{... | collective-permute-start | bytes 589832 | tf_op jit(solution)/shard_map/ppermute | solution.py:43
  46.6 6.9 %collective-permute-start.9 = (f16[4,3,8,1024]{3,2,1,0:T(8,128)(2,1)S(1)}, f16[4,3,8,1024]{3,2,1,0:T(8,128)(2,1)S(1)}, u32[]{:S(2)}, u32[]{:S(2)}) collective-permute-start(f16[4,3,8,1024]{3,2,1,0:T(8,128)(2,1)S(1)} %pad_maximum_fusion), channel_id=1, source_target_pairs={{0,2},{1,9},{2,4},{3,11},{4,6},{5,13},{6,0},{7,15},{8,10},{9,17},{... | collective-permute-start | bytes 589832 | tf_op jit(solution)/shard_map/ppermute | solution.py:43
  53.7 5.7 %collective-permute-start.14 = (f16[3,8,1024]{2,1,0:T(8,128)(2,1)S(1)}, f16[3,8,1024]{2,1,0:T(8,128)(2,1)S(1)}, u32[]{:S(2)}, u32[]{:S(2)}) collective-permute-start(f16[3,8,1024]{2,1,0:T(8,128)(2,1)S(1)} %get-tuple-element.21), channel_id=1, source_target_pairs={{0,16},{1,5},{2,18},{3,7},{4,20},{5,1},{6,22},{7,3},{8,24},{9,13},... | collective-permute-start | bytes 147464 | tf_op jit(solution)/shard_map/ppermute | solution.py:43
  53.8 7.7 %collective-permute-start.13 = (f16[3,8,1024]{2,1,0:T(8,128)(2,1)S(1)}, f16[3,8,1024]{2,1,0:T(8,128)(2,1)S(1)}, u32[]{:S(2)}, u32[]{:S(2)}) collective-permute-start(f16[3,8,1024]{2,1,0:T(8,128)(2,1)S(1)} %get-tuple-element.22), channel_id=1, source_target_pairs={{0,24},{1,7},{2,26},{3,1},{4,28},{5,3},{6,30},{7,5},{8,0},{9,15},{... | collective-permute-start | bytes 147464 | tf_op jit(solution)/shard_map/ppermute | solution.py:43
  58.1 5.3 %collective-permute-start.12 = (f16[3,8,1024]{2,1,0:T(8,128)(2,1)S(1)}, f16[3,8,1024]{2,1,0:T(8,128)(2,1)S(1)}, u32[]{:S(2)}, u32[]{:S(2)}) collective-permute-start(f16[3,8,1024]{2,1,0:T(8,128)(2,1)S(1)} %get-tuple-element.20), channel_id=1, source_target_pairs={{0,8},{1,3},{2,10},{3,5},{4,12},{5,7},{6,14},{7,1},{8,16},{9,11},{... | collective-permute-start | bytes 147464 | tf_op jit(solution)/shard_map/ppermute | solution.py:43
  63.7 1.2 %collective-permute-start.15 = (f32[3,4,8]{2,1,0:T(4,128)S(1)}, f32[3,4,8]{2,1,0:T(4,128)S(1)}, u32[]{:S(2)}, u32[]{:S(2)}) collective-permute-start(f32[3,4,8]{2,1,0:T(4,128)S(1)} %dynamic-slice_bitcast_fusion), channel_id=1, source_target_pairs={{0,1},{1,0},{2,3},{3,2},{4,5},{5,4},{6,7},{7,6},{8,9},{9,8},{10,11... | collective-permute-start | bytes 1160 | tf_op jit(solution)/shard_map/ppermute | solution.py:47
  64.9 5.2 %collective-permute-start.18 = (f32[3,4,8]{2,1,0:T(4,128)S(1)}, f32[3,4,8]{2,1,0:T(4,128)S(1)}, u32[]{:S(2)}, u32[]{:S(2)}) collective-permute-start(f32[3,4,8]{2,1,0:T(4,128)S(1)} %bitcast_add_fusion), channel_id=1, source_target_pairs={{0,64},{32,96},{64,0},{96,32},{1,65},{33,97},{65,1},{97,33},{2,66}... | collective-permute-start | bytes 1160 | tf_op jit(solution)/shard_map/ppermute | solution.py:269
  68.1 3.6 %collective-permute-start.17 = (f32[3,4,8]{2,1,0:T(4,128)S(1)}, f32[3,4,8]{2,1,0:T(4,128)S(1)}, u32[]{:S(2)}, u32[]{:S(2)}) collective-permute-start(f32[3,4,8]{2,1,0:T(4,128)S(1)} %bitcast_add_fusion), channel_id=1, source_target_pairs={{0,96},{32,0},{64,32},{96,64},{1,97},{33,1},{65,33},{97,65},{2,98}... | collective-permute-start | bytes 1160 | tf_op jit(solution)/shard_map/ppermute | solution.py:269
  69.2 4.8 %collective-permute-start.16 = (f32[3,4,8]{2,1,0:T(4,128)S(1)}, f32[3,4,8]{2,1,0:T(4,128)S(1)}, u32[]{:S(2)}, u32[]{:S(2)}) collective-permute-start(f32[3,4,8]{2,1,0:T(4,128)S(1)} %bitcast_add_fusion), channel_id=1, source_target_pairs={{0,32},{32,64},{64,96},{96,0},{1,33},{33,65},{65,97},{97,1},{2,34}... | collective-permute-start | bytes 1160 | tf_op jit(solution)/shard_map/ppermute | solution.py:269
  74.1 0.8 %copy-start.1 = (f32[3,4]{1,0:T(4,128)}, f32[3,4]{1,0:T(4,128)S(1)}, u32[]{:S(2)}) copy-start(f32[3,4]{1,0:T(4,128)S(1)} %broadcast_multiply_fusion) | copy-start | bytes 148

commit v6 on v5

--- a/solution.py
+++ b/solution.py
@@ -19,6 +19,7 @@
 CHUNK = SIDE * ROWS
 OWN = 2 * SPD
 GROUP = 4
+ORDER = ((3,), (2, 1))
 F32 = jnp.float32
 BF16 = jnp.bfloat16
 
@@ -51,25 +52,19 @@
     return lax.dot_general(a, b, (dims, ((), ())), preferred_element_type=F32)
 
 
-def net_rows(
-    live_ref, rows_ref, held_ref, other_ref, my_floor_ref, other_floor_ref, hot_ref, out_ref, sums_ref,
-    copies=None,
-):
+def net_rows(live_ref, rows_ref, weights, floor_ref, hot_ref, out_ref, sums_ref, copies=None):
     trade = lax.broadcasted_iota(jnp.int32, (TB, CHUNK), 0)
     for step in range(STEPS):
         rows = rows_ref[:, step].reshape(CHUNK, BASIS)
-        for half, (weights, floors) in enumerate(
-            ((held_ref, my_floor_ref), (other_ref, other_floor_ref))
-        ):
+        for half in range(2):
             if copies and half == 0:
                 copies[step].wait()
-            floors = jnp.transpose(floors[step])
             for first in range(0, BPD, GROUP):
                 trades = slice(first * TB, (first + GROUP) * TB)
-                values = dot(weights[step, trades, :], rows, ((1,), (1,)))
+                values = dot(weights[half][step, trades, :], rows, ((1,), (1,)))
                 for block in range(GROUP):
                     spot = half * BPD + first + block
-                    floor = floors[:, first + block : first + block + 1]
+                    floor = floor_ref[step, half, :, first + block : first + block + 1]
                     value = jnp.maximum(values[block * TB : (block + 1) * TB], floor)
                     value = jnp.where(trade < live_ref[spot], value, 0.0)
                     sums = value[:8]
@@ -84,8 +79,18 @@
 
 
 def net_first_kernel(
-    live_ref, rows_ref, mine_ref, other_ref, my_floor_ref, other_floor_ref, hot_ref, out_ref, held_ref,
-    sums_ref, sems,
+    live_ref,
+    rows_ref,
+    mine_ref,
+    other_ref,
+    my_floor_ref,
+    other_floor_ref,
+    hot_ref,
+    out_ref,
+    held_ref,
+    floor_ref,
+    sums_ref,
+    sems,
 ):
     copies = [
         pltpu.make_async_copy(mine_ref.at[step], held_ref.at[step], sems.at[step])
@@ -93,14 +98,18 @@
     ]
     for copy in copies:
         copy.start()
-    net_rows(
-        live_ref, rows_ref, held_ref, other_ref, my_floor_ref, other_floor_ref, hot_ref, out_ref,
-        sums_ref, copies,
-    )
-
-
-def net_next_kernel(*refs):
-    net_rows(*refs)
+    for step in range(STEPS):
+        floor_ref[step, 0] = jnp.transpose(my_floor_ref[step])
+        floor_ref[step, 1] = jnp.transpose(other_floor_ref[step])
+    weights = (held_ref, other_ref)
+    net_rows(live_ref, rows_ref, weights, floor_ref, hot_ref, out_ref, sums_ref, copies)
+
+
+def net_next_kernel(live_ref, held_ref, other_ref, floor_ref, hot_ref, *refs):
+    count = len(refs) // 2
+    weights = (held_ref, other_ref)
+    for rows_ref, out_ref in zip(refs[:count], refs[count:-1]):
+        net_rows(live_ref, rows_ref, weights, floor_ref, hot_ref, out_ref, refs[-1])
 
 
 VMEM = pl.BlockSpec(memory_space=pltpu.VMEM)
@@ -118,8 +127,12 @@
     return pl.pallas_call(
         net_first_kernel,
         in_specs=[SMEM, VMEM, HBM, VMEM, VMEM, VMEM, VMEM],
-        out_specs=(VMEM, VMEM),
-        out_shape=(jax.ShapeDtypeStruct(TERMS, F32), pltpu.VMEM(HELD, BF16)),
+        out_specs=(VMEM, VMEM, VMEM),
+        out_shape=(
+            jax.ShapeDtypeStruct(TERMS, F32),
+            pltpu.VMEM(HELD, BF16),
+            jax.ShapeDtypeStruct((STEPS, 2, TB, BPD), F32),
+        ),
         scratch_shapes=[
             pltpu.VMEM((2 * BPD * 8, CHUNK), F32),
             pltpu.SemaphoreType.DMA((STEPS,)),
@@ -129,18 +142,18 @@
     )(live, rows, mine, other, my_floors, other_floors, hot)
 
 
-def net_next(rows, live, held, other, my_floors, other_floors, hot):
+def net_next(chunks, live, held, other, floors, hot):
     held = pltpu.with_memory_space_constraint(held, pltpu.VMEM)
     other = pltpu.with_memory_space_constraint(other, pltpu.VMEM)
     return pl.pallas_call(
         net_next_kernel,
-        in_specs=[SMEM] + [VMEM] * 6,
-        out_specs=VMEM,
-        out_shape=jax.ShapeDtypeStruct(TERMS, F32),
+        in_specs=[SMEM] + [VMEM] * (4 + len(chunks)),
+        out_specs=[VMEM] * len(chunks),
+        out_shape=[jax.ShapeDtypeStruct(TERMS, F32)] * len(chunks),
         scratch_shapes=[pltpu.VMEM((2 * BPD * 8, CHUNK), F32)],
         compiler_params=pltpu.CompilerParams(vmem_limit_bytes=12 << 20),
         name="net_next",
-    )(live, rows, held, other, my_floors, other_floors, hot)
+    )(live, held, other, floors, hot, *chunks)
 
 
 def basis_kernel(scenarios_ref, projection_ref, out_ref, sums_ref):
@@ -211,6 +224,7 @@
     line = make_line(first, [basis] + [shift_by(basis, shift, 0) for shift in (3, 2, 1)])
 
     other_weights = swap_core(weights)
+    exercise, line = lax.optimization_barrier((exercise, line))
     other_floors = swap_core(exercise)
     blocks = jnp.stack([block_set, block_live])
     blocks = jnp.concatenate([blocks, swap_core(blocks)], axis=1)
@@ -227,17 +241,23 @@
 
     arrived = {shift: shift_by(line, shift, 1) for shift in (1, 3, 2)}
     terms, sent = {}, {}
-    rows = line
-    for shift, following in ((0, 3), (3, 2), (2, 1), (1, None)):
-        fixed = (other_weights, exercise, other_floors, hot)
-        if shift == 0:
-            term, held = net_first(rows, blocks[1], weights, *fixed)
-        else:
-            term = net_next(rows, blocks[1], held, *fixed)
-        terms[shift] = term.reshape(STEPS, SIDE, SIDE, OWN, CHUNK)
-        sent[shift] = terms[shift][:, 1:].astype(jnp.float16)
-        if following:
-            rows, sent[shift] = lax.optimization_barrier((arrived[following], sent[shift]))
+
+    def keep(shifts, results):
+        for shift, term in zip(shifts, results):
+            terms[shift] = term.reshape(STEPS, SIDE, SIDE, OWN, CHUNK)
+            sent[shift] = terms[shift][:, 1:].astype(jnp.float16)
+
+    term, held, floors = net_first(
+        line, blocks[1], weights, other_weights, exercise, other_floors, hot
+    )
+    keep((0,), (term,))
+    last = 0
+    for shifts in ORDER:
+        chunks, sent[last] = lax.optimization_barrier(
+            ([arrived[shift] for shift in shifts], sent[last])
+        )
+        keep(shifts, net_next(chunks, blocks[1], held, other_weights, floors, hot))
+        last = shifts[-1]
 
     def message(values, near_step):
         return jnp.stack(

time: 75.1 us -> 74.6 us (level)
  Pallas kernels: 23.9 us -> 21.8 us
  other arithmetic: 1.94 us -> 3.2 us
  local copies, waits for them, and re-layouts: 1.89 us -> 2.67 us
    pallas_call x3 -> x2, Pallas kernels: 10.2 us -> 9.16 us  [net_next(): pl.pallas_call(net_next_kernel, in_specs=[SMEM] + [VMEM] * (4 + len(chunk...]
    pallas_call x1, Pallas kernels: 0.92 us -> 0.03 us  [make_line(): pl.pallas_call(line_kernel, in_specs=[SMEM] + [pl.BlockSpec()] * SIDE, ou...]
    unnamed x20 -> x16, local copies, waits for them, and re-layouts: 0.06 us -> 0.84 us
  transfers between devices with their start and end apart: 19 -> 19, of which waited for: 12 -> 14; matrix products, arithmetic and copies ran while one was open for 3% -> 5% of each run, Pallas kernels for 27% -> 21%
where the time goes in v6:
time: 74.6 us; the launch traced here: 74.4 us
  starting transfers between devices  24.7 us (33%)
  Pallas kernels  21.8 us (29%)
  waiting for transfers between devices  20.7 us (28%)
  other arithmetic  3.2 us (4%)
  local copies, waits for them, and re-layouts  2.67 us (4%)
  between operations  1.11 us (1%)
    ppermute x12, starting transfers between devices, shift_by(): return lax.ppermute(value, 'set', ring_pairs(shift, stage))  18.6 us
    ppermute x12, waiting for transfers between devices, shift_by(): return lax.ppermute(value, 'set', ring_pairs(shift, stage))  14.9 us
    pallas_call x2, Pallas kernels, net_next(): pl.pallas_call(net_next_kernel, in_specs=[SMEM] + [VMEM] * (4 + len(chunk...  9.16 us
    pallas_call x1, Pallas kernels, make_basis(): pl.pallas_call(basis_kernel, grid=(-(-FACTORS // FACTOR_TILE),), in_specs...  7.43 us
    ppermute x3, starting transfers between devices, body(): lax.ppermute(sums, 'rep', [(i, (i + shift) % SIDE) for i in range(SIDE)])  5.22 us
    pallas_call x1, Pallas kernels, net_first(): pl.pallas_call(net_first_kernel, in_specs=[SMEM, VMEM, HBM, VMEM, VMEM, V...  5.2 us
    ppermute x3, waiting for transfers between devices, body(): lax.ppermute(sums, 'rep', [(i, (i + shift) % SIDE) for i in range(SIDE)])  3.87 us
    ppermute x4, waiting for transfers between devices, swap_core(): return lax.ppermute(value, 'set', CORE_PAIRS)  1.91 us
  transfers between devices with their start and end apart: 19, of which 14 were waited for; matrix products, arithmetic and copies ran while one was open for 5% of the time, Pallas kernels for 21%

profile of v6, /device:TPU:0, one launch (start us, length us, event | category | flops | bytes accessed | tf_op | source)
XLA Modules:
  0.0 74.4 jit_solution(9817291371879856080)
XLA Ops:
  0.7 7.4 %basis.1.refs_0_ = bf16[3,64,256]{2,1,0:T(8,128)(2,1)S(1)} custom-call(bf16[3,64,20000]{2,1,0:T(8,128)(2,1)} %scenarios_ref.1, bf16[20000,256]{1,0:T(8,128)(2,1)} %projection_ref.1), custom_call_target="tpu_custom_call" | custom-call | tf_op jit(solution)/shard_map/basis/pallas_call | solution.py:184
  8.2 2.9 %collective-permute-start.1 = (bf16[3,64,256]{2,1,0:T(8,128)(2,1)S(1)}, bf16[3,64,256]{2,1,0:T(8,128)(2,1)S(1)}, u32[]{:S(2)}, u32[]{:S(2)}) collective-permute-start(bf16[3,64,256]{2,1,0:T(8,128)(2,1)S(1)} %basis.1.refs_0_), channel_id=1, source_target_pairs={{0,6},{1,25},{2,0},{3,27},{4,2},{5,29},{6,4},{7,31},{8,14},{9,1},{... | collective-permute-start | bytes 294920 | tf_op jit(solution)/shard_map/ppermute | solution.py:44
  11.1 0.8 %collective-permute-start.2 = (bf16[3,64,256]{2,1,0:T(8,128)(2,1)S(1)}, bf16[3,64,256]{2,1,0:T(8,128)(2,1)S(1)}, u32[]{:S(2)}, u32[]{:S(2)}) collective-permute-start(bf16[3,64,256]{2,1,0:T(8,128)(2,1)S(1)} %basis.1.refs_0_), channel_id=1, source_target_pairs={{0,4},{1,17},{2,6},{3,19},{4,0},{5,21},{6,2},{7,23},{8,12},{9,25},... | collective-permute-start | bytes 294920 | tf_op jit(solution)/shard_map/ppermute | solution.py:44
  11.9 0.9 %collective-permute-start.3 = (bf16[3,64,256]{2,1,0:T(8,128)(2,1)S(1)}, bf16[3,64,256]{2,1,0:T(8,128)(2,1)S(1)}, u32[]{:S(2)}, u32[]{:S(2)}) collective-permute-start(bf16[3,64,256]{2,1,0:T(8,128)(2,1)S(1)} %basis.1.refs_0_), channel_id=1, source_target_pairs={{0,2},{1,9},{2,4},{3,11},{4,6},{5,13},{6,0},{7,15},{8,10},{9,17},{... | collective-permute-start | bytes 294920 | tf_op jit(solution)/shard_map/ppermute | solution.py:44
  14.2 0.8 %collective-permute-done = s32[2,32]{1,0:T(2,128)} collective-permute-done((s32[2,32]{1,0:T(2,128)}, s32[2,32]{1,0:T(2,128)}, u32[]{:S(2)}, u32[]{:S(2)}) %collective-permute-start) | collective-permute-done | bytes 288 | tf_op jit(solution)/shard_map/ppermute | solution.py:48
  14.9 0.7 %pad_add_fusion.1 = s32[2,64]{1,0:T(2,128)S(1)} fusion(s32[2,32]{1,0:T(2,128)} %collective-permute-done, s32[1,32]{1,0:T(1,128)S(1)} %bitcast.256, s32[1,32]{1,0:T(1,128)} %bitcast.257), kind=kLoop, calls=%fused_computation.126 | loop fusion | flops 256 | bytes 1024 | tf_op jit(solution)/shard_map/concatenate | solution.py:230
  15.7 0.7 broadcast_in_dim.2
  16.3 0.8 %eq.43 = s32[512]{0:T(512)S(1)} reshape(s32[64,8]{1,0:T(8,128)} %broadcast_in_dim.2) | data formatting | bytes 4096 | tf_op jit(solution)/shard_map/eq | solution.py:240
  17.3 1.0 %collective-permute-done.3.refs_3_ = bf16[3,64,256]{2,1,0:T(8,128)(2,1)S(1)} collective-permute-done((bf16[3,64,256]{2,1,0:T(8,128)(2,1)S(1)}, bf16[3,64,256]{2,1,0:T(8,128)(2,1)S(1)}, u32[]{:S(2)}, u32[]{:S(2)}) %collective-permute-start.3) | collective-permute-done | bytes 98336 | tf_op jit(solution)/shard_map/ppermute | solution.py:44
  18.6 4.0 %collective-permute-start.8 = (bf16[4,3,64,256]{3,2,1,0:T(8,128)(2,1)S(1)}, bf16[4,3,64,256]{3,2,1,0:T(8,128)(2,1)S(1)}, u32[]{:S(2)}, u32[]{:S(2)}) collective-permute-start(bf16[4,3,64,256]{3,2,1,0:T(8,128)(2,1)S(1)} %line.1.rows_ref), channel_id=1, source_target_pairs={{0,24},{1,7},{2,26},{3,1},{4,28},{5,3},{6,30},{7,5},{8,0},{9,15},{... | collective-permute-start | bytes 1179656 | tf_op jit(solution)/shard_map/ppermute | solution.py:44
  22.6 1.3 %collective-permute-start.7 = (bf16[4,3,64,256]{3,2,1,0:T(8,128)(2,1)S(1)}, bf16[4,3,64,256]{3,2,1,0:T(8,128)(2,1)S(1)}, u32[]{:S(2)}, u32[]{:S(2)}) collective-permute-start(bf16[4,3,64,256]{3,2,1,0:T(8,128)(2,1)S(1)} %line.1.rows_ref), channel_id=1, source_target_pairs={{0,8},{1,3},{2,10},{3,5},{4,12},{5,7},{6,14},{7,1},{8,16},{9,11},{... | collective-permute-start | bytes 1179656 | tf_op jit(solution)/shard_map/ppermute | solution.py:44
  23.9 0.8 %copy-done = f32[3,32,64]{2,1,0:T(8,128)S(1)} copy-done((f32[3,32,64]{2,1,0:T(8,128)S(1)}, f32[3,32,64]{2,1,0:T(8,128)}, u32[]{:S(2)}) %copy-start) | copy-done | bytes 24600
  24.7 5.2 %net_first.1 = (f32[3,128,256]{2,1,0:T(8,128)S(1)}, bf16[3,2048,256]{2,1,0:T(8,128)(2,1)S(1)}, f32[3,2,64,32]{3,2,1,0:T(8,128)S(1)}) custom-call(s32[64]{0:T(128)S(1)} %get-tuple-element.98.live_ref, bf16[4,3,64,256]{3,2,1,0:T(8,128)(2,1)S(1)} %line.1.rows_ref, bf16[3,2048,256]{2,1,0:T(8,128)(2,1)} %bitcast.246, ...), custom_call_target="tpu_custom_call" | custom-call | tf_op jit(solution)/shard_map/net_first/pallas_call | solution.py:127
  30.0 2.2 %collective-permute-done.8.refs_0_ = bf16[4,3,64,256]{3,2,1,0:T(8,128)(2,1)S(1)} collective-permute-done((bf16[4,3,64,256]{3,2,1,0:T(8,128)(2,1)S(1)}, bf16[4,3,64,256]{3,2,1,0:T(8,128)(2,1)S(1)}, u32[]{:S(2)}, u32[]{:S(2)}) %collective-permute-start.8) | collective-permute-done | bytes 393248 | tf_op jit(solution)/shard_map/ppermute | solution.py:44
  32.1 3.3 %net_next.2 = f32[3,128,256]{2,1,0:T(8,128)S(1)} custom-call(s32[64]{0:T(128)S(1)} %get-tuple-element.98.live_ref, bf16[3,2048,256]{2,1,0:T(8,128)(2,1)S(1)} %get-tuple-element.17.held_ref, bf16[3,2048,256]{2,1,0:T(8,128)(2,1)S(1)} %collective-permute-done.4.other_ref, f32[3,2,64,32]{3,2,1,0:T(8,128)S(1)} %get-tuple-element.18.floor_ref, ...), custom_call_target="tpu_custom_call" | custom-call | tf_op jit(solution)/shard_map/net_next/pallas_call | solution.py:148
  35.8 5.8 %net_next.3 = (f32[3,128,256]{2,1,0:T(8,128)S(1)}, f32[3,128,256]{2,1,0:T(8,128)S(1)}) custom-call(s32[64]{0:T(128)S(1)} %get-tuple-element.98.live_ref, bf16[3,2048,256]{2,1,0:T(8,128)(2,1)S(1)} %get-tuple-element.17.held_ref, bf16[3,2048,256]{2,1,0:T(8,128)(2,1)S(1)} %collective-permute-done.4.other_ref, f32[3,2,64,32]{3,2,1,0:T(8,128)S(1)} %get-tuple-element.18.floor_ref, ...), custom_call_target="tpu_custom_call" | custom-call | tf_op jit(solution)/shard_map/net_next/pallas_call | solution.py:148
  42.2 1.3 %collective-permute-start.11 = (f16[4,3,8,1024]{3,2,1,0:T(8,128)(2,1)S(1)}, f16[4,3,8,1024]{3,2,1,0:T(8,128)(2,1)S(1)}, u32[]{:S(2)}, u32[]{:S(2)}) collective-permute-start(f16[4,3,8,1024]{3,2,1,0:T(8,128)(2,1)S(1)} %pad_maximum_fusion.2), channel_id=1, source_target_pairs={{0,4},{1,17},{2,6},{3,19},{4,0},{5,21},{6,2},{7,23},{8,12},{9,25},... | collective-permute-start | bytes 589832 | tf_op jit(solution)/shard_map/ppermute | solution.py:44
  43.8 2.7 %collective-permute-start.10 = (f16[4,3,8,1024]{3,2,1,0:T(8,128)(2,1)S(1)}, f16[4,3,8,1024]{3,2,1,0:T(8,128)(2,1)S(1)}, u32[]{:S(2)}, u32[]{:S(2)}) collective-permute-start(f16[4,3,8,1024]{3,2,1,0:T(8,128)(2,1)S(1)} %pad_maximum_fusion.1), channel_id=1, source_target_pairs={{0,6},{1,25},{2,0},{3,27},{4,2},{5,29},{6,4},{7,31},{8,14},{9,1},{... | collective-permute-start | bytes 589832 | tf_op jit(solution)/shard_map/ppermute | solution.py:44
  46.8 2.7 %collective-permute-done.11 = f16[4,3,8,1024]{3,2,1,0:T(8,128)(2,1)S(1)} collective-permute-done((f16[4,3,8,1024]{3,2,1,0:T(8,128)(2,1)S(1)}, f16[4,3,8,1024]{3,2,1,0:T(8,128)(2,1)S(1)}, u32[]{:S(2)}, u32[]{:S(2)}) %collective-permute-start.11) | collective-permute-done | bytes 196640 | tf_op jit(solution)/shard_map/ppermute | solution.py:44
  49.5 1.0 %collective-permute-done.10 = f16[4,3,8,1024]{3,2,1,0:T(8,128)(2,1)S(1)} collective-permute-done((f16[4,3,8,1024]{3,2,1,0:T(8,128)(2,1)S(1)}, f16[4,3,8,1024]{3,2,1,0:T(8,128)(2,1)S(1)}, u32[]{:S(2)}, u32[]{:S(2)}) %collective-permute-start.10) | collective-permute-done | bytes 196640 | tf_op jit(solution)/shard_map/ppermute | solution.py:44
  50.5 3.1 %collective-permute-done.9 = f16[4,3,8,1024]{3,2,1,0:T(8,128)(2,1)S(1)} collective-permute-done((f16[4,3,8,1024]{3,2,1,0:T(8,128)(2,1)S(1)}, f16[4,3,8,1024]{3,2,1,0:T(8,128)(2,1)S(1)}, u32[]{:S(2)}, u32[]{:S(2)}) %collective-permute-start.9) | collective-permute-done | bytes 196640 | tf_op jit(solution)/shard_map/ppermute | solution.py:44
  54.1 3.5 %collective-permute-start.13 = (f16[3,8,1024]{2,1,0:T(8,128)(2,1)S(1)}, f16[3,8,1024]{2,1,0:T(8,128)(2,1)S(1)}, u32[]{:S(2)}, u32[]{:S(2)}) collective-permute-start(f16[3,8,1024]{2,1,0:T(8,128)(2,1)S(1)} %get-tuple-element.30), channel_id=1, source_target_pairs={{0,24},{1,7},{2,26},{3,1},{4,28},{5,3},{6,30},{7,5},{8,0},{9,15},{... | collective-permute-start | bytes 147464 | tf_op jit(solution)/shard_map/ppermute | solution.py:44
  57.6 0.8 %collective-permute-start.12 = (f16[3,8,1024]{2,1,0:T(8,128)(2,1)S(1)}, f16[3,8,1024]{2,1,0:T(8,128)(2,1)S(1)}, u32[]{:S(2)}, u32[]{:S(2)}) collective-permute-start(f16[3,8,1024]{2,1,0:T(8,128)(2,1)S(1)} %get-tuple-element.28), channel_id=1, source_target_pairs={{0,8},{1,3},{2,10},{3,5},{4,12},{5,7},{6,14},{7,1},{8,16},{9,11},{... | collective-permute-start | bytes 147464 | tf_op jit(solution)/shard_map/ppermute | solution.py:44
  58.4 1.0 %collective-permute-done.14 = f16[3,8,1024]{2,1,0:T(8,128)(2,1)S(1)} collective-permute-done((f16[3,8,1024]{2,1,0:T(8,128)(2,1)S(1)}, f16[3,8,1024]{2,1,0:T(8,128)(2,1)S(1)}, u32[]{:S(2)}, u32[]{:S(2)}) %collective-permute-start.14) | collective-permute-done | bytes 49184 | tf_op jit(solution)/shard_map/ppermute | solution.py:44
  59.4 1.5 %collective-permute-done.13 = f16[3,8,1024]{2,1,0:T(8,128)(2,1)S(1)} collective-permute-done((f16[3,8,1024]{2,1,0:T(8,128)(2,1)S(1)}, f16[3,8,1024]{2,1,0:T(8,128)(2,1)S(1)}, u32[]{:S(2)}, u32[]{:S(2)}) %collective-permute-start.13) | collective-permute-done | bytes 49184 | tf_op jit(solution)/shard_map/ppermute | solution.py:44
  60.9 1.9 %collective-permute-done.12 = f16[3,8,1024]{2,1,0:T(8,128)(2,1)S(1)} collective-permute-done((f16[3,8,1024]{2,1,0:T(8,128)(2,1)S(1)}, f16[3,8,1024]{2,1,0:T(8,128)(2,1)S(1)}, u32[]{:S(2)}, u32[]{:S(2)}) %collective-permute-start.12) | collective-permute-done | bytes 49184 | tf_op jit(solution)/shard_map/ppermute | solution.py:44
  63.3 1.1 %collective-permute-done.15 = f32[3,4,8]{2,1,0:T(4,128)S(1)} collective-permute-done((f32[3,4,8]{2,1,0:T(4,128)S(1)}, f32[3,4,8]{2,1,0:T(4,128)S(1)}, u32[]{:S(2)}, u32[]{:S(2)}) %collective-permute-start.15) | collective-permute-done | bytes 416 | tf_op jit(solution)/shard_map/ppermute | solution.py:48
  64.4 3.2 %collective-permute-start.18 = (f32[3,4,8]{2,1,0:T(4,128)S(1)}, f32[3,4,8]{2,1,0:T(4,128)S(1)}, u32[]{:S(2)}, u32[]{:S(2)}) collective-permute-start(f32[3,4,8]{2,1,0:T(4,128)S(1)} %bitcast_add_fusion), channel_id=1, source_target_pairs={{0,64},{32,96},{64,0},{96,32},{1,65},{33,97},{65,1},{97,33},{2,66}... | collective-permute-start | bytes 1160 | tf_op jit(solution)/shard_map/ppermute | solution.py:289
  67.6 1.1 %collective-permute-start.17 = (f32[3,4,8]{2,1,0:T(4,128)S(1)}, f32[3,4,8]{2,1,0:T(4,128)S(1)}, u32[]{:S(2)}, u32[]{:S(2)}) collective-permute-start(f32[3,4,8]{2,1,0:T(4,128)S(1)} %bitcast_add_fusion), channel_id=1, source_target_pairs={{0,96},{32,0},{64,32},{96,64},{1,97},{33,1},{65,33},{97,65},{2,98}... | collective-permute-start | bytes 1160 | tf_op jit(solution)/shard_map/ppermute | solution.py:289
  68.7 1.0 %collective-permute-start.16 = (f32[3,4,8]{2,1,0:T(4,128)S(1)}, f32[3,4,8]{2,1,0:T(4,128)S(1)}, u32[]{:S(2)}, u32[]{:S(2)}) collective-permute-start(f32[3,4,8]{2,1,0:T(4,128)S(1)} %bitcast_add_fusion), channel_id=1, source_target_pairs={{0,32},{32,64},{64,96},{96,0},{1,33},{33,65},{65,97},{97,1},{2,34}... | collective-permute-start | bytes 1160 | tf_op jit(solution)/shard_map/ppermute | solution.py:289
  69.7 1.6 %collective-permute-done.17 = f32[3,4,8]{2,1,0:T(4,128)S(1)} collective-permute-done((f32[3,4,8]{2,1,0:T(4,128)S(1)}, f32[3,4,8]{2,1,0:T(4,128)S(1)}, u32[]{:S(2)}, u32[]{:S(2)}) %collective-permute-start.17) | collective-permute-done | bytes 416 | tf_op jit(solution)/shard_map/ppermute | solution.py:289
  71.3 2.3 %collective-permute-done.16 = f32[3,4,8]{2,1,0:T(4,128)S(1)} collective-permute-done((f32[3,4,8]{2,1,0:T(4,128)S(1)}, f32[3,4,8]{2,1,0:T(4,128)S(1)}, u32[]{:S(2)}, u32[]{:S(2)}) %collective-permute-start.16) | collective-permute-done | bytes 416 | tf_op jit(solution)/shard_map/ppermute | solution.py:289
  (81 shorter events, 4.8 us)
Async XLA Ops:
  0.6 12.2 %copy-start.2 = (s32[32]{0:T(128)S(1)}, s32[32]{0:T(128)}, u32[]{:S(2)}) copy-start(s32[32]{0:T(128)} %param.11) | copy-start | bytes 388
  0.6 12.2 %copy-start.3 = (s32[32]{0:T(128)S(1)}, s32[32]{0:T(128)}, u32[]{:S(2)}) copy-start(s32[32]{0:T(128)} %param.10) | copy-start | bytes 388
  0.7 23.2 %collective-permute-start.4 = (bf16[3,2048,256]{2,1,0:T(8,128)(2,1)}, bf16[3,2048,256]{2,1,0:T(8,128)(2,1)S(1)}, u32[]{:S(2)}, u32[]{:S(2)}) collective-permute-start(bf16[3,2048,256]{2,1,0:T(8,128)(2,1)} %bitcast.245), channel_id=1, source_target_pairs={{0,1},{1,0},{2,3},{3,2},{4,5},{5,4},{6,7},{7,6},{8,9},{9,8},{10,11... | collective-permute-start | bytes 9437192 | tf_op jit(solution)/shard_map/ppermute | solution.py:48
  8.2 9.0 %collective-permute-start.1 = (bf16[3,64,256]{2,1,0:T(8,128)(2,1)S(1)}, bf16[3,64,256]{2,1,0:T(8,128)(2,1)S(1)}, u32[]{:S(2)}, u32[]{:S(2)}) collective-permute-start(bf16[3,64,256]{2,1,0:T(8,128)(2,1)S(1)} %basis.1.refs_0_), channel_id=1, source_target_pairs={{0,6},{1,25},{2,0},{3,27},{4,2},{5,29},{6,4},{7,31},{8,14},{9,1},{... | collective-permute-start | bytes 294920 | tf_op jit(solution)/shard_map/ppermute | solution.py:44
  11.1 6.2 %collective-permute-start.2 = (bf16[3,64,256]{2,1,0:T(8,128)(2,1)S(1)}, bf16[3,64,256]{2,1,0:T(8,128)(2,1)S(1)}, u32[]{:S(2)}, u32[]{:S(2)}) collective-permute-start(bf16[3,64,256]{2,1,0:T(8,128)(2,1)S(1)} %basis.1.refs_0_), channel_id=1, source_target_pairs={{0,4},{1,17},{2,6},{3,19},{4,0},{5,21},{6,2},{7,23},{8,12},{9,25},... | collective-permute-start | bytes 294920 | tf_op jit(solution)/shard_map/ppermute | solution.py:44
  11.9 6.4 %collective-permute-start.3 = (bf16[3,64,256]{2,1,0:T(8,128)(2,1)S(1)}, bf16[3,64,256]{2,1,0:T(8,128)(2,1)S(1)}, u32[]{:S(2)}, u32[]{:S(2)}) collective-permute-start(bf16[3,64,256]{2,1,0:T(8,128)(2,1)S(1)} %basis.1.refs_0_), channel_id=1, source_target_pairs={{0,2},{1,9},{2,4},{3,11},{4,6},{5,13},{6,0},{7,15},{8,10},{9,17},{... | collective-permute-start | bytes 294920 | tf_op jit(solution)/shard_map/ppermute | solution.py:44
  13.4 1.5 %collective-permute-start = (s32[2,32]{1,0:T(2,128)}, s32[2,32]{1,0:T(2,128)}, u32[]{:S(2)}, u32[]{:S(2)}) collective-permute-start(s32[2,32]{1,0:T(2,128)} %pad_add_fusion), channel_id=1, source_target_pairs={{0,1},{1,0},{2,3},{3,2},{4,5},{5,4},{6,7},{7,6},{8,9},{9,8},{10,11... | collective-permute-start | bytes 776 | tf_op jit(solution)/shard_map/ppermute | solution.py:48
  18.3 5.6 %collective-permute-start.5 = (f32[3,32,64]{2,1,0:T(8,128)}, f32[3,32,64]{2,1,0:T(8,128)S(1)}, u32[]{:S(2)}, u32[]{:S(2)}) collective-permute-start(f32[3,32,64]{2,1,0:T(8,128)} %my_floor_ref), channel_id=1, source_target_pairs={{0,1},{1,0},{2,3},{3,2},{4,5},{5,4},{6,7},{7,6},{8,9},{9,8},{10,11... | collective-permute-start | bytes 73736 | tf_op jit(solution)/shard_map/ppermute | solution.py:48
  18.6 13.5 %collective-permute-start.8 = (bf16[4,3,64,256]{3,2,1,0:T(8,128)(2,1)S(1)}, bf16[4,3,64,256]{3,2,1,0:T(8,128)(2,1)S(1)}, u32[]{:S(2)}, u32[]{:S(2)}) collective-permute-start(bf16[4,3,64,256]{3,2,1,0:T(8,128)(2,1)S(1)} %line.1.rows_ref), channel_id=1, source_target_pairs={{0,24},{1,7},{2,26},{3,1},{4,28},{5,3},{6,30},{7,5},{8,0},{9,15},{... | collective-permute-start | bytes 1179656 | tf_op jit(solution)/shard_map/ppermute | solution.py:44
  22.6 12.9 %collective-permute-start.6 = (bf16[4,3,64,256]{3,2,1,0:T(8,128)(2,1)S(1)}, bf16[4,3,64,256]{3,2,1,0:T(8,128)(2,1)S(1)}, u32[]{:S(2)}, u32[]{:S(2)}) collective-permute-start(bf16[4,3,64,256]{3,2,1,0:T(8,128)(2,1)S(1)} %line.1.rows_ref), channel_id=1, source_target_pairs={{0,16},{1,5},{2,18},{3,7},{4,20},{5,1},{6,22},{7,3},{8,24},{9,13},... | collective-permute-start | bytes 1179656 | tf_op jit(solution)/shard_map/ppermute | solution.py:44
  22.6 13.2 %collective-permute-start.7 = (bf16[4,3,64,256]{3,2,1,0:T(8,128)(2,1)S(1)}, bf16[4,3,64,256]{3,2,1,0:T(8,128)(2,1)S(1)}, u32[]{:S(2)}, u32[]{:S(2)}) collective-permute-start(bf16[4,3,64,256]{3,2,1,0:T(8,128)(2,1)S(1)} %line.1.rows_ref), channel_id=1, source_target_pairs={{0,8},{1,3},{2,10},{3,5},{4,12},{5,7},{6,14},{7,1},{8,16},{9,11},{... | collective-permute-start | bytes 1179656 | tf_op jit(solution)/shard_map/ppermute | solution.py:44
  23.9 0.8 %copy-start = (f32[3,32,64]{2,1,0:T(8,128)S(1)}, f32[3,32,64]{2,1,0:T(8,128)}, u32[]{:S(2)}) copy-start(f32[3,32,64]{2,1,0:T(8,128)} %my_floor_ref) | copy-start | bytes 73732
  42.2 7.3 %collective-permute-start.11 = (f16[4,3,8,1024]{3,2,1,0:T(8,128)(2,1)S(1)}, f16[4,3,8,1024]{3,2,1,0:T(8,128)(2,1)S(1)}, u32[]{:S(2)}, u32[]{:S(2)}) collective-permute-start(f16[4,3,8,1024]{3,2,1,0:T(8,128)(2,1)S(1)} %pad_maximum_fusion.2), channel_id=1, source_target_pairs={{0,4},{1,17},{2,6},{3,19},{4,0},{5,21},{6,2},{7,23},{8,12},{9,25},... | collective-permute-start | bytes 589832 | tf_op jit(solution)/shard_map/ppermute | solution.py:44
  43.8 6.7 %collective-permute-start.10 = (f16[4,3,8,1024]{3,2,1,0:T(8,128)(2,1)S(1)}, f16[4,3,8,1024]{3,2,1,0:T(8,128)(2,1)S(1)}, u32[]{:S(2)}, u32[]{:S(2)}) collective-permute-start(f16[4,3,8,1024]{3,2,1,0:T(8,128)(2,1)S(1)} %pad_maximum_fusion.1), channel_id=1, source_target_pairs={{0,6},{1,25},{2,0},{3,27},{4,2},{5,29},{6,4},{7,31},{8,14},{9,1},{... | collective-permute-start | bytes 589832 | tf_op jit(solution)/shard_map/ppermute | solution.py:44
  46.6 6.9 %collective-permute-start.9 = (f16[4,3,8,1024]{3,2,1,0:T(8,128)(2,1)S(1)}, f16[4,3,8,1024]{3,2,1,0:T(8,128)(2,1)S(1)}, u32[]{:S(2)}, u32[]{:S(2)}) collective-permute-start(f16[4,3,8,1024]{3,2,1,0:T(8,128)(2,1)S(1)} %pad_maximum_fusion), channel_id=1, source_target_pairs={{0,2},{1,9},{2,4},{3,11},{4,6},{5,13},{6,0},{7,15},{8,10},{9,17},{... | collective-permute-start | bytes 589832 | tf_op jit(solution)/shard_map/ppermute | solution.py:44
  53.7 5.7 %collective-permute-start.14 = (f16[3,8,1024]{2,1,0:T(8,128)(2,1)S(1)}, f16[3,8,1024]{2,1,0:T(8,128)(2,1)S(1)}, u32[]{:S(2)}, u32[]{:S(2)}) collective-permute-start(f16[3,8,1024]{2,1,0:T(8,128)(2,1)S(1)} %get-tuple-element.29), channel_id=1, source_target_pairs={{0,16},{1,5},{2,18},{3,7},{4,20},{5,1},{6,22},{7,3},{8,24},{9,13},... | collective-permute-start | bytes 147464 | tf_op jit(solution)/shard_map/ppermute | solution.py:44
  54.1 6.8 %collective-permute-start.13 = (f16[3,8,1024]{2,1,0:T(8,128)(2,1)S(1)}, f16[3,8,1024]{2,1,0:T(8,128)(2,1)S(1)}, u32[]{:S(2)}, u32[]{:S(2)}) collective-permute-start(f16[3,8,1024]{2,1,0:T(8,128)(2,1)S(1)} %get-tuple-element.30), channel_id=1, source_target_pairs={{0,24},{1,7},{2,26},{3,1},{4,28},{5,3},{6,30},{7,5},{8,0},{9,15},{... | collective-permute-start | bytes 147464 | tf_op jit(solution)/shard_map/ppermute | solution.py:44
  57.6 5.3 %collective-permute-start.12 = (f16[3,8,1024]{2,1,0:T(8,128)(2,1)S(1)}, f16[3,8,1024]{2,1,0:T(8,128)(2,1)S(1)}, u32[]{:S(2)}, u32[]{:S(2)}) collective-permute-start(f16[3,8,1024]{2,1,0:T(8,128)(2,1)S(1)} %get-tuple-element.28), channel_id=1, source_target_pairs={{0,8},{1,3},{2,10},{3,5},{4,12},{5,7},{6,14},{7,1},{8,16},{9,11},{... | collective-permute-start | bytes 147464 | tf_op jit(solution)/shard_map/ppermute | solution.py:44
  63.2 1.2 %collective-permute-start.15 = (f32[3,4,8]{2,1,0:T(4,128)S(1)}, f32[3,4,8]{2,1,0:T(4,128)S(1)}, u32[]{:S(2)}, u32[]{:S(2)}) collective-permute-start(f32[3,4,8]{2,1,0:T(4,128)S(1)} %dynamic-slice_bitcast_fusion), channel_id=1, source_target_pairs={{0,1},{1,0},{2,3},{3,2},{4,5},{5,4},{6,7},{7,6},{8,9},{9,8},{10,11... | collective-permute-start | bytes 1160 | tf_op jit(solution)/shard_map/ppermute | solution.py:48
  64.4 5.2 %collective-permute-start.18 = (f32[3,4,8]{2,1,0:T(4,128)S(1)}, f32[3,4,8]{2,1,0:T(4,128)S(1)}, u32[]{:S(2)}, u32[]{:S(2)}) collective-permute-start(f32[3,4,8]{2,1,0:T(4,128)S(1)} %bitcast_add_fusion), channel_id=1, source_target_pairs={{0,64},{32,96},{64,0},{96,32},{1,65},{33,97},{65,1},{97,33},{2,66}... | collective-permute-start | bytes 1160 | tf_op jit(solution)/shard_map/ppermute | solution.py:289
  67.6 3.6 %collective-permute-start.17 = (f32[3,4,8]{2,1,0:T(4,128)S(1)}, f32[3,4,8]{2,1,0:T(4,128)S(1)}, u32[]{:S(2)}, u32[]{:S(2)}) collective-permute-start(f32[3,4,8]{2,1,0:T(4,128)S(1)} %bitcast_add_fusion), channel_id=1, source_target_pairs={{0,96},{32,0},{64,32},{96,64},{1,97},{33,1},{65,33},{97,65},{2,98}... | collective-permute-start | bytes 1160 | tf_op jit(solution)/shard_map/ppermute | solution.py:289
  68.7 4.8 %collective-permute-start.16 = (f32[3,4,8]{2,1,0:T(4,128)S(1)}, f32[3,4,8]{2,1,0:T(4,128)S(1)}, u32[]{:S(2)}, u32[]{:S(2)}) collective-permute-start(f32[3,4,8]{2,1,0:T(4,128)S(1)} %bitcast_add_fusion), channel_id=1, source_target_pairs={{0,32},{32,64},{64,96},{96,0},{1,33},{33,65},{65,97},{97,1},{2,34}... | collective-permute-start | bytes 1160 | tf_op jit(solution)/shard_map/ppermute | solution.py:289
  73.6 0.8 %copy-start.1 = (f32[3,4]{1,0:T(4,128)}, f32[3,4]{1,0:T(4,128)S(1)}, u32[]{:S(2)}) copy-start(f32[3,4]{1,0:T(4,128)S(1)} %broadcast_multiply_fusion) | copy-start | bytes 148

commit v7 on v6

--- a/solution.py
+++ b/solution.py
@@ -90,16 +90,20 @@
     held_ref,
     floor_ref,
     sums_ref,
+    stage_ref,
     sems,
 ):
+    floor_copy = pltpu.make_async_copy(my_floor_ref, stage_ref, sems.at[STEPS])
+    floor_copy.start()
     copies = [
         pltpu.make_async_copy(mine_ref.at[step], held_ref.at[step], sems.at[step])
         for step in range(STEPS)
     ]
     for copy in copies:
         copy.start()
+    floor_copy.wait()
     for step in range(STEPS):
-        floor_ref[step, 0] = jnp.transpose(my_floor_ref[step])
+        floor_ref[step, 0] = jnp.transpose(stage_ref[step])
         floor_ref[step, 1] = jnp.transpose(other_floor_ref[step])
     weights = (held_ref, other_ref)
     net_rows(live_ref, rows_ref, weights, floor_ref, hot_ref, out_ref, sums_ref, copies)
@@ -123,10 +127,11 @@
 
 def net_first(rows, live, mine, other, my_floors, other_floors, hot):
     mine = pltpu.with_memory_space_constraint(mine, pltpu.HBM)
+    my_floors = pltpu.with_memory_space_constraint(my_floors, pltpu.HBM)
     other = pltpu.with_memory_space_constraint(other, pltpu.VMEM)
     return pl.pallas_call(
         net_first_kernel,
-        in_specs=[SMEM, VMEM, HBM, VMEM, VMEM, VMEM, VMEM],
+        in_specs=[SMEM, VMEM, HBM, VMEM, HBM, VMEM, VMEM],
         out_specs=(VMEM, VMEM, VMEM),
         out_shape=(
             jax.ShapeDtypeStruct(TERMS, F32),
@@ -135,7 +140,8 @@
         ),
         scratch_shapes=[
             pltpu.VMEM((2 * BPD * 8, CHUNK), F32),
-            pltpu.SemaphoreType.DMA((STEPS,)),
+            pltpu.VMEM((STEPS, BPD, TB), F32),
+            pltpu.SemaphoreType.DMA((STEPS + 1,)),
         ],
         compiler_params=pltpu.CompilerParams(vmem_limit_bytes=12 << 20),
         name="net_first",
@@ -224,8 +230,8 @@
     line = make_line(first, [basis] + [shift_by(basis, shift, 0) for shift in (3, 2, 1)])
 
     other_weights = swap_core(weights)
-    exercise, line = lax.optimization_barrier((exercise, line))
-    other_floors = swap_core(exercise)
+    sent_floors, line = lax.optimization_barrier((exercise, line))
+    other_floors = swap_core(sent_floors)
     blocks = jnp.stack([block_set, block_live])
     blocks = jnp.concatenate([blocks, swap_core(blocks)], axis=1)
 
@@ -271,10 +277,10 @@
         )
 
     held = message(terms, 0)
-    for shift in (1, 3, 2):
+    for shift in (2, 3, 1):
         held = held + shift_by(message(sent, shift - 1), shift, 0).astype(F32)
     netted = held[0]
-    for shift in (1, 3, 2):
+    for shift in (2, 3, 1):
         half = (held[shift] * 0.5).astype(jnp.float16)
         netted = netted + shift_by(half, shift, 1).astype(F32) * 2.0
 
@@ -285,7 +291,7 @@
     given = lax.dynamic_index_in_dim(sums, 1 - core, 1, keepdims=False)
     sums = kept + swap_core(given)
     total = sums
-    for shift in (1, 3, 2):
+    for shift in (2, 3, 1):
         total = total + lax.ppermute(
             sums, "rep", [(i, (i + shift) % SIDE) for i in range(SIDE)]
         )

time: 74.6 us -> 73.8 us (0.989)
  local copies, waits for them, and re-layouts: 2.67 us -> 1.88 us
    unnamed x16 -> x14, local copies, waits for them, and re-layouts: 0.84 us -> 0.04 us
  transfers between devices with their start and end apart: 19 -> 19, of which waited for: 14 -> 11; matrix products, arithmetic and copies ran while one was open for 5% -> 5% of each run, Pallas kernels for 21% -> 22%
where the time goes in v7:
time: 73.8 us; the launch traced here: 73.6 us
  starting transfers between devices  24.7 us (33%)
  Pallas kernels  21.9 us (30%)
  waiting for transfers between devices  20.7 us (28%)
  other arithmetic  3.18 us (4%)
  local copies, waits for them, and re-layouts  1.88 us (3%)
  between operations  1.1 us (1%)
    ppermute x12, starting transfers between devices, shift_by(): return lax.ppermute(value, 'set', ring_pairs(shift, stage))  18.6 us
    ppermute x12, waiting for transfers between devices, shift_by(): return lax.ppermute(value, 'set', ring_pairs(shift, stage))  15.5 us
    pallas_call x2, Pallas kernels, net_next(): pl.pallas_call(net_next_kernel, in_specs=[SMEM] + [VMEM] * (4 + len(chunk...  9.16 us
    pallas_call x1, Pallas kernels, make_basis(): pl.pallas_call(basis_kernel, grid=(-(-FACTORS // FACTOR_TILE),), in_specs...  7.43 us
    pallas_call x1, Pallas kernels, net_first(): pl.pallas_call(net_first_kernel, in_specs=[SMEM, VMEM, HBM, VMEM, HBM, VM...  5.23 us
    ppermute x3, starting transfers between devices, body(): lax.ppermute(sums, 'rep', [(i, (i + shift) % SIDE) for i in range(SIDE)])  5.21 us
    ppermute x3, waiting for transfers between devices, body(): lax.ppermute(sums, 'rep', [(i, (i + shift) % SIDE) for i in range(SIDE)])  3.15 us
    ppermute x4, waiting for transfers between devices, swap_core(): return lax.ppermute(value, 'set', CORE_PAIRS)  2.04 us
  transfers between devices with their start and end apart: 19, of which 11 were waited for; matrix products, arithmetic and copies ran while one was open for 5% of the time, Pallas kernels for 22%

profile of v7, /device:TPU:0, one launch (start us, length us, event | category | flops | bytes accessed | tf_op | source)
XLA Modules:
  0.0 73.6 jit_solution(4800245052933250723)
XLA Ops:
  0.7 7.4 %basis.1.refs_0_ = bf16[3,64,256]{2,1,0:T(8,128)(2,1)S(1)} custom-call(bf16[3,64,20000]{2,1,0:T(8,128)(2,1)} %scenarios_ref.1, bf16[20000,256]{1,0:T(8,128)(2,1)} %projection_ref.1), custom_call_target="tpu_custom_call" | custom-call | tf_op jit(solution)/shard_map/basis/pallas_call | solution.py:190
  8.2 2.9 %collective-permute-start.1 = (bf16[3,64,256]{2,1,0:T(8,128)(2,1)S(1)}, bf16[3,64,256]{2,1,0:T(8,128)(2,1)S(1)}, u32[]{:S(2)}, u32[]{:S(2)}) collective-permute-start(bf16[3,64,256]{2,1,0:T(8,128)(2,1)S(1)} %basis.1.refs_0_), channel_id=1, source_target_pairs={{0,6},{1,25},{2,0},{3,27},{4,2},{5,29},{6,4},{7,31},{8,14},{9,1},{... | collective-permute-start | bytes 294920 | tf_op jit(solution)/shard_map/ppermute | solution.py:44
  11.1 0.8 %collective-permute-start.2 = (bf16[3,64,256]{2,1,0:T(8,128)(2,1)S(1)}, bf16[3,64,256]{2,1,0:T(8,128)(2,1)S(1)}, u32[]{:S(2)}, u32[]{:S(2)}) collective-permute-start(bf16[3,64,256]{2,1,0:T(8,128)(2,1)S(1)} %basis.1.refs_0_), channel_id=1, source_target_pairs={{0,4},{1,17},{2,6},{3,19},{4,0},{5,21},{6,2},{7,23},{8,12},{9,25},... | collective-permute-start | bytes 294920 | tf_op jit(solution)/shard_map/ppermute | solution.py:44
  11.9 0.9 %collective-permute-start.3 = (bf16[3,64,256]{2,1,0:T(8,128)(2,1)S(1)}, bf16[3,64,256]{2,1,0:T(8,128)(2,1)S(1)}, u32[]{:S(2)}, u32[]{:S(2)}) collective-permute-start(bf16[3,64,256]{2,1,0:T(8,128)(2,1)S(1)} %basis.1.refs_0_), channel_id=1, source_target_pairs={{0,2},{1,9},{2,4},{3,11},{4,6},{5,13},{6,0},{7,15},{8,10},{9,17},{... | collective-permute-start | bytes 294920 | tf_op jit(solution)/shard_map/ppermute | solution.py:44
  12.8 0.6 pad_add_fusion
  13.4 0.5 collective-permute-start
  14.2 0.9 %collective-permute-done = s32[2,32]{1,0:T(2,128)} collective-permute-done((s32[2,32]{1,0:T(2,128)}, s32[2,32]{1,0:T(2,128)}, u32[]{:S(2)}, u32[]{:S(2)}) %collective-permute-start) | collective-permute-done | bytes 288 | tf_op jit(solution)/shard_map/ppermute | solution.py:48
  15.0 0.7 pad_add_fusion.1
  15.8 0.7 broadcast_in_dim.2
  16.5 0.8 %eq.43 = s32[512]{0:T(512)S(1)} reshape(s32[64,8]{1,0:T(8,128)} %broadcast_in_dim.2) | data formatting | bytes 4096 | tf_op jit(solution)/shard_map/eq | solution.py:246
  17.3 1.0 %collective-permute-done.3.refs_3_ = bf16[3,64,256]{2,1,0:T(8,128)(2,1)S(1)} collective-permute-done((bf16[3,64,256]{2,1,0:T(8,128)(2,1)S(1)}, bf16[3,64,256]{2,1,0:T(8,128)(2,1)S(1)}, u32[]{:S(2)}, u32[]{:S(2)}) %collective-permute-start.3) | collective-permute-done | bytes 98336 | tf_op jit(solution)/shard_map/ppermute | solution.py:44
  18.6 4.0 %collective-permute-start.8 = (bf16[4,3,64,256]{3,2,1,0:T(8,128)(2,1)S(1)}, bf16[4,3,64,256]{3,2,1,0:T(8,128)(2,1)S(1)}, u32[]{:S(2)}, u32[]{:S(2)}) collective-permute-start(bf16[4,3,64,256]{3,2,1,0:T(8,128)(2,1)S(1)} %line.1.rows_ref), channel_id=1, source_target_pairs={{0,24},{1,7},{2,26},{3,1},{4,28},{5,3},{6,30},{7,5},{8,0},{9,15},{... | collective-permute-start | bytes 1179656 | tf_op jit(solution)/shard_map/ppermute | solution.py:44
  22.6 1.3 %collective-permute-start.7 = (bf16[4,3,64,256]{3,2,1,0:T(8,128)(2,1)S(1)}, bf16[4,3,64,256]{3,2,1,0:T(8,128)(2,1)S(1)}, u32[]{:S(2)}, u32[]{:S(2)}) collective-permute-start(bf16[4,3,64,256]{3,2,1,0:T(8,128)(2,1)S(1)} %line.1.rows_ref), channel_id=1, source_target_pairs={{0,8},{1,3},{2,10},{3,5},{4,12},{5,7},{6,14},{7,1},{8,16},{9,11},{... | collective-permute-start | bytes 1179656 | tf_op jit(solution)/shard_map/ppermute | solution.py:44
  23.9 5.2 %net_first.1 = (f32[3,128,256]{2,1,0:T(8,128)S(1)}, bf16[3,2048,256]{2,1,0:T(8,128)(2,1)S(1)}, f32[3,2,64,32]{3,2,1,0:T(8,128)S(1)}) custom-call(s32[64]{0:T(128)S(1)} %get-tuple-element.98.live_ref, bf16[4,3,64,256]{3,2,1,0:T(8,128)(2,1)S(1)} %line.1.rows_ref, bf16[3,2048,256]{2,1,0:T(8,128)(2,1)} %bitcast.246, ...), custom_call_target="tpu_custom_call" | custom-call | tf_op jit(solution)/shard_map/net_first/pallas_call | solution.py:132
  29.2 3.0 %collective-permute-done.8.refs_0_ = bf16[4,3,64,256]{3,2,1,0:T(8,128)(2,1)S(1)} collective-permute-done((bf16[4,3,64,256]{3,2,1,0:T(8,128)(2,1)S(1)}, bf16[4,3,64,256]{3,2,1,0:T(8,128)(2,1)S(1)}, u32[]{:S(2)}, u32[]{:S(2)}) %collective-permute-start.8) | collective-permute-done | bytes 393248 | tf_op jit(solution)/shard_map/ppermute | solution.py:44
  32.1 3.3 %net_next.2 = f32[3,128,256]{2,1,0:T(8,128)S(1)} custom-call(s32[64]{0:T(128)S(1)} %get-tuple-element.98.live_ref, bf16[3,2048,256]{2,1,0:T(8,128)(2,1)S(1)} %get-tuple-element.17.held_ref, bf16[3,2048,256]{2,1,0:T(8,128)(2,1)S(1)} %collective-permute-done.4.other_ref, f32[3,2,64,32]{3,2,1,0:T(8,128)S(1)} %get-tuple-element.18.floor_ref, ...), custom_call_target="tpu_custom_call" | custom-call | tf_op jit(solution)/shard_map/net_next/pallas_call | solution.py:154
  35.8 5.8 %net_next.3 = (f32[3,128,256]{2,1,0:T(8,128)S(1)}, f32[3,128,256]{2,1,0:T(8,128)S(1)}) custom-call(s32[64]{0:T(128)S(1)} %get-tuple-element.98.live_ref, bf16[3,2048,256]{2,1,0:T(8,128)(2,1)S(1)} %get-tuple-element.17.held_ref, bf16[3,2048,256]{2,1,0:T(8,128)(2,1)S(1)} %collective-permute-done.4.other_ref, f32[3,2,64,32]{3,2,1,0:T(8,128)S(1)} %get-tuple-element.18.floor_ref, ...), custom_call_target="tpu_custom_call" | custom-call | tf_op jit(solution)/shard_map/net_next/pallas_call | solution.py:154
  42.2 1.2 %collective-permute-start.11 = (f16[4,3,8,1024]{3,2,1,0:T(8,128)(2,1)S(1)}, f16[4,3,8,1024]{3,2,1,0:T(8,128)(2,1)S(1)}, u32[]{:S(2)}, u32[]{:S(2)}) collective-permute-start(f16[4,3,8,1024]{3,2,1,0:T(8,128)(2,1)S(1)} %pad_maximum_fusion.2), channel_id=1, source_target_pairs={{0,2},{1,9},{2,4},{3,11},{4,6},{5,13},{6,0},{7,15},{8,10},{9,17},{... | collective-permute-start | bytes 589832 | tf_op jit(solution)/shard_map/ppermute | solution.py:44
  43.6 2.4 %collective-permute-start.10 = (f16[4,3,8,1024]{3,2,1,0:T(8,128)(2,1)S(1)}, f16[4,3,8,1024]{3,2,1,0:T(8,128)(2,1)S(1)}, u32[]{:S(2)}, u32[]{:S(2)}) collective-permute-start(f16[4,3,8,1024]{3,2,1,0:T(8,128)(2,1)S(1)} %pad_maximum_fusion.1), channel_id=1, source_target_pairs={{0,6},{1,25},{2,0},{3,27},{4,2},{5,29},{6,4},{7,31},{8,14},{9,1},{... | collective-permute-start | bytes 589832 | tf_op jit(solution)/shard_map/ppermute | solution.py:44
  46.4 2.8 %collective-permute-done.11 = f16[4,3,8,1024]{3,2,1,0:T(8,128)(2,1)S(1)} collective-permute-done((f16[4,3,8,1024]{3,2,1,0:T(8,128)(2,1)S(1)}, f16[4,3,8,1024]{3,2,1,0:T(8,128)(2,1)S(1)}, u32[]{:S(2)}, u32[]{:S(2)}) %collective-permute-start.11) | collective-permute-done | bytes 196640 | tf_op jit(solution)/shard_map/ppermute | solution.py:44
  49.2 2.2 %collective-permute-done.10 = f16[4,3,8,1024]{3,2,1,0:T(8,128)(2,1)S(1)} collective-permute-done((f16[4,3,8,1024]{3,2,1,0:T(8,128)(2,1)S(1)}, f16[4,3,8,1024]{3,2,1,0:T(8,128)(2,1)S(1)}, u32[]{:S(2)}, u32[]{:S(2)}) %collective-permute-start.10) | collective-permute-done | bytes 196640 | tf_op jit(solution)/shard_map/ppermute | solution.py:44
  51.3 2.1 %collective-permute-done.9 = f16[4,3,8,1024]{3,2,1,0:T(8,128)(2,1)S(1)} collective-permute-done((f16[4,3,8,1024]{3,2,1,0:T(8,128)(2,1)S(1)}, f16[4,3,8,1024]{3,2,1,0:T(8,128)(2,1)S(1)}, u32[]{:S(2)}, u32[]{:S(2)}) %collective-permute-start.9) | collective-permute-done | bytes 196640 | tf_op jit(solution)/shard_map/ppermute | solution.py:44
  53.7 3.5 %collective-permute-start.13 = (f16[3,8,1024]{2,1,0:T(8,128)(2,1)S(1)}, f16[3,8,1024]{2,1,0:T(8,128)(2,1)S(1)}, u32[]{:S(2)}, u32[]{:S(2)}) collective-permute-start(f16[3,8,1024]{2,1,0:T(8,128)(2,1)S(1)} %get-tuple-element.30), channel_id=1, source_target_pairs={{0,24},{1,7},{2,26},{3,1},{4,28},{5,3},{6,30},{7,5},{8,0},{9,15},{... | collective-permute-start | bytes 147464 | tf_op jit(solution)/shard_map/ppermute | solution.py:44
  57.2 1.4 %collective-permute-start.12 = (f16[3,8,1024]{2,1,0:T(8,128)(2,1)S(1)}, f16[3,8,1024]{2,1,0:T(8,128)(2,1)S(1)}, u32[]{:S(2)}, u32[]{:S(2)}) collective-permute-start(f16[3,8,1024]{2,1,0:T(8,128)(2,1)S(1)} %get-tuple-element.28), channel_id=1, source_target_pairs={{0,16},{1,5},{2,18},{3,7},{4,20},{5,1},{6,22},{7,3},{8,24},{9,13},... | collective-permute-start | bytes 147464 | tf_op jit(solution)/shard_map/ppermute | solution.py:44
  58.6 0.6 collective-permute-done.14
  59.2 3.6 %collective-permute-done.12 = f16[3,8,1024]{2,1,0:T(8,128)(2,1)S(1)} collective-permute-done((f16[3,8,1024]{2,1,0:T(8,128)(2,1)S(1)}, f16[3,8,1024]{2,1,0:T(8,128)(2,1)S(1)}, u32[]{:S(2)}, u32[]{:S(2)}) %collective-permute-start.12) | collective-permute-done | bytes 49184 | tf_op jit(solution)/shard_map/ppermute | solution.py:44
  63.2 1.1 %collective-permute-done.15 = f32[3,4,8]{2,1,0:T(4,128)S(1)} collective-permute-done((f32[3,4,8]{2,1,0:T(4,128)S(1)}, f32[3,4,8]{2,1,0:T(4,128)S(1)}, u32[]{:S(2)}, u32[]{:S(2)}) %collective-permute-start.15) | collective-permute-done | bytes 416 | tf_op jit(solution)/shard_map/ppermute | solution.py:48
  64.4 1.6 %collective-permute-start.18 = (f32[3,4,8]{2,1,0:T(4,128)S(1)}, f32[3,4,8]{2,1,0:T(4,128)S(1)}, u32[]{:S(2)}, u32[]{:S(2)}) collective-permute-start(f32[3,4,8]{2,1,0:T(4,128)S(1)} %bitcast_add_fusion), channel_id=1, source_target_pairs={{0,32},{32,64},{64,96},{96,0},{1,33},{33,65},{65,97},{97,1},{2,34}... | collective-permute-start | bytes 1160 | tf_op jit(solution)/shard_map/ppermute | solution.py:295
  66.0 1.7 %collective-permute-start.17 = (f32[3,4,8]{2,1,0:T(4,128)S(1)}, f32[3,4,8]{2,1,0:T(4,128)S(1)}, u32[]{:S(2)}, u32[]{:S(2)}) collective-permute-start(f32[3,4,8]{2,1,0:T(4,128)S(1)} %bitcast_add_fusion), channel_id=1, source_target_pairs={{0,96},{32,0},{64,32},{96,64},{1,97},{33,1},{65,33},{97,65},{2,98}... | collective-permute-start | bytes 1160 | tf_op jit(solution)/shard_map/ppermute | solution.py:295
  67.6 2.0 %collective-permute-start.16 = (f32[3,4,8]{2,1,0:T(4,128)S(1)}, f32[3,4,8]{2,1,0:T(4,128)S(1)}, u32[]{:S(2)}, u32[]{:S(2)}) collective-permute-start(f32[3,4,8]{2,1,0:T(4,128)S(1)} %bitcast_add_fusion), channel_id=1, source_target_pairs={{0,64},{32,96},{64,0},{96,32},{1,65},{33,97},{65,1},{97,33},{2,66}... | collective-permute-start | bytes 1160 | tf_op jit(solution)/shard_map/ppermute | solution.py:295
  69.6 3.1 %collective-permute-done.16 = f32[3,4,8]{2,1,0:T(4,128)S(1)} collective-permute-done((f32[3,4,8]{2,1,0:T(4,128)S(1)}, f32[3,4,8]{2,1,0:T(4,128)S(1)}, u32[]{:S(2)}, u32[]{:S(2)}) %collective-permute-start.16) | collective-permute-done | bytes 416 | tf_op jit(solution)/shard_map/ppermute | solution.py:295
  73.0 0.6 multiply_sqrt_fusion
  (79 shorter events, 2.8 us)
Async XLA Ops:
  0.6 12.2 %copy-start.1 = (s32[32]{0:T(128)S(1)}, s32[32]{0:T(128)}, u32[]{:S(2)}) copy-start(s32[32]{0:T(128)} %param.11) | copy-start | bytes 388
  0.6 12.2 %copy-start.2 = (s32[32]{0:T(128)S(1)}, s32[32]{0:T(128)}, u32[]{:S(2)}) copy-start(s32[32]{0:T(128)} %param.10) | copy-start | bytes 388
  0.7 23.2 %collective-permute-start.4 = (bf16[3,2048,256]{2,1,0:T(8,128)(2,1)}, bf16[3,2048,256]{2,1,0:T(8,128)(2,1)S(1)}, u32[]{:S(2)}, u32[]{:S(2)}) collective-permute-start(bf16[3,2048,256]{2,1,0:T(8,128)(2,1)} %bitcast.245), channel_id=1, source_target_pairs={{0,1},{1,0},{2,3},{3,2},{4,5},{5,4},{6,7},{7,6},{8,9},{9,8},{10,11... | collective-permute-start | bytes 9437192 | tf_op jit(solution)/shard_map/ppermute | solution.py:48
  8.2 9.1 %collective-permute-start.1 = (bf16[3,64,256]{2,1,0:T(8,128)(2,1)S(1)}, bf16[3,64,256]{2,1,0:T(8,128)(2,1)S(1)}, u32[]{:S(2)}, u32[]{:S(2)}) collective-permute-start(bf16[3,64,256]{2,1,0:T(8,128)(2,1)S(1)} %basis.1.refs_0_), channel_id=1, source_target_pairs={{0,6},{1,25},{2,0},{3,27},{4,2},{5,29},{6,4},{7,31},{8,14},{9,1},{... | collective-permute-start | bytes 294920 | tf_op jit(solution)/shard_map/ppermute | solution.py:44
  11.1 6.2 %collective-permute-start.2 = (bf16[3,64,256]{2,1,0:T(8,128)(2,1)S(1)}, bf16[3,64,256]{2,1,0:T(8,128)(2,1)S(1)}, u32[]{:S(2)}, u32[]{:S(2)}) collective-permute-start(bf16[3,64,256]{2,1,0:T(8,128)(2,1)S(1)} %basis.1.refs_0_), channel_id=1, source_target_pairs={{0,4},{1,17},{2,6},{3,19},{4,0},{5,21},{6,2},{7,23},{8,12},{9,25},... | collective-permute-start | bytes 294920 | tf_op jit(solution)/shard_map/ppermute | solution.py:44
  11.9 6.4 %collective-permute-start.3 = (bf16[3,64,256]{2,1,0:T(8,128)(2,1)S(1)}, bf16[3,64,256]{2,1,0:T(8,128)(2,1)S(1)}, u32[]{:S(2)}, u32[]{:S(2)}) collective-permute-start(bf16[3,64,256]{2,1,0:T(8,128)(2,1)S(1)} %basis.1.refs_0_), channel_id=1, source_target_pairs={{0,2},{1,9},{2,4},{3,11},{4,6},{5,13},{6,0},{7,15},{8,10},{9,17},{... | collective-permute-start | bytes 294920 | tf_op jit(solution)/shard_map/ppermute | solution.py:44
  13.4 1.7 %collective-permute-start = (s32[2,32]{1,0:T(2,128)}, s32[2,32]{1,0:T(2,128)}, u32[]{:S(2)}, u32[]{:S(2)}) collective-permute-start(s32[2,32]{1,0:T(2,128)} %pad_add_fusion), channel_id=1, source_target_pairs={{0,1},{1,0},{2,3},{3,2},{4,5},{5,4},{6,7},{7,6},{8,9},{9,8},{10,11... | collective-permute-start | bytes 776 | tf_op jit(solution)/shard_map/ppermute | solution.py:48
  18.3 5.6 %collective-permute-start.5 = (f32[3,32,64]{2,1,0:T(8,128)}, f32[3,32,64]{2,1,0:T(8,128)S(1)}, u32[]{:S(2)}, u32[]{:S(2)}) collective-permute-start(f32[3,32,64]{2,1,0:T(8,128)} %my_floor_ref.1), channel_id=1, source_target_pairs={{0,1},{1,0},{2,3},{3,2},{4,5},{5,4},{6,7},{7,6},{8,9},{9,8},{10,11... | collective-permute-start | bytes 73736 | tf_op jit(solution)/shard_map/ppermute | solution.py:48
  18.6 13.5 %collective-permute-start.8 = (bf16[4,3,64,256]{3,2,1,0:T(8,128)(2,1)S(1)}, bf16[4,3,64,256]{3,2,1,0:T(8,128)(2,1)S(1)}, u32[]{:S(2)}, u32[]{:S(2)}) collective-permute-start(bf16[4,3,64,256]{3,2,1,0:T(8,128)(2,1)S(1)} %line.1.rows_ref), channel_id=1, source_target_pairs={{0,24},{1,7},{2,26},{3,1},{4,28},{5,3},{6,30},{7,5},{8,0},{9,15},{... | collective-permute-start | bytes 1179656 | tf_op jit(solution)/shard_map/ppermute | solution.py:44
  22.6 12.9 %collective-permute-start.6 = (bf16[4,3,64,256]{3,2,1,0:T(8,128)(2,1)S(1)}, bf16[4,3,64,256]{3,2,1,0:T(8,128)(2,1)S(1)}, u32[]{:S(2)}, u32[]{:S(2)}) collective-permute-start(bf16[4,3,64,256]{3,2,1,0:T(8,128)(2,1)S(1)} %line.1.rows_ref), channel_id=1, source_target_pairs={{0,16},{1,5},{2,18},{3,7},{4,20},{5,1},{6,22},{7,3},{8,24},{9,13},... | collective-permute-start | bytes 1179656 | tf_op jit(solution)/shard_map/ppermute | solution.py:44
  22.6 13.2 %collective-permute-start.7 = (bf16[4,3,64,256]{3,2,1,0:T(8,128)(2,1)S(1)}, bf16[4,3,64,256]{3,2,1,0:T(8,128)(2,1)S(1)}, u32[]{:S(2)}, u32[]{:S(2)}) collective-permute-start(bf16[4,3,64,256]{3,2,1,0:T(8,128)(2,1)S(1)} %line.1.rows_ref), channel_id=1, source_target_pairs={{0,8},{1,3},{2,10},{3,5},{4,12},{5,7},{6,14},{7,1},{8,16},{9,11},{... | collective-permute-start | bytes 1179656 | tf_op jit(solution)/shard_map/ppermute | solution.py:44
  42.2 6.9 %collective-permute-start.11 = (f16[4,3,8,1024]{3,2,1,0:T(8,128)(2,1)S(1)}, f16[4,3,8,1024]{3,2,1,0:T(8,128)(2,1)S(1)}, u32[]{:S(2)}, u32[]{:S(2)}) collective-permute-start(f16[4,3,8,1024]{3,2,1,0:T(8,128)(2,1)S(1)} %pad_maximum_fusion.2), channel_id=1, source_target_pairs={{0,2},{1,9},{2,4},{3,11},{4,6},{5,13},{6,0},{7,15},{8,10},{9,17},{... | collective-permute-start | bytes 589832 | tf_op jit(solution)/shard_map/ppermute | solution.py:44
  43.6 7.7 %collective-permute-start.10 = (f16[4,3,8,1024]{3,2,1,0:T(8,128)(2,1)S(1)}, f16[4,3,8,1024]{3,2,1,0:T(8,128)(2,1)S(1)}, u32[]{:S(2)}, u32[]{:S(2)}) collective-permute-start(f16[4,3,8,1024]{3,2,1,0:T(8,128)(2,1)S(1)} %pad_maximum_fusion.1), channel_id=1, source_target_pairs={{0,6},{1,25},{2,0},{3,27},{4,2},{5,29},{6,4},{7,31},{8,14},{9,1},{... | collective-permute-start | bytes 589832 | tf_op jit(solution)/shard_map/ppermute | solution.py:44
  46.2 7.3 %collective-permute-start.9 = (f16[4,3,8,1024]{3,2,1,0:T(8,128)(2,1)S(1)}, f16[4,3,8,1024]{3,2,1,0:T(8,128)(2,1)S(1)}, u32[]{:S(2)}, u32[]{:S(2)}) collective-permute-start(f16[4,3,8,1024]{3,2,1,0:T(8,128)(2,1)S(1)} %pad_maximum_fusion), channel_id=1, source_target_pairs={{0,4},{1,17},{2,6},{3,19},{4,0},{5,21},{6,2},{7,23},{8,12},{9,25},... | collective-permute-start | bytes 589832 | tf_op jit(solution)/shard_map/ppermute | solution.py:44
  53.6 5.6 %collective-permute-start.14 = (f16[3,8,1024]{2,1,0:T(8,128)(2,1)S(1)}, f16[3,8,1024]{2,1,0:T(8,128)(2,1)S(1)}, u32[]{:S(2)}, u32[]{:S(2)}) collective-permute-start(f16[3,8,1024]{2,1,0:T(8,128)(2,1)S(1)} %get-tuple-element.29), channel_id=1, source_target_pairs={{0,8},{1,3},{2,10},{3,5},{4,12},{5,7},{6,14},{7,1},{8,16},{9,11},{... | collective-permute-start | bytes 147464 | tf_op jit(solution)/shard_map/ppermute | solution.py:44
  53.7 5.5 %collective-permute-start.13 = (f16[3,8,1024]{2,1,0:T(8,128)(2,1)S(1)}, f16[3,8,1024]{2,1,0:T(8,128)(2,1)S(1)}, u32[]{:S(2)}, u32[]{:S(2)}) collective-permute-start(f16[3,8,1024]{2,1,0:T(8,128)(2,1)S(1)} %get-tuple-element.30), channel_id=1, source_target_pairs={{0,24},{1,7},{2,26},{3,1},{4,28},{5,3},{6,30},{7,5},{8,0},{9,15},{... | collective-permute-start | bytes 147464 | tf_op jit(solution)/shard_map/ppermute | solution.py:44
  57.2 5.6 %collective-permute-start.12 = (f16[3,8,1024]{2,1,0:T(8,128)(2,1)S(1)}, f16[3,8,1024]{2,1,0:T(8,128)(2,1)S(1)}, u32[]{:S(2)}, u32[]{:S(2)}) collective-permute-start(f16[3,8,1024]{2,1,0:T(8,128)(2,1)S(1)} %get-tuple-element.28), channel_id=1, source_target_pairs={{0,16},{1,5},{2,18},{3,7},{4,20},{5,1},{6,22},{7,3},{8,24},{9,13},... | collective-permute-start | bytes 147464 | tf_op jit(solution)/shard_map/ppermute | solution.py:44
  63.1 1.2 %collective-permute-start.15 = (f32[3,4,8]{2,1,0:T(4,128)S(1)}, f32[3,4,8]{2,1,0:T(4,128)S(1)}, u32[]{:S(2)}, u32[]{:S(2)}) collective-permute-start(f32[3,4,8]{2,1,0:T(4,128)S(1)} %dynamic-slice_bitcast_fusion), channel_id=1, source_target_pairs={{0,1},{1,0},{2,3},{3,2},{4,5},{5,4},{6,7},{7,6},{8,9},{9,8},{10,11... | collective-permute-start | bytes 1160 | tf_op jit(solution)/shard_map/ppermute | solution.py:48
  64.4 5.2 %collective-permute-start.18 = (f32[3,4,8]{2,1,0:T(4,128)S(1)}, f32[3,4,8]{2,1,0:T(4,128)S(1)}, u32[]{:S(2)}, u32[]{:S(2)}) collective-permute-start(f32[3,4,8]{2,1,0:T(4,128)S(1)} %bitcast_add_fusion), channel_id=1, source_target_pairs={{0,32},{32,64},{64,96},{96,0},{1,33},{33,65},{65,97},{97,1},{2,34}... | collective-permute-start | bytes 1160 | tf_op jit(solution)/shard_map/ppermute | solution.py:295
  66.0 3.7 %collective-permute-start.17 = (f32[3,4,8]{2,1,0:T(4,128)S(1)}, f32[3,4,8]{2,1,0:T(4,128)S(1)}, u32[]{:S(2)}, u32[]{:S(2)}) collective-permute-start(f32[3,4,8]{2,1,0:T(4,128)S(1)} %bitcast_add_fusion), channel_id=1, source_target_pairs={{0,96},{32,0},{64,32},{96,64},{1,97},{33,1},{65,33},{97,65},{2,98}... | collective-permute-start | bytes 1160 | tf_op jit(solution)/shard_map/ppermute | solution.py:295
  67.6 5.1 %collective-permute-start.16 = (f32[3,4,8]{2,1,0:T(4,128)S(1)}, f32[3,4,8]{2,1,0:T(4,128)S(1)}, u32[]{:S(2)}, u32[]{:S(2)}) collective-permute-start(f32[3,4,8]{2,1,0:T(4,128)S(1)} %bitcast_add_fusion), channel_id=1, source_target_pairs={{0,64},{32,96},{64,0},{96,32},{1,65},{33,97},{65,1},{97,33},{2,66}... | collective-permute-start | bytes 1160 | tf_op jit(solution)/shard_map/ppermute | solution.py:295
  72.9 0.8 %copy-start = (f32[3,4]{1,0:T(4,128)}, f32[3,4]{1,0:T(4,128)S(1)}, u32[]{:S(2)}) copy-start(f32[3,4]{1,0:T(4,128)S(1)} %broadcast_multiply_fusion) | copy-start | bytes 148

commit v8 on v7

--- a/solution.py
+++ b/solution.py
@@ -19,7 +19,7 @@
 CHUNK = SIDE * ROWS
 OWN = 2 * SPD
 GROUP = 4
-ORDER = ((3,), (2, 1))
+ORDER = ((1,), (3, 2))
 F32 = jnp.float32
 BF16 = jnp.bfloat16
 

time: 73.8 us -> 73.7 us (level)
  waiting for transfers between devices: 20.7 us -> 15.8 us
  starting transfers between devices: 24.7 us -> 29.2 us
    ppermute x12, waiting for transfers between devices: 15.5 us -> 10.6 us  [shift_by(): return lax.ppermute(value, 'set', ring_pairs(shift, stage))]
    ppermute x12, starting transfers between devices: 18.6 us -> 22.9 us  [shift_by(): return lax.ppermute(value, 'set', ring_pairs(shift, stage))]
  transfers between devices with their start and end apart: 19 -> 19, of which waited for: 11 -> 8; matrix products, arithmetic and copies ran while one was open for 5% -> 5% of each run, Pallas kernels for 22% -> 22%
where the time goes in v8:
time: 73.7 us; the launch traced here: 73.6 us
  starting transfers between devices  29.2 us (40%)
  Pallas kernels  22.2 us (30%)
  waiting for transfers between devices  15.8 us (21%)
  other arithmetic  3.19 us (4%)
  local copies, waits for them, and re-layouts  1.88 us (3%)
  between operations  1.11 us (2%)
    ppermute x12, starting transfers between devices, shift_by(): return lax.ppermute(value, 'set', ring_pairs(shift, stage))  22.9 us
    ppermute x12, waiting for transfers between devices, shift_by(): return lax.ppermute(value, 'set', ring_pairs(shift, stage))  10.6 us
    pallas_call x2, Pallas kernels, net_next(): pl.pallas_call(net_next_kernel, in_specs=[SMEM] + [VMEM] * (4 + len(chunk...  9.38 us
    pallas_call x1, Pallas kernels, make_basis(): pl.pallas_call(basis_kernel, grid=(-(-FACTORS // FACTOR_TILE),), in_specs...  7.43 us
    pallas_call x1, Pallas kernels, net_first(): pl.pallas_call(net_first_kernel, in_specs=[SMEM, VMEM, HBM, VMEM, HBM, VM...  5.31 us
    ppermute x3, starting transfers between devices, body(): lax.ppermute(sums, 'rep', [(i, (i + shift) % SIDE) for i in range(SIDE)])  5.22 us
    ppermute x3, waiting for transfers between devices, body(): lax.ppermute(sums, 'rep', [(i, (i + shift) % SIDE) for i in range(SIDE)])  3.15 us
    ppermute x4, waiting for transfers between devices, swap_core(): return lax.ppermute(value, 'set', CORE_PAIRS)  2.04 us
  transfers between devices with their start and end apart: 19, of which 8 were waited for; matrix products, arithmetic and copies ran while one was open for 5% of the time, Pallas kernels for 22%

profile of v8, /device:TPU:0, one launch (start us, length us, event | category | flops | bytes accessed | tf_op | source)
XLA Modules:
  0.0 73.6 jit_solution(10985199111055622448)
XLA Ops:
  0.7 7.4 %basis.1.refs_0_ = bf16[3,64,256]{2,1,0:T(8,128)(2,1)S(1)} custom-call(bf16[3,64,20000]{2,1,0:T(8,128)(2,1)} %scenarios_ref.1, bf16[20000,256]{1,0:T(8,128)(2,1)} %projection_ref.1), custom_call_target="tpu_custom_call" | custom-call | tf_op jit(solution)/shard_map/basis/pallas_call | solution.py:190
  8.2 1.7 %collective-permute-start.3 = (bf16[3,64,256]{2,1,0:T(8,128)(2,1)S(1)}, bf16[3,64,256]{2,1,0:T(8,128)(2,1)S(1)}, u32[]{:S(2)}, u32[]{:S(2)}) collective-permute-start(bf16[3,64,256]{2,1,0:T(8,128)(2,1)S(1)} %basis.1.refs_0_), channel_id=1, source_target_pairs={{0,2},{1,9},{2,4},{3,11},{4,6},{5,13},{6,0},{7,15},{8,10},{9,17},{... | collective-permute-start | bytes 294920 | tf_op jit(solution)/shard_map/ppermute | solution.py:44
  9.9 2.7 %collective-permute-start.2 = (bf16[3,64,256]{2,1,0:T(8,128)(2,1)S(1)}, bf16[3,64,256]{2,1,0:T(8,128)(2,1)S(1)}, u32[]{:S(2)}, u32[]{:S(2)}) collective-permute-start(bf16[3,64,256]{2,1,0:T(8,128)(2,1)S(1)} %basis.1.refs_0_), channel_id=1, source_target_pairs={{0,4},{1,17},{2,6},{3,19},{4,0},{5,21},{6,2},{7,23},{8,12},{9,25},... | collective-permute-start | bytes 294920 | tf_op jit(solution)/shard_map/ppermute | solution.py:44
  12.6 1.4 %collective-permute-start.1 = (bf16[3,64,256]{2,1,0:T(8,128)(2,1)S(1)}, bf16[3,64,256]{2,1,0:T(8,128)(2,1)S(1)}, u32[]{:S(2)}, u32[]{:S(2)}) collective-permute-start(bf16[3,64,256]{2,1,0:T(8,128)(2,1)S(1)} %basis.1.refs_0_), channel_id=1, source_target_pairs={{0,6},{1,25},{2,0},{3,27},{4,2},{5,29},{6,4},{7,31},{8,14},{9,1},{... | collective-permute-start | bytes 294920 | tf_op jit(solution)/shard_map/ppermute | solution.py:44
  14.0 0.6 pad_add_fusion
  14.6 0.5 collective-permute-start
  15.4 0.9 %collective-permute-done = s32[2,32]{1,0:T(2,128)} collective-permute-done((s32[2,32]{1,0:T(2,128)}, s32[2,32]{1,0:T(2,128)}, u32[]{:S(2)}, u32[]{:S(2)}) %collective-permute-start) | collective-permute-done | bytes 288 | tf_op jit(solution)/shard_map/ppermute | solution.py:48
  16.3 0.7 pad_add_fusion.1
  17.0 0.7 broadcast_in_dim.2
  17.7 0.8 %eq.43 = s32[512]{0:T(512)S(1)} reshape(s32[64,8]{1,0:T(8,128)} %broadcast_in_dim.2) | data formatting | bytes 4096 | tf_op jit(solution)/shard_map/eq | solution.py:246
  19.1 3.6 %collective-permute-start.8 = (bf16[4,3,64,256]{3,2,1,0:T(8,128)(2,1)S(1)}, bf16[4,3,64,256]{3,2,1,0:T(8,128)(2,1)S(1)}, u32[]{:S(2)}, u32[]{:S(2)}) collective-permute-start(bf16[4,3,64,256]{3,2,1,0:T(8,128)(2,1)S(1)} %line.1.rows_ref), channel_id=1, source_target_pairs={{0,16},{1,5},{2,18},{3,7},{4,20},{5,1},{6,22},{7,3},{8,24},{9,13},... | collective-permute-start | bytes 1179656 | tf_op jit(solution)/shard_map/ppermute | solution.py:44
  22.7 0.7 collective-permute-start.7
  23.5 1.3 %collective-permute-start.6 = (bf16[4,3,64,256]{3,2,1,0:T(8,128)(2,1)S(1)}, bf16[4,3,64,256]{3,2,1,0:T(8,128)(2,1)S(1)}, u32[]{:S(2)}, u32[]{:S(2)}) collective-permute-start(bf16[4,3,64,256]{3,2,1,0:T(8,128)(2,1)S(1)} %line.1.rows_ref), channel_id=1, source_target_pairs={{0,8},{1,3},{2,10},{3,5},{4,12},{5,7},{6,14},{7,1},{8,16},{9,11},{... | collective-permute-start | bytes 1179656 | tf_op jit(solution)/shard_map/ppermute | solution.py:44
  24.8 5.3 %net_first.1 = (f32[3,128,256]{2,1,0:T(8,128)S(1)}, bf16[3,2048,256]{2,1,0:T(8,128)(2,1)S(1)}, f32[3,2,64,32]{3,2,1,0:T(8,128)S(1)}) custom-call(s32[64]{0:T(128)S(1)} %get-tuple-element.98.live_ref, bf16[4,3,64,256]{3,2,1,0:T(8,128)(2,1)S(1)} %line.1.rows_ref, bf16[3,2048,256]{2,1,0:T(8,128)(2,1)} %bitcast.246, ...), custom_call_target="tpu_custom_call" | custom-call | tf_op jit(solution)/shard_map/net_first/pallas_call | solution.py:132
  30.1 2.6 %collective-permute-done.6.refs_0_ = bf16[4,3,64,256]{3,2,1,0:T(8,128)(2,1)S(1)} collective-permute-done((bf16[4,3,64,256]{3,2,1,0:T(8,128)(2,1)S(1)}, bf16[4,3,64,256]{3,2,1,0:T(8,128)(2,1)S(1)}, u32[]{:S(2)}, u32[]{:S(2)}) %collective-permute-start.6) | collective-permute-done | bytes 393248 | tf_op jit(solution)/shard_map/ppermute | solution.py:44
  32.7 3.4 %net_next.2 = f32[3,128,256]{2,1,0:T(8,128)S(1)} custom-call(s32[64]{0:T(128)S(1)} %get-tuple-element.98.live_ref, bf16[3,2048,256]{2,1,0:T(8,128)(2,1)S(1)} %get-tuple-element.17.held_ref, bf16[3,2048,256]{2,1,0:T(8,128)(2,1)S(1)} %collective-permute-done.4.other_ref, f32[3,2,64,32]{3,2,1,0:T(8,128)S(1)} %get-tuple-element.18.floor_ref, ...), custom_call_target="tpu_custom_call" | custom-call | tf_op jit(solution)/shard_map/net_next/pallas_call | solution.py:154
  36.2 6.0 %net_next.3 = (f32[3,128,256]{2,1,0:T(8,128)S(1)}, f32[3,128,256]{2,1,0:T(8,128)S(1)}) custom-call(s32[64]{0:T(128)S(1)} %get-tuple-element.98.live_ref, bf16[3,2048,256]{2,1,0:T(8,128)(2,1)S(1)} %get-tuple-element.17.held_ref, bf16[3,2048,256]{2,1,0:T(8,128)(2,1)S(1)} %collective-permute-done.4.other_ref, f32[3,2,64,32]{3,2,1,0:T(8,128)S(1)} %get-tuple-element.18.floor_ref, ...), custom_call_target="tpu_custom_call" | custom-call | tf_op jit(solution)/shard_map/net_next/pallas_call | solution.py:154
  42.7 3.1 %collective-permute-start.9 = (f16[4,3,8,1024]{3,2,1,0:T(8,128)(2,1)S(1)}, f16[4,3,8,1024]{3,2,1,0:T(8,128)(2,1)S(1)}, u32[]{:S(2)}, u32[]{:S(2)}) collective-permute-start(f16[4,3,8,1024]{3,2,1,0:T(8,128)(2,1)S(1)} %pad_maximum_fusion), channel_id=1, source_target_pairs={{0,4},{1,17},{2,6},{3,19},{4,0},{5,21},{6,2},{7,23},{8,12},{9,25},... | collective-permute-start | bytes 589832 | tf_op jit(solution)/shard_map/ppermute | solution.py:44
  46.0 1.4 %collective-permute-start.10 = (f16[4,3,8,1024]{3,2,1,0:T(8,128)(2,1)S(1)}, f16[4,3,8,1024]{3,2,1,0:T(8,128)(2,1)S(1)}, u32[]{:S(2)}, u32[]{:S(2)}) collective-permute-start(f16[4,3,8,1024]{3,2,1,0:T(8,128)(2,1)S(1)} %pad_maximum_fusion.1), channel_id=1, source_target_pairs={{0,6},{1,25},{2,0},{3,27},{4,2},{5,29},{6,4},{7,31},{8,14},{9,1},{... | collective-permute-start | bytes 589832 | tf_op jit(solution)/shard_map/ppermute | solution.py:44
  47.6 1.0 %collective-permute-start.11 = (f16[4,3,8,1024]{3,2,1,0:T(8,128)(2,1)S(1)}, f16[4,3,8,1024]{3,2,1,0:T(8,128)(2,1)S(1)}, u32[]{:S(2)}, u32[]{:S(2)}) collective-permute-start(f16[4,3,8,1024]{3,2,1,0:T(8,128)(2,1)S(1)} %pad_maximum_fusion.2), channel_id=1, source_target_pairs={{0,2},{1,9},{2,4},{3,11},{4,6},{5,13},{6,0},{7,15},{8,10},{9,17},{... | collective-permute-start | bytes 589832 | tf_op jit(solution)/shard_map/ppermute | solution.py:44
  48.6 1.4 %collective-permute-done.9 = f16[4,3,8,1024]{3,2,1,0:T(8,128)(2,1)S(1)} collective-permute-done((f16[4,3,8,1024]{3,2,1,0:T(8,128)(2,1)S(1)}, f16[4,3,8,1024]{3,2,1,0:T(8,128)(2,1)S(1)}, u32[]{:S(2)}, u32[]{:S(2)}) %collective-permute-start.9) | collective-permute-done | bytes 196640 | tf_op jit(solution)/shard_map/ppermute | solution.py:44
  50.0 2.2 %collective-permute-done.10 = f16[4,3,8,1024]{3,2,1,0:T(8,128)(2,1)S(1)} collective-permute-done((f16[4,3,8,1024]{3,2,1,0:T(8,128)(2,1)S(1)}, f16[4,3,8,1024]{3,2,1,0:T(8,128)(2,1)S(1)}, u32[]{:S(2)}, u32[]{:S(2)}) %collective-permute-start.10) | collective-permute-done | bytes 196640 | tf_op jit(solution)/shard_map/ppermute | solution.py:44
  52.2 2.4 %collective-permute-done.11 = f16[4,3,8,1024]{3,2,1,0:T(8,128)(2,1)S(1)} collective-permute-done((f16[4,3,8,1024]{3,2,1,0:T(8,128)(2,1)S(1)}, f16[4,3,8,1024]{3,2,1,0:T(8,128)(2,1)S(1)}, u32[]{:S(2)}, u32[]{:S(2)}) %collective-permute-start.11) | collective-permute-done | bytes 196640 | tf_op jit(solution)/shard_map/ppermute | solution.py:44
  54.7 2.7 %collective-permute-start.12 = (f16[3,8,1024]{2,1,0:T(8,128)(2,1)S(1)}, f16[3,8,1024]{2,1,0:T(8,128)(2,1)S(1)}, u32[]{:S(2)}, u32[]{:S(2)}) collective-permute-start(f16[3,8,1024]{2,1,0:T(8,128)(2,1)S(1)} %get-tuple-element.28), channel_id=1, source_target_pairs={{0,16},{1,5},{2,18},{3,7},{4,20},{5,1},{6,22},{7,3},{8,24},{9,13},... | collective-permute-start | bytes 147464 | tf_op jit(solution)/shard_map/ppermute | solution.py:44
  57.5 3.2 %collective-permute-start.13 = (f16[3,8,1024]{2,1,0:T(8,128)(2,1)S(1)}, f16[3,8,1024]{2,1,0:T(8,128)(2,1)S(1)}, u32[]{:S(2)}, u32[]{:S(2)}) collective-permute-start(f16[3,8,1024]{2,1,0:T(8,128)(2,1)S(1)} %get-tuple-element.30), channel_id=1, source_target_pairs={{0,24},{1,7},{2,26},{3,1},{4,28},{5,3},{6,30},{7,5},{8,0},{9,15},{... | collective-permute-start | bytes 147464 | tf_op jit(solution)/shard_map/ppermute | solution.py:44
  60.7 2.1 %collective-permute-done.14 = f16[3,8,1024]{2,1,0:T(8,128)(2,1)S(1)} collective-permute-done((f16[3,8,1024]{2,1,0:T(8,128)(2,1)S(1)}, f16[3,8,1024]{2,1,0:T(8,128)(2,1)S(1)}, u32[]{:S(2)}, u32[]{:S(2)}) %collective-permute-start.14) | collective-permute-done | bytes 49184 | tf_op jit(solution)/shard_map/ppermute | solution.py:44
  63.2 1.1 %collective-permute-done.15 = f32[3,4,8]{2,1,0:T(4,128)S(1)} collective-permute-done((f32[3,4,8]{2,1,0:T(4,128)S(1)}, f32[3,4,8]{2,1,0:T(4,128)S(1)}, u32[]{:S(2)}, u32[]{:S(2)}) %collective-permute-start.15) | collective-permute-done | bytes 416 | tf_op jit(solution)/shard_map/ppermute | solution.py:48
  64.3 1.6 %collective-permute-start.18 = (f32[3,4,8]{2,1,0:T(4,128)S(1)}, f32[3,4,8]{2,1,0:T(4,128)S(1)}, u32[]{:S(2)}, u32[]{:S(2)}) collective-permute-start(f32[3,4,8]{2,1,0:T(4,128)S(1)} %bitcast_add_fusion), channel_id=1, source_target_pairs={{0,32},{32,64},{64,96},{96,0},{1,33},{33,65},{65,97},{97,1},{2,34}... | collective-permute-start | bytes 1160 | tf_op jit(solution)/shard_map/ppermute | solution.py:295
  65.9 1.7 %collective-permute-start.17 = (f32[3,4,8]{2,1,0:T(4,128)S(1)}, f32[3,4,8]{2,1,0:T(4,128)S(1)}, u32[]{:S(2)}, u32[]{:S(2)}) collective-permute-start(f32[3,4,8]{2,1,0:T(4,128)S(1)} %bitcast_add_fusion), channel_id=1, source_target_pairs={{0,96},{32,0},{64,32},{96,64},{1,97},{33,1},{65,33},{97,65},{2,98}... | collective-permute-start | bytes 1160 | tf_op jit(solution)/shard_map/ppermute | solution.py:295
  67.6 2.0 %collective-permute-start.16 = (f32[3,4,8]{2,1,0:T(4,128)S(1)}, f32[3,4,8]{2,1,0:T(4,128)S(1)}, u32[]{:S(2)}, u32[]{:S(2)}) collective-permute-start(f32[3,4,8]{2,1,0:T(4,128)S(1)} %bitcast_add_fusion), channel_id=1, source_target_pairs={{0,64},{32,96},{64,0},{96,32},{1,65},{33,97},{65,1},{97,33},{2,66}... | collective-permute-start | bytes 1160 | tf_op jit(solution)/shard_map/ppermute | solution.py:295
  69.6 3.1 %collective-permute-done.16 = f32[3,4,8]{2,1,0:T(4,128)S(1)} collective-permute-done((f32[3,4,8]{2,1,0:T(4,128)S(1)}, f32[3,4,8]{2,1,0:T(4,128)S(1)}, u32[]{:S(2)}, u32[]{:S(2)}) %collective-permute-start.16) | collective-permute-done | bytes 416 | tf_op jit(solution)/shard_map/ppermute | solution.py:295
  73.0 0.6 multiply_sqrt_fusion
  (79 shorter events, 2.5 us)
Async XLA Ops:
  0.6 13.4 %copy-start.1 = (s32[32]{0:T(128)S(1)}, s32[32]{0:T(128)}, u32[]{:S(2)}) copy-start(s32[32]{0:T(128)} %param.11) | copy-start | bytes 388
  0.6 13.4 %copy-start.2 = (s32[32]{0:T(128)S(1)}, s32[32]{0:T(128)}, u32[]{:S(2)}) copy-start(s32[32]{0:T(128)} %param.10) | copy-start | bytes 388
  0.7 24.1 %collective-permute-start.4 = (bf16[3,2048,256]{2,1,0:T(8,128)(2,1)}, bf16[3,2048,256]{2,1,0:T(8,128)(2,1)S(1)}, u32[]{:S(2)}, u32[]{:S(2)}) collective-permute-start(bf16[3,2048,256]{2,1,0:T(8,128)(2,1)} %bitcast.245), channel_id=1, source_target_pairs={{0,1},{1,0},{2,3},{3,2},{4,5},{5,4},{6,7},{7,6},{8,9},{9,8},{10,11... | collective-permute-start | bytes 9437192 | tf_op jit(solution)/shard_map/ppermute | solution.py:48
  8.2 10.3 %collective-permute-start.3 = (bf16[3,64,256]{2,1,0:T(8,128)(2,1)S(1)}, bf16[3,64,256]{2,1,0:T(8,128)(2,1)S(1)}, u32[]{:S(2)}, u32[]{:S(2)}) collective-permute-start(bf16[3,64,256]{2,1,0:T(8,128)(2,1)S(1)} %basis.1.refs_0_), channel_id=1, source_target_pairs={{0,2},{1,9},{2,4},{3,11},{4,6},{5,13},{6,0},{7,15},{8,10},{9,17},{... | collective-permute-start | bytes 294920 | tf_op jit(solution)/shard_map/ppermute | solution.py:44
  9.9 8.7 %collective-permute-start.2 = (bf16[3,64,256]{2,1,0:T(8,128)(2,1)S(1)}, bf16[3,64,256]{2,1,0:T(8,128)(2,1)S(1)}, u32[]{:S(2)}, u32[]{:S(2)}) collective-permute-start(bf16[3,64,256]{2,1,0:T(8,128)(2,1)S(1)} %basis.1.refs_0_), channel_id=1, source_target_pairs={{0,4},{1,17},{2,6},{3,19},{4,0},{5,21},{6,2},{7,23},{8,12},{9,25},... | collective-permute-start | bytes 294920 | tf_op jit(solution)/shard_map/ppermute | solution.py:44
  12.6 6.0 %collective-permute-start.1 = (bf16[3,64,256]{2,1,0:T(8,128)(2,1)S(1)}, bf16[3,64,256]{2,1,0:T(8,128)(2,1)S(1)}, u32[]{:S(2)}, u32[]{:S(2)}) collective-permute-start(bf16[3,64,256]{2,1,0:T(8,128)(2,1)S(1)} %basis.1.refs_0_), channel_id=1, source_target_pairs={{0,6},{1,25},{2,0},{3,27},{4,2},{5,29},{6,4},{7,31},{8,14},{9,1},{... | collective-permute-start | bytes 294920 | tf_op jit(solution)/shard_map/ppermute | solution.py:44
  14.6 1.7 %collective-permute-start = (s32[2,32]{1,0:T(2,128)}, s32[2,32]{1,0:T(2,128)}, u32[]{:S(2)}, u32[]{:S(2)}) collective-permute-start(s32[2,32]{1,0:T(2,128)} %pad_add_fusion), channel_id=1, source_target_pairs={{0,1},{1,0},{2,3},{3,2},{4,5},{5,4},{6,7},{7,6},{8,9},{9,8},{10,11... | collective-permute-start | bytes 776 | tf_op jit(solution)/shard_map/ppermute | solution.py:48
  18.6 6.2 %collective-permute-start.5 = (f32[3,32,64]{2,1,0:T(8,128)}, f32[3,32,64]{2,1,0:T(8,128)S(1)}, u32[]{:S(2)}, u32[]{:S(2)}) collective-permute-start(f32[3,32,64]{2,1,0:T(8,128)} %my_floor_ref.1), channel_id=1, source_target_pairs={{0,1},{1,0},{2,3},{3,2},{4,5},{5,4},{6,7},{7,6},{8,9},{9,8},{10,11... | collective-permute-start | bytes 73736 | tf_op jit(solution)/shard_map/ppermute | solution.py:48
  19.1 17.0 %collective-permute-start.8 = (bf16[4,3,64,256]{3,2,1,0:T(8,128)(2,1)S(1)}, bf16[4,3,64,256]{3,2,1,0:T(8,128)(2,1)S(1)}, u32[]{:S(2)}, u32[]{:S(2)}) collective-permute-start(bf16[4,3,64,256]{3,2,1,0:T(8,128)(2,1)S(1)} %line.1.rows_ref), channel_id=1, source_target_pairs={{0,16},{1,5},{2,18},{3,7},{4,20},{5,1},{6,22},{7,3},{8,24},{9,13},... | collective-permute-start | bytes 1179656 | tf_op jit(solution)/shard_map/ppermute | solution.py:44
  22.7 13.4 %collective-permute-start.7 = (bf16[4,3,64,256]{3,2,1,0:T(8,128)(2,1)S(1)}, bf16[4,3,64,256]{3,2,1,0:T(8,128)(2,1)S(1)}, u32[]{:S(2)}, u32[]{:S(2)}) collective-permute-start(bf16[4,3,64,256]{3,2,1,0:T(8,128)(2,1)S(1)} %line.1.rows_ref), channel_id=1, source_target_pairs={{0,24},{1,7},{2,26},{3,1},{4,28},{5,3},{6,30},{7,5},{8,0},{9,15},{... | collective-permute-start | bytes 1179656 | tf_op jit(solution)/shard_map/ppermute | solution.py:44
  23.5 9.3 %collective-permute-start.6 = (bf16[4,3,64,256]{3,2,1,0:T(8,128)(2,1)S(1)}, bf16[4,3,64,256]{3,2,1,0:T(8,128)(2,1)S(1)}, u32[]{:S(2)}, u32[]{:S(2)}) collective-permute-start(bf16[4,3,64,256]{3,2,1,0:T(8,128)(2,1)S(1)} %line.1.rows_ref), channel_id=1, source_target_pairs={{0,8},{1,3},{2,10},{3,5},{4,12},{5,7},{6,14},{7,1},{8,16},{9,11},{... | collective-permute-start | bytes 1179656 | tf_op jit(solution)/shard_map/ppermute | solution.py:44
  42.7 7.3 %collective-permute-start.9 = (f16[4,3,8,1024]{3,2,1,0:T(8,128)(2,1)S(1)}, f16[4,3,8,1024]{3,2,1,0:T(8,128)(2,1)S(1)}, u32[]{:S(2)}, u32[]{:S(2)}) collective-permute-start(f16[4,3,8,1024]{3,2,1,0:T(8,128)(2,1)S(1)} %pad_maximum_fusion), channel_id=1, source_target_pairs={{0,4},{1,17},{2,6},{3,19},{4,0},{5,21},{6,2},{7,23},{8,12},{9,25},... | collective-permute-start | bytes 589832 | tf_op jit(solution)/shard_map/ppermute | solution.py:44
  46.0 6.2 %collective-permute-start.10 = (f16[4,3,8,1024]{3,2,1,0:T(8,128)(2,1)S(1)}, f16[4,3,8,1024]{3,2,1,0:T(8,128)(2,1)S(1)}, u32[]{:S(2)}, u32[]{:S(2)}) collective-permute-start(f16[4,3,8,1024]{3,2,1,0:T(8,128)(2,1)S(1)} %pad_maximum_fusion.1), channel_id=1, source_target_pairs={{0,6},{1,25},{2,0},{3,27},{4,2},{5,29},{6,4},{7,31},{8,14},{9,1},{... | collective-permute-start | bytes 589832 | tf_op jit(solution)/shard_map/ppermute | solution.py:44
  47.6 6.9 %collective-permute-start.11 = (f16[4,3,8,1024]{3,2,1,0:T(8,128)(2,1)S(1)}, f16[4,3,8,1024]{3,2,1,0:T(8,128)(2,1)S(1)}, u32[]{:S(2)}, u32[]{:S(2)}) collective-permute-start(f16[4,3,8,1024]{3,2,1,0:T(8,128)(2,1)S(1)} %pad_maximum_fusion.2), channel_id=1, source_target_pairs={{0,2},{1,9},{2,4},{3,11},{4,6},{5,13},{6,0},{7,15},{8,10},{9,17},{... | collective-permute-start | bytes 589832 | tf_op jit(solution)/shard_map/ppermute | solution.py:44
  54.7 6.0 %collective-permute-start.12 = (f16[3,8,1024]{2,1,0:T(8,128)(2,1)S(1)}, f16[3,8,1024]{2,1,0:T(8,128)(2,1)S(1)}, u32[]{:S(2)}, u32[]{:S(2)}) collective-permute-start(f16[3,8,1024]{2,1,0:T(8,128)(2,1)S(1)} %get-tuple-element.28), channel_id=1, source_target_pairs={{0,16},{1,5},{2,18},{3,7},{4,20},{5,1},{6,22},{7,3},{8,24},{9,13},... | collective-permute-start | bytes 147464 | tf_op jit(solution)/shard_map/ppermute | solution.py:44
  57.5 5.3 %collective-permute-start.14 = (f16[3,8,1024]{2,1,0:T(8,128)(2,1)S(1)}, f16[3,8,1024]{2,1,0:T(8,128)(2,1)S(1)}, u32[]{:S(2)}, u32[]{:S(2)}) collective-permute-start(f16[3,8,1024]{2,1,0:T(8,128)(2,1)S(1)} %get-tuple-element.29), channel_id=1, source_target_pairs={{0,8},{1,3},{2,10},{3,5},{4,12},{5,7},{6,14},{7,1},{8,16},{9,11},{... | collective-permute-start | bytes 147464 | tf_op jit(solution)/shard_map/ppermute | solution.py:44
  57.5 5.3 %collective-permute-start.13 = (f16[3,8,1024]{2,1,0:T(8,128)(2,1)S(1)}, f16[3,8,1024]{2,1,0:T(8,128)(2,1)S(1)}, u32[]{:S(2)}, u32[]{:S(2)}) collective-permute-start(f16[3,8,1024]{2,1,0:T(8,128)(2,1)S(1)} %get-tuple-element.30), channel_id=1, source_target_pairs={{0,24},{1,7},{2,26},{3,1},{4,28},{5,3},{6,30},{7,5},{8,0},{9,15},{... | collective-permute-start | bytes 147464 | tf_op jit(solution)/shard_map/ppermute | solution.py:44
  63.1 1.2 %collective-permute-start.15 = (f32[3,4,8]{2,1,0:T(4,128)S(1)}, f32[3,4,8]{2,1,0:T(4,128)S(1)}, u32[]{:S(2)}, u32[]{:S(2)}) collective-permute-start(f32[3,4,8]{2,1,0:T(4,128)S(1)} %dynamic-slice_bitcast_fusion), channel_id=1, source_target_pairs={{0,1},{1,0},{2,3},{3,2},{4,5},{5,4},{6,7},{7,6},{8,9},{9,8},{10,11... | collective-permute-start | bytes 1160 | tf_op jit(solution)/shard_map/ppermute | solution.py:48
  64.3 5.2 %collective-permute-start.18 = (f32[3,4,8]{2,1,0:T(4,128)S(1)}, f32[3,4,8]{2,1,0:T(4,128)S(1)}, u32[]{:S(2)}, u32[]{:S(2)}) collective-permute-start(f32[3,4,8]{2,1,0:T(4,128)S(1)} %bitcast_add_fusion), channel_id=1, source_target_pairs={{0,32},{32,64},{64,96},{96,0},{1,33},{33,65},{65,97},{97,1},{2,34}... | collective-permute-start | bytes 1160 | tf_op jit(solution)/shard_map/ppermute | solution.py:295
  65.9 3.7 %collective-permute-start.17 = (f32[3,4,8]{2,1,0:T(4,128)S(1)}, f32[3,4,8]{2,1,0:T(4,128)S(1)}, u32[]{:S(2)}, u32[]{:S(2)}) collective-permute-start(f32[3,4,8]{2,1,0:T(4,128)S(1)} %bitcast_add_fusion), channel_id=1, source_target_pairs={{0,96},{32,0},{64,32},{96,64},{1,97},{33,1},{65,33},{97,65},{2,98}... | collective-permute-start | bytes 1160 | tf_op jit(solution)/shard_map/ppermute | solution.py:295
  67.6 5.1 %collective-permute-start.16 = (f32[3,4,8]{2,1,0:T(4,128)S(1)}, f32[3,4,8]{2,1,0:T(4,128)S(1)}, u32[]{:S(2)}, u32[]{:S(2)}) collective-permute-start(f32[3,4,8]{2,1,0:T(4,128)S(1)} %bitcast_add_fusion), channel_id=1, source_target_pairs={{0,64},{32,96},{64,0},{96,32},{1,65},{33,97},{65,1},{97,33},{2,66}... | collective-permute-start | bytes 1160 | tf_op jit(solution)/shard_map/ppermute | solution.py:295
  72.8 0.8 %copy-start = (f32[3,4]{1,0:T(4,128)}, f32[3,4]{1,0:T(4,128)S(1)}, u32[]{:S(2)}) copy-start(f32[3,4]{1,0:T(4,128)S(1)} %broadcast_multiply_fusion) | copy-start | bytes 148
